TPU v7x, 32 devices: a whole 2x2x4 slice. The times are simulated.
32 devices in a mesh: shot: 2 (over y), gx: 16 (over z, x, core).
Axes of the slice: x: 2, y: 2, z: 4, core: 2. Of those that a mesh axis runs over, the one named last changes fastest.
Arguments:
- wave_now: float32 [4, 128, 16, 128], P('shot', 'gx'), parts along dimension 0, may hold values from -6 to 6
- wave_prev: float32 [4, 128, 16, 128], P('shot', 'gx'), parts along dimension 0, may hold values from -6 to 6
- speed_term: float32 [128, 16, 128], P('gx'), may hold values from 0.02 to 0.07
- thomsen_epsilon: float32 [128, 16, 128], P('gx'), may hold values from 0.15 to 0.35
- thomsen_delta: float32 [128, 16, 128], P('gx'), may hold values from 0 to 0.1
- tilt_angle: float32 [128, 16, 128], P('gx'), may hold values from -3.140625 to 3.140625
- source_store: bfloat16 [4, 4, 128, 16, 128], P('shot', None, None, 'gx'), parts along dimension 0, may hold values from -6 to 6
- receiver_row: int32 [256], P('shot'), parts along dimension 0, may hold values from 0 to 127
- receiver_column: int32 [256], P('shot'), parts along dimension 0, may hold values from 0 to 15
- receiver_traces: float32 [8, 128], P('shot'), parts along dimension 0, may hold values from -12 to 12
- angle_table: int32 [32], replicated, may hold values from 0 to 7, as said below
Outputs:
- angle_images: bfloat16 [16, 128, 16, 128], P('shot', 'gx'), parts along dimension 0
- wave_final: float32 [4, 128, 16, 128], P('shot', 'gx'), parts along dimension 0
There are 2 independent parts, one for each index of `shot`. A program takes and returns all parts, laid end to end along the dimension named above; an argument that names none is the same for every part. Nothing has to cross between parts.
Inputs may be any that keep to these rules, and one draw needn't show every extreme that they name: angle_table is non-decreasing: angle_table[f] <= angle_table[f+1] for every fine bin f, and every one of the 8 angle images is named by at least one fine bin.
All inputs are finite; a program needn't handle non-finite values.
Results may differ from a plain program's by a relative error of at most 0.001.
Values may be sent and summed in bfloat16 or wider, within the bound.
No kernel may reach another device: no remote copies, remote signals or barrier semaphores. Data moves between devices by JAX's collectives and lax.ppermute only.
A program may use at most 128 MiB of HBM per device.

v0:
```python
import jax
import jax.numpy as jnp
from jax import lax
from jax.sharding import PartitionSpec as P

STEPS = 4
IMAGE_EVERY = 2
NBIN = 8
FINE = 32
REC_DEPTH = 2


second_coeffs = (-205.0 / 72.0, 8.0 / 5.0, -1.0 / 5.0, 8.0 / 315.0, -1.0 / 560.0)
first_coeffs = (4.0 / 5.0, -1.0 / 5.0, 4.0 / 105.0, -1.0 / 280.0)
stencil_reach = 4


def padded_2(cells, sides, width):
    for axis, dim in sides:
        count = lax.axis_size(axis)
        ends = count - 1
        head = lax.slice_in_dim(cells, 0, width, axis=dim)
        tail = lax.slice_in_dim(cells, cells.shape[dim] - width, cells.shape[dim], axis=dim)
        cells = jnp.concatenate(
            [
                lax.ppermute(tail, axis, [(i, (i + 1) % count) for i in range(ends)]),
                cells,
                lax.ppermute(head, axis, [((i + 1) % count, i) for i in range(ends)]),
            ],
            axis=dim,
        )
    return cells


def window(array_in, direction, begin_at, extent):
    return lax.slice_in_dim(array_in, begin_at, begin_at + extent, axis=direction)


def moved(field, direction, offset):
    length = field.shape[direction]
    shape = list(field.shape)
    shape[direction] = abs(offset)
    zeros = jnp.zeros(tuple(shape), field.dtype)
    if offset > 0:
        return jnp.concatenate(
            [lax.slice_in_dim(field, offset, length, axis=direction), zeros], axis=direction
        )
    return jnp.concatenate(
        [zeros, lax.slice_in_dim(field, 0, length + offset, axis=direction)], axis=direction
    )


def second_along(field, direction):
    summed = second_coeffs[0] * field
    for offset in range(1, 5):
        summed = summed + second_coeffs[offset] * (
            moved(field, direction, offset) + moved(field, direction, -offset)
        )
    return summed


def first_along(field, direction):
    summed = first_coeffs[0] * (moved(field, direction, 1) - moved(field, direction, -1))
    for offset in range(2, 5):
        summed = summed + first_coeffs[offset - 1] * (
            moved(field, direction, offset) - moved(field, direction, -offset)
        )
    return summed


def second_diff(padded, direction, extent):
    summed = second_coeffs[0] * window(padded, direction, stencil_reach, extent)
    for offset in range(1, 5):
        summed = summed + second_coeffs[offset] * (
            window(padded, direction, stencil_reach + offset, extent)
            + window(padded, direction, stencil_reach - offset, extent)
        )
    return summed


def first_diff(padded, direction, extent):
    summed = first_coeffs[0] * (
        window(padded, direction, stencil_reach + 1, extent)
        - window(padded, direction, stencil_reach - 1, extent)
    )
    for offset in range(2, 5):
        summed = summed + first_coeffs[offset - 1] * (
            window(padded, direction, stencil_reach + offset, extent)
            - window(padded, direction, stencil_reach - offset, extent)
        )
    return summed


def advance(padded, earlier, medium, traces_now, receiver_row, receiver_column, first_row):
    extent_x = earlier.shape[1]
    extent_y = earlier.shape[2]
    speed, epsilon, thomsen, tilt = medium
    second_x = second_diff(padded, 1, extent_x)
    inner_rows = padded[:, 4:-4]
    second_y = second_along(inner_rows[0], 1)
    second_z = second_along(inner_rows, 3)
    slope_z_all = first_along(padded, 3)
    mixed = first_diff(slope_z_all, 1, extent_x)
    slope_x = first_diff(padded[0], 0, extent_x)
    slope_y = first_along(inner_rows[0], 1)
    slope_z = slope_z_all[0, 4:-4]
    cosine = jnp.cos(tilt)
    sine = jnp.sin(tilt)
    rotated = cosine * cosine * second_z + sine * sine * second_x + 2.0 * sine * cosine * mixed
    across_p = second_x[0] + second_y + second_z[0] - rotated[0]
    ratio = jnp.sqrt(1.0 + 2.0 * thomsen)
    p_next = (
        2.0 * inner_rows[0]
        - earlier[0]
        + speed * ((1.0 + 2.0 * epsilon) * across_p + ratio * rotated[1])
    )
    q_next = 2.0 * inner_rows[1] - earlier[1] + speed * (ratio * across_p + rotated[1])
    local_row = receiver_row - first_row
    inside = (local_row >= 0) & (local_row < extent_x)
    flat_index = jnp.where(inside, local_row * extent_y + receiver_column, extent_x * extent_y)
    plane = (
        jnp.zeros((extent_x * extent_y,), jnp.float32).at[flat_index].add(traces_now, mode="drop")
    )
    p_next = p_next.at[:, :, REC_DEPTH].add(plane.reshape(extent_x, extent_y))
    return (jnp.stack([p_next, q_next]), (slope_x, slope_y, slope_z))


def angle_image(snapshot, wave_field, earlier_field, slopes, bounds):
    lower, upper = bounds
    rate = wave_field - earlier_field
    flux_x = -rate * slopes[0]
    flux_y = -rate * slopes[1]
    flux_z = -rate * slopes[2]
    inner = snapshot[1] * flux_x + snapshot[2] * flux_y + snapshot[3] * flux_z
    lengths = jnp.sqrt(
        snapshot[1] * snapshot[1] + snapshot[2] * snapshot[2] + snapshot[3] * snapshot[3]
    ) * jnp.sqrt(flux_x * flux_x + flux_y * flux_y + flux_z * flux_z)
    cosine = inner / jnp.maximum(lengths, 1.0)
    scaled = (cosine + 1.0) * (0.5 * (FINE - 1))
    shaped = (lower.shape[0],) + (1,) * scaled.ndim
    rising = jnp.clip(scaled[None] - lower.reshape(shaped) + 1.0, 0.0, 1.0)
    falling = jnp.clip(upper.reshape(shaped) + 1.0 - scaled[None], 0.0, 1.0)
    return jnp.minimum(rising, falling) * (snapshot[0] * wave_field)[None]


def local(
    wave_now,
    wave_prev,
    speed_term,
    thomsen_epsilon,
    thomsen_delta,
    tilt_angle,
    source_store,
    receiver_row,
    receiver_column,
    receiver_traces,
    angle_table,
):
    extent_x = wave_now.shape[1]
    first_row = lax.axis_index("gx") * extent_x
    image_ids = jnp.arange(NBIN, dtype=jnp.int32)[:, None]
    lower = jnp.sum((angle_table[None, :] < image_ids).astype(jnp.float32), axis=1)
    upper = jnp.sum((angle_table[None, :] <= image_ids).astype(jnp.float32), axis=1) - 1.0
    bounds = (lower, upper)
    medium = (speed_term, thomsen_epsilon, thomsen_delta, tilt_angle)
    arrived = lax.all_to_all(source_store, "gx", split_axis=2, concat_axis=3, tiled=True)
    images = jnp.zeros((NBIN,) + wave_now.shape[1:], jnp.float32)
    current = wave_now
    earlier = wave_prev
    for time_step in range(STEPS):
        padded = padded_2(current, (("gx", 1),), 4)
        following, slopes = advance(
            padded,
            earlier,
            medium,
            receiver_traces[time_step],
            receiver_row,
            receiver_column,
            first_row,
        )
        if time_step % IMAGE_EVERY == IMAGE_EVERY - 1:
            snap_index = time_step // IMAGE_EVERY
            snapshot = arrived[snap_index]
            images = images + angle_image(
                snapshot.astype(jnp.float32), current[0], earlier[0], slopes, bounds
            )
        earlier = current
        current = following
    return (images.astype(jnp.bfloat16), current)


def solution(mesh):
    placed = (
        P("shot", "gx", None, None),
        P("shot", "gx", None, None),
        P("gx", None, None),
        P("gx", None, None),
        P("gx", None, None),
        P("gx", None, None),
        P("shot", None, None, "gx", None),
        P("shot"),
        P("shot"),
        P("shot", None),
        P(),
    )
    return jax.shard_map(
        local,
        mesh=mesh,
        in_specs=placed,
        out_specs=(P("shot", "gx", None, None), P("shot", "gx", None, None)),
        check_vma=False,
    )
```

profile of v0, /device:TPU:1, one launch (start us, length us, event | category | flops | bytes accessed | tf_op | source)
XLA Modules:
  0.0 363.9 jit_solution(14505903367550043758)
XLA Ops:
  2.2 4.5 %collective-permute-start.1 = (f32[2,4,16,128]{3,2,1,0:T(8,128)}, f32[2,4,16,128]{3,2,1,0:T(8,128)}, u32[]{:S(2)}, u32[]{:S(2)}) collective-permute-start(f32[2,4,16,128]{3,2,1,0:T(8,128)} %get-tuple-element.268), channel_id=1, source_target_pairs={{0,1},{1,2},{2,3},{3,4},{4,5},{5,6},{6,7},{7,8},{8,9},{9,10},{10,1... | collective-permute-start | bytes 196616 | tf_op jit(solution)/shard_map/ppermute | solution.py:26
  6.7 1.9 collective-permute-start
  10.4 6.5 %all-to-all-start = ((bf16[2,4,128,1,128]{4,1,0,3,2:T(4,128)(2,1)}), bf16[2,4,128,1,128]{4,1,0,3,2:T(4,128)(2,1)}, u32[]{:S(2)}, u32[]{:S(2)}) async-start(bf16[2,4,128,1,128]{4,1,0,3,2:T(4,128)(2,1)} %copy.520), calls=%async_computation | async-start | bytes 524288 | tf_op jit(solution)/shard_map/all_to_all | solution.py:166
  30.3 2.6 fusion.168
  39.7 1.9 scatter_custom_fusion.3
  42.3 2.1 multiply_multiply_fusion
  49.7 3.1 copy.635
  52.7 3.1 copy.634
  55.8 3.1 copy.633
  58.9 3.0 copy.632
  62.0 2.2 copy.631
  64.2 3.1 copy.630
  67.3 3.1 copy.629
  70.4 2.1 copy.628
  73.2 2.3 copy.534
  76.2 2.3 copy.535
  86.6 6.5 %multiply_add_fusion.3 = f32[2,16,16,128]{2,1,3,0:T(8,128)S(1)} fusion(f32[2,16,16,124]{2,1,3,0:T(8,128)} %copy.635, f32[2,16,16,124]{2,1,3,0:T(8,128)} %copy.634, f32[2,16,16,125]{2,1,3,0:T(8,128)} %copy.633, f32[2,16,16,125]{2,1,3,0:T(8,128)} %copy.632, f32[2,16,16,126]{2,1,3,0:T(8,128)} %copy.631, f32[2,16,16,126]{2,1,3,0:T(8,128)} %copy.630, ...), kind=kLoop, calls=%fused_computation.73 | loop fusion | flops 720896 | bytes 2318336 | tf_op jit(solution)/shard_map/add | solution.py:65
  95.8 5.0 %fusion.30 = (f32[2,8,16,128]{2,1,3,0:T(8,128)S(1)}, f32[2,8,16,128]{2,1,3,0:T(8,128)}, f32[2,8,16,128]{2,1,3,0:T(8,128)}) fusion(f32[2,16,16,128]{2,1,3,0:T(8,128)S(1)} %multiply_add_fusion.3, f32[8,16,128]{1,0,2:T(8,128)S(1)} %get-tuple-element.146, f32[8,16,128]{1,0,2:T(8,128)S(1)} %copy-done.19, f32[8,16,128]{1,0,2:T(8,128)S(1)} %copy-done.23, ...), kind=kLoop, calls=%fused_computation.118 | loop fusion | flops 1343488 | bytes 3846144 | tf_op jit(solution)/shard_map/add | solution.py:109
  100.8 3.4 fusion.82
  116.1 2.1 collective-permute-start.2
  118.2 3.7 %collective-permute-start.3 = (f32[2,4,16,128]{2,1,3,0:T(4,128)}, f32[2,4,16,128]{2,1,3,0:T(4,128)}, u32[]{:S(2)}, u32[]{:S(2)}) collective-permute-start(f32[2,4,16,128]{2,1,3,0:T(4,128)} %get-tuple-element.136), channel_id=1, source_target_pairs={{0,1},{1,2},{2,3},{3,4},{4,5},{5,6},{6,7},{7,8},{8,9},{9,10},{10,1... | collective-permute-start | bytes 196616 | tf_op jit(solution)/shard_map/ppermute | solution.py:26
  124.4 2.4 collective-permute-done.2
  126.8 6.1 %collective-permute-done.3 = f32[2,4,16,128]{2,1,3,0:T(4,128)} collective-permute-done((f32[2,4,16,128]{2,1,3,0:T(4,128)}, f32[2,4,16,128]{2,1,3,0:T(4,128)}, u32[]{:S(2)}, u32[]{:S(2)}) %collective-permute-start.3) | collective-permute-done | bytes 65568 | tf_op jit(solution)/shard_map/ppermute | solution.py:26
  134.4 2.4 fusion.147
  136.8 2.3 fusion.146
  139.0 2.3 fusion.145
  141.3 2.4 fusion.144
  145.9 2.2 copy.581
  148.1 2.3 copy.582
  150.4 2.2 copy.579
  159.3 6.5 %multiply_add_fusion.2 = f32[2,16,16,128]{2,1,3,0:T(8,128)S(1)} fusion(f32[2,16,16,124]{2,1,3,0:T(8,128)} %get-tuple-element.107, f32[2,16,16,124]{2,1,3,0:T(8,128)} %get-tuple-element.106, f32[2,16,16,125]{2,1,3,0:T(8,128)} %get-tuple-element.105, f32[2,16,16,125]{2,1,3,0:T(8,128)} %get-tuple-element.104, f32[2,16,16,126]{2,1,3,0:T(8,128)} %get-tuple-element.103, ...), kind=kLoop, calls=%fused_computation.72 | loop fusion | flops 720896 | bytes 2318336 | tf_op jit(solution)/shard_map/add | solution.py:65
  168.1 6.3 %fusion.21 = (f32[2,8,16,128]{2,1,3,0:T(8,128)S(1)}, f32[2,8,16,128]{2,1,3,0:T(8,128)}, f32[2,8,16,128]{2,1,3,0:T(8,128)}) fusion(f32[2,16,16,128]{2,1,3,0:T(8,128)S(1)} %multiply_add_fusion.2, f32[8,16,128]{1,0,2:T(8,128)S(1)} %copy-done.16, f32[8,16,128]{1,0,2:T(8,128)S(1)} %copy-done.20, f32[8,16,128]{1,0,2:T(8,128)S(1)} %copy-done.24, ...), kind=kLoop, calls=%fused_computation.104 | loop fusion | flops 1376256 | bytes 3846144 | tf_op jit(solution)/shard_map/add | solution.py:109
  174.5 2.1 multiply_add_fusion.15
  190.9 1.9 collective-permute-start.4
  192.9 4.6 %collective-permute-start.5 = (f32[2,4,16,128]{2,1,3,0:T(4,128)}, f32[2,4,16,128]{2,1,3,0:T(4,128)}, u32[]{:S(2)}, u32[]{:S(2)}) collective-permute-start(f32[2,4,16,128]{2,1,3,0:T(4,128)} %get-tuple-element.126), channel_id=1, source_target_pairs={{0,1},{1,2},{2,3},{3,4},{4,5},{5,6},{6,7},{7,8},{8,9},{9,10},{10,1... | collective-permute-start | bytes 196616 | tf_op jit(solution)/shard_map/ppermute | solution.py:26
  199.8 1.9 copy.571
  201.7 1.9 copy.572
  213.0 2.4 fusion.143
  215.3 2.3 fusion.142
  217.6 2.3 fusion.141
  219.9 2.3 fusion.140
  227.8 2.2 copy.595
  230.0 2.3 copy.596
  232.3 2.3 copy.593
  234.6 2.2 copy.594
  236.8 2.2 copy.591
  243.0 6.5 %multiply_add_fusion.1 = f32[2,16,16,128]{2,1,3,0:T(8,128)S(1)} fusion(f32[2,16,16,124]{2,1,3,0:T(8,128)} %get-tuple-element.99, f32[2,16,16,124]{2,1,3,0:T(8,128)} %get-tuple-element.98, f32[2,16,16,125]{2,1,3,0:T(8,128)} %get-tuple-element.97, f32[2,16,16,125]{2,1,3,0:T(8,128)} %get-tuple-element.96, f32[2,16,16,126]{2,1,3,0:T(8,128)} %get-tuple-element.95, ...), kind=kLoop, calls=%fused_computation.71 | loop fusion | flops 720896 | bytes 2318336 | tf_op jit(solution)/shard_map/add | solution.py:65
  251.9 5.4 %fusion.12 = (f32[2,8,16,128]{2,1,3,0:T(8,128)S(1)}, f32[2,8,16,128]{2,1,3,0:T(8,128)}, f32[2,8,16,128]{2,1,3,0:T(8,128)}) fusion(f32[2,16,16,128]{2,1,3,0:T(8,128)S(1)} %multiply_add_fusion.1, f32[8,16,128]{1,0,2:T(8,128)S(1)} %copy-done.17, f32[8,16,128]{1,0,2:T(8,128)S(1)} %copy-done.21, f32[8,16,128]{1,0,2:T(8,128)S(1)} %copy-done.25, ...), kind=kLoop, calls=%fused_computation.91 | loop fusion | flops 1376256 | bytes 3846144 | tf_op jit(solution)/shard_map/add | solution.py:109
  258.2 4.2 %fusion.84 = (f32[1,8,16,128]{2,1,3,0:T(8,128)}, f32[8,16,128]{1,0,2:T(8,128)}) fusion(f32[8,16,128]{1,0,2:T(8,128)S(1)} %copy-done.7, f32[2,8,16,128]{2,1,3,0:T(8,128)S(1)} %get-tuple-element.69, f32[8,16,128]{1,0,2:T(8,128)S(1)} %get-tuple-element.77, f32[8,16,128]{1,0,2:T(8,128)S(1)} %get-tuple-element.72, f32[8,16,128]{1,0,2:T(8,128)S(1)} %copy-done.12, ...), kind=kLoop, calls=%fused_computation.254 | loop fusion | flops 360448 | bytes 1163264 | tf_op jit(solution)/shard_map/stack | solution.py:125
  262.4 3.3 copy.522
  265.7 3.3 slice_convert_fusion.1
  281.8 1.9 collective-permute-start.6
  283.7 3.9 %collective-permute-start.7 = (f32[2,4,16,128]{2,1,3,0:T(4,128)}, f32[2,4,16,128]{2,1,3,0:T(4,128)}, u32[]{:S(2)}, u32[]{:S(2)}) collective-permute-start(f32[2,4,16,128]{2,1,3,0:T(4,128)} %get-tuple-element.116), channel_id=1, source_target_pairs={{0,1},{1,2},{2,3},{3,4},{4,5},{5,6},{6,7},{7,8},{8,9},{9,10},{10,1... | collective-permute-start | bytes 196616 | tf_op jit(solution)/shard_map/ppermute | solution.py:26
  287.8 3.4 add_multiply_fusion.1
  295.3 2.1 collective-permute-done.7
  299.0 2.3 fusion.139
  301.3 2.3 fusion.138
  303.6 2.3 fusion.137
  306.0 2.3 fusion.136
  322.4 6.8 %multiply_add_fusion = f32[2,16,16,128]{2,1,3,0:T(8,128)S(1)} fusion(f32[2,16,16,124]{2,1,3,0:T(8,128)} %get-tuple-element.91, f32[2,16,16,124]{2,1,3,0:T(8,128)} %get-tuple-element.90, f32[2,16,16,125]{2,1,3,0:T(8,128)} %get-tuple-element.89, f32[2,16,16,125]{2,1,3,0:T(8,128)} %get-tuple-element.88, f32[2,16,16,126]{2,1,3,0:T(8,128)} %get-tuple-element.87, ...), kind=kLoop, calls=%fused_computation.70 | loop fusion | flops 720896 | bytes 2318336 | tf_op jit(solution)/shard_map/add | solution.py:65
  330.9 6.3 %fusion.3 = (f32[2,8,16,128]{2,1,3,0:T(8,128)S(1)}, f32[2,8,16,128]{2,1,3,0:T(8,128)}, f32[2,8,16,128]{2,1,3,0:T(8,128)}) fusion(f32[2,16,16,128]{2,1,3,0:T(8,128)S(1)} %multiply_add_fusion, f32[8,16,128]{1,0,2:T(8,128)S(1)} %copy-done.18, f32[8,16,128]{1,0,2:T(8,128)S(1)} %copy-done.22, f32[8,16,128]{1,0,2:T(8,128)S(1)} %copy-done.26, ...), kind=kLoop, calls=%fused_computation.78 | loop fusion | flops 1376256 | bytes 3846144 | tf_op jit(solution)/shard_map/add | solution.py:109
  337.3 3.6 multiply_add_fusion.12
  351.6 6.4 %add_multiply_fusion = f32[8,16,128]{1,0,2:T(8,128)} fusion(f32[1,4,8,16,1,128]{3,2,5,4,1,0:T(8,128)} %get-tuple-element.83, f32[2,16,16,128]{2,1,3,0:T(8,128)} %copy-done.3, f32[1,8,16,128]{2,1,3,0:T(8,128)} %copy.609, f32[1,8,16,128]{2,1,3,0:T(8,128)} %copy.610, f32[1,8,16,128]{2,1,3,0:T(8,128)} %copy.607, f32[1,8,16,128]{2,1,3,0:T(8,128)} %copy.608, ...), kind=kLoop, calls=%fused_computation.219 | loop fusion | flops 770048 | bytes 1425408 | tf_op jit(solution)/shard_map/mul | solution.py:139
  359.2 1.9 add_bitcast_fusion
  (407 shorter events, 155.6 us)
Async XLA Ops:
  2.2 43.1 %collective-permute-start.1 = (f32[2,4,16,128]{3,2,1,0:T(8,128)}, f32[2,4,16,128]{3,2,1,0:T(8,128)}, u32[]{:S(2)}, u32[]{:S(2)}) collective-permute-start(f32[2,4,16,128]{3,2,1,0:T(8,128)} %get-tuple-element.268), channel_id=1, source_target_pairs={{0,1},{1,2},{2,3},{3,4},{4,5},{5,6},{6,7},{7,8},{8,9},{9,10},{10,1... | collective-permute-start | bytes 196616 | tf_op jit(solution)/shard_map/ppermute | solution.py:26
  6.7 39.5 %collective-permute-start = (f32[2,4,16,128]{3,2,1,0:T(8,128)}, f32[2,4,16,128]{3,2,1,0:T(8,128)S(1)}, u32[]{:S(2)}, u32[]{:S(2)}) collective-permute-start(f32[2,4,16,128]{3,2,1,0:T(8,128)} %get-tuple-element.267), channel_id=1, source_target_pairs={{1,0},{2,1},{3,2},{4,3},{5,4},{6,5},{7,6},{8,7},{9,8},{10,9},{11,1... | collective-permute-start | bytes 196616 | tf_op jit(solution)/shard_map/ppermute | solution.py:28
  10.4 252.0 %all-to-all-start = ((bf16[2,4,128,1,128]{4,1,0,3,2:T(4,128)(2,1)}), bf16[2,4,128,1,128]{4,1,0,3,2:T(4,128)(2,1)}, u32[]{:S(2)}, u32[]{:S(2)}) async-start(bf16[2,4,128,1,128]{4,1,0,3,2:T(4,128)(2,1)} %copy.520), calls=%async_computation | async-start | bytes 524288 | tf_op jit(solution)/shard_map/all_to_all | solution.py:166
  29.0 145.4 %copy-start.6 = (f32[8,16,128]{1,0,2:T(8,128)}, f32[8,16,128]{1,0,2:T(8,128)S(1)}, u32[]{:S(2)}) copy-start(f32[8,16,128]{1,0,2:T(8,128)S(1)} %copy.557) | copy-start | bytes 196612
  33.1 71.1 %copy-start.10 = (f32[8,16,128]{1,0,2:T(8,128)}, f32[8,16,128]{1,0,2:T(8,128)S(1)}, u32[]{:S(2)}) copy-start(f32[8,16,128]{1,0,2:T(8,128)S(1)} %copy.556) | copy-start | bytes 196612
  33.1 11.4 %copy-start.130 = (s32[32]{0:T(128)S(1)}, s32[32]{0:T(128)}, u32[]{:S(2)}) copy-start(s32[32]{0:T(128)} %param.29) | copy-start | bytes 388
  33.1 13.0 %copy-start.103 = (f32[2,8,16,128]{3,2,1,0:T(8,128)S(1)}, f32[2,8,16,128]{3,2,1,0:T(8,128)}, u32[]{:S(2)}) copy-start(f32[2,8,16,128]{3,2,1,0:T(8,128)} %param.19) | copy-start | bytes 393220
  44.5 48.6 %copy-start.15 = (f32[8,16,128]{1,0,2:T(8,128)}, f32[8,16,128]{1,0,2:T(8,128)S(1)}, u32[]{:S(2)}) copy-start(f32[8,16,128]{1,0,2:T(8,128)S(1)} %get-tuple-element.146) | copy-start | bytes 196612
  86.5 7.2 %copy-start.78 = (f32[2,8,16,128]{2,1,3,0:T(8,128)S(1)}, f32[2,8,16,128]{2,1,3,0:T(8,128)}, u32[]{:S(2)}) copy-start(f32[2,8,16,128]{2,1,3,0:T(8,128)} %copy.533) | copy-start | bytes 393220
  86.5 7.5 %copy-start.81 = (f32[2,8,16,128]{2,1,3,0:T(8,128)S(1)}, f32[2,8,16,128]{2,1,3,0:T(8,128)}, u32[]{:S(2)}) copy-start(f32[2,8,16,128]{2,1,3,0:T(8,128)} %copy.530) | copy-start | bytes 393220
  86.5 7.8 %copy-start.83 = (f32[2,8,16,128]{2,1,3,0:T(8,128)S(1)}, f32[2,8,16,128]{2,1,3,0:T(8,128)}, u32[]{:S(2)}) copy-start(f32[2,8,16,128]{2,1,3,0:T(8,128)} %copy.531) | copy-start | bytes 393220
  86.5 8.1 %copy-start.85 = (f32[2,8,16,128]{2,1,3,0:T(8,128)S(1)}, f32[2,8,16,128]{2,1,3,0:T(8,128)}, u32[]{:S(2)}) copy-start(f32[2,8,16,128]{2,1,3,0:T(8,128)} %copy.528) | copy-start | bytes 393220
  86.5 8.4 %copy-start.86 = (f32[2,8,16,128]{2,1,3,0:T(8,128)S(1)}, f32[2,8,16,128]{2,1,3,0:T(8,128)}, u32[]{:S(2)}) copy-start(f32[2,8,16,128]{2,1,3,0:T(8,128)} %copy.529) | copy-start | bytes 393220
  86.5 8.7 %copy-start.88 = (f32[2,8,16,127]{2,1,3,0:T(8,128)S(1)}, f32[2,8,16,127]{2,1,3,0:T(8,128)}, u32[]{:S(2)}) copy-start(f32[2,8,16,127]{2,1,3,0:T(8,128)} %get-tuple-element.138) | copy-start | bytes 390148
  86.5 9.0 %copy-start.89 = (f32[2,8,16,127]{2,1,3,0:T(8,128)S(1)}, f32[2,8,16,127]{2,1,3,0:T(8,128)}, u32[]{:S(2)}) copy-start(f32[2,8,16,127]{2,1,3,0:T(8,128)} %get-tuple-element.139) | copy-start | bytes 390148
  86.6 9.3 %copy-start.90 = (f32[2,8,16,126]{2,1,3,0:T(8,128)S(1)}, f32[2,8,16,126]{2,1,3,0:T(8,128)}, u32[]{:S(2)}) copy-start(f32[2,8,16,126]{2,1,3,0:T(8,128)} %get-tuple-element.140) | copy-start | bytes 387076
  116.1 10.7 %collective-permute-start.2 = (f32[2,4,16,128]{2,1,3,0:T(4,128)}, f32[2,4,16,128]{2,1,3,0:T(4,128)S(1)}, u32[]{:S(2)}, u32[]{:S(2)}) collective-permute-start(f32[2,4,16,128]{2,1,3,0:T(4,128)} %get-tuple-element.137), channel_id=1, source_target_pairs={{1,0},{2,1},{3,2},{4,3},{5,4},{6,5},{7,6},{8,7},{9,8},{10,9},{11,1... | collective-permute-start | bytes 196616 | tf_op jit(solution)/shard_map/ppermute | solution.py:28
  118.2 14.7 %collective-permute-start.3 = (f32[2,4,16,128]{2,1,3,0:T(4,128)}, f32[2,4,16,128]{2,1,3,0:T(4,128)}, u32[]{:S(2)}, u32[]{:S(2)}) collective-permute-start(f32[2,4,16,128]{2,1,3,0:T(4,128)} %get-tuple-element.136), channel_id=1, source_target_pairs={{0,1},{1,2},{2,3},{3,4},{4,5},{5,6},{6,7},{7,8},{8,9},{9,10},{10,1... | collective-permute-start | bytes 196616 | tf_op jit(solution)/shard_map/ppermute | solution.py:26
  159.3 7.1 %copy-start.70 = (f32[2,8,16,128]{2,1,3,0:T(8,128)S(1)}, f32[2,8,16,128]{2,1,3,0:T(8,128)}, u32[]{:S(2)}) copy-start(f32[2,8,16,128]{2,1,3,0:T(8,128)} %copy.579) | copy-start | bytes 393220
  159.3 7.4 %copy-start.73 = (f32[2,8,16,128]{2,1,3,0:T(8,128)S(1)}, f32[2,8,16,128]{2,1,3,0:T(8,128)}, u32[]{:S(2)}) copy-start(f32[2,8,16,128]{2,1,3,0:T(8,128)} %copy.580) | copy-start | bytes 393220
  159.3 8.2 %copy-start.76 = (f32[2,8,16,128]{2,1,3,0:T(8,128)S(1)}, f32[2,8,16,128]{2,1,3,0:T(8,128)}, u32[]{:S(2)}) copy-start(f32[2,8,16,128]{2,1,3,0:T(8,128)} %copy.577) | copy-start | bytes 393220
  159.3 8.7 %copy-start.79 = (f32[2,8,16,128]{2,1,3,0:T(8,128)S(1)}, f32[2,8,16,128]{2,1,3,0:T(8,128)}, u32[]{:S(2)}) copy-start(f32[2,8,16,128]{2,1,3,0:T(8,128)} %copy.578) | copy-start | bytes 393220
  165.8 8.6 %copy-start.2 = (f32[2,16,16,128]{2,1,3,0:T(8,128)}, f32[2,16,16,128]{2,1,3,0:T(8,128)S(1)}, u32[]{:S(2)}) copy-start(f32[2,16,16,128]{2,1,3,0:T(8,128)S(1)} %multiply_add_fusion.2) | copy-start | bytes 786436
  176.6 80.6 %copy-start = (f32[8,16,128]{1,0,2:T(8,128)}, f32[8,16,128]{1,0,2:T(8,128)S(1)}, u32[]{:S(2)}) copy-start(f32[8,16,128]{1,0,2:T(8,128)S(1)} %get-tuple-element.72) | copy-start | bytes 196612
  190.9 20.4 %collective-permute-start.4 = (f32[2,4,16,128]{2,1,3,0:T(4,128)}, f32[2,4,16,128]{2,1,3,0:T(4,128)}, u32[]{:S(2)}, u32[]{:S(2)}) collective-permute-start(f32[2,4,16,128]{2,1,3,0:T(4,128)} %get-tuple-element.127), channel_id=1, source_target_pairs={{1,0},{2,1},{3,2},{4,3},{5,4},{6,5},{7,6},{8,7},{9,8},{10,9},{11,1... | collective-permute-start | bytes 196616 | tf_op jit(solution)/shard_map/ppermute | solution.py:28
  192.9 18.4 %collective-permute-start.5 = (f32[2,4,16,128]{2,1,3,0:T(4,128)}, f32[2,4,16,128]{2,1,3,0:T(4,128)}, u32[]{:S(2)}, u32[]{:S(2)}) collective-permute-start(f32[2,4,16,128]{2,1,3,0:T(4,128)} %get-tuple-element.126), channel_id=1, source_target_pairs={{0,1},{1,2},{2,3},{3,4},{4,5},{5,6},{6,7},{7,8},{8,9},{9,10},{10,1... | collective-permute-start | bytes 196616 | tf_op jit(solution)/shard_map/ppermute | solution.py:26
  199.8 7.4 %copy-start.115 = (f32[1,8,16,128]{3,2,1,0:T(8,128)S(1)}, f32[1,8,16,128]{3,2,1,0:T(8,128)}, u32[]{:S(2)}) copy-start(f32[1,8,16,128]{3,2,1,0:T(8,128)} %get-tuple-element.248) | copy-start | bytes 196612
  199.8 8.4 %copy-start.114 = (f32[1,8,16,128]{3,2,1,0:T(8,128)S(1)}, f32[1,8,16,128]{3,2,1,0:T(8,128)}, u32[]{:S(2)}) copy-start(f32[1,8,16,128]{3,2,1,0:T(8,128)} %get-tuple-element.203) | copy-start | bytes 196612
  199.8 9.4 %copy-start.113 = (f32[1,8,16,128]{3,2,1,0:T(8,128)S(1)}, f32[1,8,16,128]{3,2,1,0:T(8,128)}, u32[]{:S(2)}) copy-start(f32[1,8,16,128]{3,2,1,0:T(8,128)} %get-tuple-element.249) | copy-start | bytes 196612
  199.8 10.4 %copy-start.112 = (f32[1,8,16,128]{3,2,1,0:T(8,128)S(1)}, f32[1,8,16,128]{3,2,1,0:T(8,128)}, u32[]{:S(2)}) copy-start(f32[1,8,16,128]{3,2,1,0:T(8,128)} %get-tuple-element.202) | copy-start | bytes 196612
  230.0 9.0 %copy-start.106 = (f32[2,8,16,128]{3,2,1,0:T(8,128)S(1)}, f32[2,8,16,128]{3,2,1,0:T(8,128)}, u32[]{:S(2)}) copy-start(f32[2,8,16,128]{3,2,1,0:T(8,128)} %get-tuple-element.219) | copy-start | bytes 393220
  243.0 7.1 %copy-start.71 = (f32[2,8,16,128]{2,1,3,0:T(8,128)S(1)}, f32[2,8,16,128]{2,1,3,0:T(8,128)}, u32[]{:S(2)}) copy-start(f32[2,8,16,128]{2,1,3,0:T(8,128)} %copy.593) | copy-start | bytes 393220
  243.0 7.4 %copy-start.74 = (f32[2,8,16,128]{2,1,3,0:T(8,128)S(1)}, f32[2,8,16,128]{2,1,3,0:T(8,128)}, u32[]{:S(2)}) copy-start(f32[2,8,16,128]{2,1,3,0:T(8,128)} %copy.594) | copy-start | bytes 393220
  243.0 7.7 %copy-start.77 = (f32[2,8,16,128]{2,1,3,0:T(8,128)S(1)}, f32[2,8,16,128]{2,1,3,0:T(8,128)}, u32[]{:S(2)}) copy-start(f32[2,8,16,128]{2,1,3,0:T(8,128)} %copy.591) | copy-start | bytes 393220
  243.0 8.0 %copy-start.80 = (f32[2,8,16,128]{2,1,3,0:T(8,128)S(1)}, f32[2,8,16,128]{2,1,3,0:T(8,128)}, u32[]{:S(2)}) copy-start(f32[2,8,16,128]{2,1,3,0:T(8,128)} %copy.592) | copy-start | bytes 393220
  243.0 8.3 %copy-start.82 = (f32[2,8,16,128]{2,1,3,0:T(8,128)S(1)}, f32[2,8,16,128]{2,1,3,0:T(8,128)}, u32[]{:S(2)}) copy-start(f32[2,8,16,128]{2,1,3,0:T(8,128)} %copy.589) | copy-start | bytes 393220
  243.0 8.6 %copy-start.84 = (f32[2,8,16,128]{2,1,3,0:T(8,128)S(1)}, f32[2,8,16,128]{2,1,3,0:T(8,128)}, u32[]{:S(2)}) copy-start(f32[2,8,16,128]{2,1,3,0:T(8,128)} %copy.590) | copy-start | bytes 393220
  243.0 8.8 %copy-start.87 = (f32[2,8,16,127]{2,1,3,0:T(8,128)S(1)}, f32[2,8,16,127]{2,1,3,0:T(8,128)}, u32[]{:S(2)}) copy-start(f32[2,8,16,127]{2,1,3,0:T(8,128)} %get-tuple-element.118) | copy-start | bytes 390148
  277.2 10.5 %copy-start.97 = (f32[1,8,16,128]{2,1,3,0:T(8,128)S(1)}, f32[1,8,16,128]{2,1,3,0:T(8,128)}, u32[]{:S(2)}) copy-start(f32[1,8,16,128]{2,1,3,0:T(8,128)} %copy.567) | copy-start | bytes 196612
  277.2 10.5 %copy-start.98 = (f32[1,8,16,128]{2,1,3,0:T(8,128)S(1)}, f32[1,8,16,128]{2,1,3,0:T(8,128)}, u32[]{:S(2)}) copy-start(f32[1,8,16,128]{2,1,3,0:T(8,128)} %copy.568) | copy-start | bytes 196612
  277.2 10.5 %copy-start.99 = (f32[1,8,16,128]{2,1,3,0:T(8,128)S(1)}, f32[1,8,16,128]{2,1,3,0:T(8,128)}, u32[]{:S(2)}) copy-start(f32[1,8,16,128]{2,1,3,0:T(8,128)} %copy.565) | copy-start | bytes 196612
  277.2 10.5 %copy-start.100 = (f32[1,8,16,128]{2,1,3,0:T(8,128)S(1)}, f32[1,8,16,128]{2,1,3,0:T(8,128)}, u32[]{:S(2)}) copy-start(f32[1,8,16,128]{2,1,3,0:T(8,128)} %copy.566) | copy-start | bytes 196612
  278.3 9.4 %copy-start.93 = (f32[1,8,16,128]{2,1,3,0:T(8,128)S(1)}, f32[1,8,16,128]{2,1,3,0:T(8,128)}, u32[]{:S(2)}) copy-start(f32[1,8,16,128]{2,1,3,0:T(8,128)} %copy.571) | copy-start | bytes 196612
  278.3 9.4 %copy-start.94 = (f32[1,8,16,128]{2,1,3,0:T(8,128)S(1)}, f32[1,8,16,128]{2,1,3,0:T(8,128)}, u32[]{:S(2)}) copy-start(f32[1,8,16,128]{2,1,3,0:T(8,128)} %copy.572) | copy-start | bytes 196612
  278.3 9.4 %copy-start.95 = (f32[1,8,16,128]{2,1,3,0:T(8,128)S(1)}, f32[1,8,16,128]{2,1,3,0:T(8,128)}, u32[]{:S(2)}) copy-start(f32[1,8,16,128]{2,1,3,0:T(8,128)} %copy.569) | copy-start | bytes 196612
  278.3 9.4 %copy-start.96 = (f32[1,8,16,128]{2,1,3,0:T(8,128)S(1)}, f32[1,8,16,128]{2,1,3,0:T(8,128)}, u32[]{:S(2)}) copy-start(f32[1,8,16,128]{2,1,3,0:T(8,128)} %copy.570) | copy-start | bytes 196612
  279.5 8.2 %copy-start.36 = (f32[8,12,128]{1,0,2:T(8,128)S(1)}, f32[8,12,128]{1,0,2:T(8,128)}, u32[]{:S(2)}) copy-start(f32[8,12,128]{1,0,2:T(8,128)} %get-tuple-element.174) | copy-start | bytes 147460
  279.5 8.2 %copy-start.38 = (f32[8,12,128]{1,0,2:T(8,128)S(1)}, f32[8,12,128]{1,0,2:T(8,128)}, u32[]{:S(2)}) copy-start(f32[8,12,128]{1,0,2:T(8,128)} %get-tuple-element.175) | copy-start | bytes 147460
  279.5 8.3 %copy-start.40 = (f32[8,13,128]{1,0,2:T(8,128)S(1)}, f32[8,13,128]{1,0,2:T(8,128)}, u32[]{:S(2)}) copy-start(f32[8,13,128]{1,0,2:T(8,128)} %get-tuple-element.172) | copy-start | bytes 159748
  279.5 8.3 %copy-start.42 = (f32[8,13,128]{1,0,2:T(8,128)S(1)}, f32[8,13,128]{1,0,2:T(8,128)}, u32[]{:S(2)}) copy-start(f32[8,13,128]{1,0,2:T(8,128)} %get-tuple-element.173) | copy-start | bytes 159748
  279.5 8.3 %copy-start.44 = (f32[8,14,128]{1,0,2:T(8,128)S(1)}, f32[8,14,128]{1,0,2:T(8,128)}, u32[]{:S(2)}) copy-start(f32[8,14,128]{1,0,2:T(8,128)} %get-tuple-element.170) | copy-start | bytes 172036
  279.5 8.3 %copy-start.46 = (f32[8,14,128]{1,0,2:T(8,128)S(1)}, f32[8,14,128]{1,0,2:T(8,128)}, u32[]{:S(2)}) copy-start(f32[8,14,128]{1,0,2:T(8,128)} %get-tuple-element.171) | copy-start | bytes 172036
  279.5 8.3 %copy-start.48 = (f32[8,15,128]{1,0,2:T(8,128)S(1)}, f32[8,15,128]{1,0,2:T(8,128)}, u32[]{:S(2)}) copy-start(f32[8,15,128]{1,0,2:T(8,128)} %get-tuple-element.168) | copy-start | bytes 184324
  279.5 8.3 %copy-start.50 = (f32[8,15,128]{1,0,2:T(8,128)S(1)}, f32[8,15,128]{1,0,2:T(8,128)}, u32[]{:S(2)}) copy-start(f32[8,15,128]{1,0,2:T(8,128)} %get-tuple-element.169) | copy-start | bytes 184324
  281.8 13.5 %collective-permute-start.6 = (f32[2,4,16,128]{2,1,3,0:T(4,128)}, f32[2,4,16,128]{2,1,3,0:T(4,128)}, u32[]{:S(2)}, u32[]{:S(2)}) collective-permute-start(f32[2,4,16,128]{2,1,3,0:T(4,128)} %get-tuple-element.117), channel_id=1, source_target_pairs={{1,0},{2,1},{3,2},{4,3},{5,4},{6,5},{7,6},{8,7},{9,8},{10,9},{11,1... | collective-permute-start | bytes 196616 | tf_op jit(solution)/shard_map/ppermute | solution.py:28
  283.7 13.6 %collective-permute-start.7 = (f32[2,4,16,128]{2,1,3,0:T(4,128)}, f32[2,4,16,128]{2,1,3,0:T(4,128)}, u32[]{:S(2)}, u32[]{:S(2)}) collective-permute-start(f32[2,4,16,128]{2,1,3,0:T(4,128)} %get-tuple-element.116), channel_id=1, source_target_pairs={{0,1},{1,2},{2,3},{3,4},{4,5},{5,6},{6,7},{7,8},{8,9},{9,10},{10,1... | collective-permute-start | bytes 196616 | tf_op jit(solution)/shard_map/ppermute | solution.py:26
  322.4 7.1 %copy-start.62 = (f32[2,8,16,128]{2,1,3,0:T(8,128)S(1)}, f32[2,8,16,128]{2,1,3,0:T(8,128)}, u32[]{:S(2)}) copy-start(f32[2,8,16,128]{2,1,3,0:T(8,128)} %copy.617) | copy-start | bytes 393220
  322.4 7.4 %copy-start.63 = (f32[2,8,16,128]{2,1,3,0:T(8,128)S(1)}, f32[2,8,16,128]{2,1,3,0:T(8,128)}, u32[]{:S(2)}) copy-start(f32[2,8,16,128]{2,1,3,0:T(8,128)} %copy.618) | copy-start | bytes 393220
  322.4 7.7 %copy-start.66 = (f32[2,8,16,128]{2,1,3,0:T(8,128)S(1)}, f32[2,8,16,128]{2,1,3,0:T(8,128)}, u32[]{:S(2)}) copy-start(f32[2,8,16,128]{2,1,3,0:T(8,128)} %copy.615) | copy-start | bytes 393220
  322.4 8.4 %copy-start.69 = (f32[2,8,16,128]{2,1,3,0:T(8,128)S(1)}, f32[2,8,16,128]{2,1,3,0:T(8,128)}, u32[]{:S(2)}) copy-start(f32[2,8,16,128]{2,1,3,0:T(8,128)} %copy.616) | copy-start | bytes 393220
  329.2 7.9 %copy-start.3 = (f32[2,16,16,128]{2,1,3,0:T(8,128)}, f32[2,16,16,128]{2,1,3,0:T(8,128)S(1)}, u32[]{:S(2)}) copy-start(f32[2,16,16,128]{2,1,3,0:T(8,128)S(1)} %multiply_add_fusion) | copy-start | bytes 786436
  337.3 8.2 %copy-start.111 = (f32[1,8,16,128]{3,2,1,0:T(8,128)S(1)}, f32[1,8,16,128]{3,2,1,0:T(8,128)}, u32[]{:S(2)}) copy-start(f32[1,8,16,128]{3,2,1,0:T(8,128)} %get-tuple-element.251) | copy-start | bytes 196612
  340.9 7.6 %copy-start.108 = (f32[1,8,16,128]{3,2,1,0:T(8,128)S(1)}, f32[1,8,16,128]{3,2,1,0:T(8,128)}, u32[]{:S(2)}) copy-start(f32[1,8,16,128]{3,2,1,0:T(8,128)} %get-tuple-element.211) | copy-start | bytes 196612
  351.6 7.6 %copy-start.1 = (f32[8,16,128]{1,0,2:T(8,128)S(1)}, f32[8,16,128]{1,0,2:T(8,128)}, u32[]{:S(2)}) copy-start(f32[8,16,128]{1,0,2:T(8,128)} %copy-done) | copy-start | bytes 196612
  (76 other events, 394.3 us)
where the time goes:
time: 371 us; the launch traced here: 364 us
  local copies, waits for them, and re-layouts  196 us (53%)
  other arithmetic  124 us (33%)
  starting transfers between devices  30.9 us (8%)
  waiting for transfers between devices  10.5 us (3%)
    slice x50, local copies, waits for them, and re-layouts, window(): lax.slice_in_dim(array_in, begin_at, begin_at + extent, axis=direction)  74.5 us
    slice x36, local copies, waits for them, and re-layouts, moved(): lax.slice_in_dim(field, offset, length, axis=direction)  55.5 us
    unnamed x278, local copies, waits for them, and re-layouts  39.4 us
    another operation x21, other arithmetic, advance(): return (jnp.stack([p_next, q_next]), (slope_x, slope_y, slope_z))  30.1 us
    add x4, other arithmetic, first_along(): summed + first_coeffs[offset - 1] * (moved(field, direction, offset) - mo...  26.4 us
    add x4, other arithmetic, advance(): cosine * cosine * second_z + sine * sine * second_x  22.9 us
    ppermute x4, starting transfers between devices, padded_2(): lax.ppermute(tail, axis, [(i, (i + 1) % count) for i in range(ends)])  16.7 us
    mul x2, other arithmetic, angle_image(): scaled = (cosine + 1.0) * (0.5 * (FINE - 1))  9.83 us
  transfers between devices with their start and end apart: 9, of which 3 were waited for; matrix products, arithmetic and copies ran while one was open for 62% of the time, Pallas kernels for 0%

commit v1 on v0

v1 whole, which is shorter than its diff:
```python
import functools

import jax
import jax.numpy as jnp
from jax import lax
from jax.experimental import pallas as pl
from jax.experimental.pallas import tpu as pltpu
from jax.sharding import PartitionSpec as P

STEPS = 4
IMAGE_EVERY = 2
NBIN = 8
REC_DEPTH = 2
REACH = 4
HALO = 2 * REACH
YPAD = 8

SECOND = (-205.0 / 72.0, 8.0 / 5.0, -1.0 / 5.0, 8.0 / 315.0, -1.0 / 560.0)
FIRST = (4.0 / 5.0, -1.0 / 5.0, 4.0 / 105.0, -1.0 / 280.0)


def each_row(count, width, body):
    if width <= 16:
        for row in range(count):
            body(row)
    else:
        lax.fori_loop(0, count, lambda row, carry: (body(row), carry)[1], 0)


def second(centre, pairs):
    total = SECOND[0] * centre
    for k in range(1, 5):
        plus, minus = pairs(k)
        total = total + SECOND[k] * (plus + minus)
    return total


def first(pairs):
    total = None
    for k in range(1, 5):
        plus, minus = pairs(k)
        term = FIRST[k - 1] * (plus - minus)
        total = term if total is None else total + term
    return total


def depth_diffs(field, want_second):
    depth = field.shape[-1]
    lane = lax.broadcasted_iota(jnp.int32, field.shape, 1)
    shifted = {}
    for k in range(1, 5):
        plus = jnp.where(lane < depth - k, pltpu.roll(field, depth - k, axis=1), 0.0)
        minus = jnp.where(lane >= k, pltpu.roll(field, k, axis=1), 0.0)
        shifted[k] = (plus, minus)
    slope = first(lambda k: shifted[k])
    return slope, second(field, lambda k: shifted[k]) if want_second else None


def sine_terms(angle):
    half = 0.5 * angle
    sq = half * half
    s = 1.0
    for n in (12 * 13, 10 * 11, 8 * 9, 6 * 7, 4 * 5, 2 * 3):
        s = 1.0 - sq * s * (1.0 / n)
    s = s * half
    c = 1.0
    for n in (13 * 14, 11 * 12, 9 * 10, 7 * 8, 5 * 6, 3 * 4, 1 * 2):
        c = 1.0 - sq * c * (1.0 / n)
    sine = 2.0 * s * c
    cosine = 1.0 - 2.0 * s * s
    return sine * sine, 2.0 * sine * cosine


def injected(flat, traces, step, row, width):
    cell = lax.broadcasted_iota(jnp.int32, (width, flat.shape[1]), 0) + row * width
    hit = jnp.where(cell == flat, traces[step : step + 1, :], 0.0)
    return jnp.sum(hit, axis=1, keepdims=True)


def time_step(rows, width, fields, earlier, coeffs, slopes, curves, inject, emit):
    p, q = fields
    slope_p, slope_q = slopes
    curve_p, curve_q = curves
    inner = slice(YPAD, YPAD + width)

    def along_depth(row):
        slope_p[row], curve_p[row] = depth_diffs(p[row, inner, :], True)
        slope_q[row], curve_q[row] = depth_diffs(q[row], True)

    each_row(rows + 2 * REACH, width, along_depth)

    def update(row):
        at = row + REACH
        now_p = p[at, inner, :]
        now_q = q[at]
        xx_p = second(now_p, lambda k: (p[at + k, inner, :], p[at - k, inner, :]))
        xx_q = second(now_q, lambda k: (q[at + k], q[at - k]))
        xz_p = first(lambda k: (slope_p[at + k], slope_p[at - k]))
        xz_q = first(lambda k: (slope_q[at + k], slope_q[at - k]))
        yy_p = second(
            now_p,
            lambda k: (
                p[at, YPAD + k : YPAD + k + width, :],
                p[at, YPAD - k : YPAD - k + width, :],
            ),
        )
        speed, gain, mixed, sine_sq, sine_double = coeffs(row)
        tilt_p = sine_sq * (xx_p - curve_p[at]) + sine_double * xz_p
        tilt_q = sine_sq * (xx_q - curve_q[at]) + sine_double * xz_q
        across = xx_p + yy_p - tilt_p
        rotated = curve_q[at] + tilt_q
        prev_p, prev_q = earlier(row)
        next_p = 2.0 * now_p - prev_p + (gain * across + mixed * rotated)
        next_q = 2.0 * now_q - prev_q + (mixed * across + speed * rotated)
        lane = lax.broadcasted_iota(jnp.int32, next_p.shape, 1)
        next_p = next_p + jnp.where(lane == REC_DEPTH, inject(row), 0.0)
        emit(row, next_p, next_q)

    each_row(rows, width, update)


def flux_row(row, width, p, slope_p, before):
    at = row + REACH
    now = p[at, YPAD : YPAD + width, :]
    back = before - now
    slope_x = first(
        lambda k: (p[at + k, YPAD : YPAD + width, :], p[at - k, YPAD : YPAD + width, :])
    )
    slope_y = first(
        lambda k: (p[at, YPAD + k : YPAD + k + width, :], p[at, YPAD - k : YPAD - k + width, :])
    )
    return now, (back * slope_x, back * slope_y, back * slope_p[at])


def clear_pads(ref, width):
    rows, _, depth = ref.shape
    zeros = jnp.zeros((rows, YPAD, depth), jnp.float32)
    ref[:, :YPAD, :] = zeros
    ref[:, YPAD + width :, :] = zeros


def place(dst_p, dst_q, centre, sides, width):
    rows = centre.shape[1]
    inner = pl.ds(YPAD, width)
    dst_p[pl.ds(HALO, rows), inner, :] = centre[0]
    dst_q[pl.ds(HALO, rows)] = centre[1]
    for at, read in sides:
        dst_p[pl.ds(at, HALO), inner, :] = read(0, HALO)
        dst_q[pl.ds(at, HALO)] = read(HALO, HALO)


def side_starts(rows, reach):
    odd = lax.rem(lax.axis_index("gx"), 2)
    on_chip = jnp.where(odd == 1, 0, rows + reach)
    off_chip = jnp.where(odd == 1, rows + reach, 0)
    return on_chip, off_chip


def receivers(row_ref, column_ref, rows, width):
    begin = lax.axis_index("gx") * rows - REACH
    count = row_ref.shape[0]
    local_row = row_ref[...].reshape(1, count) - begin
    inside = (local_row >= 0) & (local_row < rows + 2 * REACH)
    return jnp.where(inside, local_row * width + column_ref[...].reshape(1, count), -1)


def two_steps(
    t, rows, width, p, q, first_prev, coeffs, flat, traces, scratch, mid_emit, emit, second_prev
):
    slope_p, slope_q, curve_p, curve_q, p1, q1 = scratch
    inner = slice(YPAD, YPAD + width)
    clear_pads(p1, width)

    def keep(row, next_p, next_q):
        p1[row, inner, :] = next_p
        q1[row] = next_q
        mid_emit(row, next_p, next_q)

    time_step(
        rows + 2 * REACH,
        width,
        (p, q),
        first_prev,
        lambda row: [coeffs[c, row] for c in range(5)],
        (slope_p, slope_q),
        (curve_p, curve_q),
        lambda row: injected(flat, traces, t, row, width),
        keep,
    )
    time_step(
        rows,
        width,
        (p1, q1),
        second_prev,
        lambda row: [coeffs[c, row + REACH] for c in range(5)],
        (slope_p, slope_q),
        (curve_p, curve_q),
        lambda row: injected(flat, traces, t + 1, row + REACH, width),
        emit,
    )


def early_kernel(
    now,
    prev,
    speed,
    epsilon,
    delta,
    tilt,
    on_chip,
    off_chip,
    receiver_row,
    receiver_column,
    traces,
    out,
    mid,
    flux,
    coeffs,
    p,
    q,
    prev_ext,
    *scratch,
):
    rows, width = now.shape[1], now.shape[2]
    near, far = side_starts(rows, HALO)
    clear_pads(p, width)
    place(
        p,
        q,
        now,
        (
            (near, lambda a, n: on_chip[pl.ds(a, n)]),
            (far, lambda a, n: off_chip[pl.ds(a, n)]),
        ),
        width,
    )
    near, far = side_starts(rows, REACH)
    base = 2 * HALO

    def derive(at, s, e, d, a):
        coeffs[0, at] = s
        coeffs[1, at] = s * (1.0 + 2.0 * e)
        coeffs[2, at] = s * jnp.sqrt(1.0 + 2.0 * d)
        coeffs[3, at], coeffs[4, at] = sine_terms(a)

    each_row(
        rows,
        width,
        lambda r: derive(r + REACH, speed[r], epsilon[r], delta[r], tilt[r]),
    )
    for f in range(2):
        prev_ext[f, pl.ds(REACH, rows)] = prev[f]
    for at, part in ((near, on_chip), (far, off_chip)):
        for f in range(2):
            prev_ext[f, pl.ds(at, REACH)] = part[pl.ds(base + f * REACH, REACH)]
        for r in range(REACH):
            derive(at + r, *[part[base + (2 + m) * REACH + r] for m in range(4)])

    flat = receivers(receiver_row, receiver_column, rows, width)

    def mid_emit(row, next_p, next_q):
        mid[0, row] = next_p
        mid[1, row] = next_q

    def emit(row, next_p, next_q):
        out[0, row] = next_p
        out[1, row] = next_q

    two_steps(
        0,
        rows,
        width,
        p,
        q,
        lambda row: (prev_ext[0, row], prev_ext[1, row]),
        coeffs,
        flat,
        traces,
        scratch,
        mid_emit,
        emit,
        lambda row: (now[0, row], now[1, row]),
    )
    slope_p, p1 = scratch[0], scratch[4]

    def fluxes(row):
        _, parts = flux_row(row, width, p1, slope_p, now[0, row])
        for a in range(3):
            flux[a, row] = parts[a]

    each_row(rows, width, fluxes)


def late_kernel(
    now,
    mid,
    flux,
    coeffs,
    on_chip,
    off_chip,
    receiver_row,
    receiver_column,
    traces,
    source,
    table,
    images,
    out,
    p,
    q,
    *scratch,
):
    rows, width = now.shape[1], now.shape[2]
    near, far = side_starts(rows, HALO)
    clear_pads(p, width)
    place(
        p,
        q,
        now,
        (
            (near, lambda a, n: on_chip[a // HALO]),
            (far, lambda a, n: off_chip[a // HALO]),
        ),
        width,
    )
    flat = receivers(receiver_row, receiver_column, rows, width)

    def emit(row, next_p, next_q):
        out[0, row] = next_p
        out[1, row] = next_q

    two_steps(
        2,
        rows,
        width,
        p,
        q,
        lambda row: (mid[0, row], mid[1, row]),
        coeffs,
        flat,
        traces,
        scratch,
        lambda row, next_p, next_q: None,
        emit,
        lambda row: (now[0, row], now[1, row]),
    )
    slope_p, p1 = scratch[0], scratch[4]

    fine = table.shape[0]
    starts = [jnp.int32(0)] * NBIN
    for f in range(fine):
        named = table[f]
        for b in range(1, NBIN):
            starts[b] = starts[b] + (named < b).astype(jnp.int32)
    offsets = [s.astype(jnp.float32) - 1.0 for s in starts] + [jnp.float32(fine - 1)]

    def image_row(row):
        totals = [None] * NBIN
        late = flux_row(row, width, p1, slope_p, now[0, row])
        early = (mid[0, row + REACH], (flux[0, row], flux[1, row], flux[2, row]))
        for n, (field, (fx, fy, fz)) in enumerate((early, late)):
            s0, s1, s2, s3 = [source[n, c, row].astype(jnp.float32) for c in range(4)]
            dot = s1 * fx + s2 * fy + s3 * fz
            lengths = jnp.sqrt(s1 * s1 + s2 * s2 + s3 * s3) * jnp.sqrt(fx * fx + fy * fy + fz * fz)
            cosine = dot / jnp.maximum(lengths, 1.0)
            scaled = (cosine + 1.0) * (0.5 * (fine - 1))
            strength = s0 * field
            ramps = [jnp.clip(scaled - o, 0.0, 1.0) * strength for o in offsets]
            for b in range(NBIN):
                term = ramps[b] - ramps[b + 1]
                totals[b] = term if totals[b] is None else totals[b] + term
        for b in range(NBIN):
            images[b, row] = totals[b].astype(images.dtype)

    each_row(rows, width, image_row)


def local(
    wave_now,
    wave_prev,
    speed_term,
    thomsen_epsilon,
    thomsen_delta,
    tilt_angle,
    source_store,
    receiver_row,
    receiver_column,
    receiver_traces,
    angle_table,
):
    _, rows, width, depth = wave_now.shape
    count = lax.axis_size("gx")
    odd = lax.rem(lax.axis_index("gx"), 2)
    on_chip_pairs = [(i, i ^ 1) for i in range(count)]
    off_chip_pairs = [(i, i + 1) for i in range(1, count - 1, 2)]
    off_chip_pairs = off_chip_pairs + [(b, a) for a, b in off_chip_pairs]

    def pack(tail):
        def edge(x, n, dim):
            return lax.dynamic_slice_in_dim(x, jnp.where(tail, rows - n, 0), n, axis=dim)

        wave = wave_now if rows == HALO else edge(wave_now, HALO, 1)
        parts = [wave.reshape(2 * HALO, width, depth)]
        parts.append(edge(wave_prev, REACH, 1).reshape(2 * REACH, width, depth))
        for x in (speed_term, thomsen_epsilon, thomsen_delta, tilt_angle):
            parts.append(edge(x, REACH, 0))
        return jnp.concatenate(parts, axis=0)

    off_chip = lax.ppermute(pack(odd == 1), "gx", off_chip_pairs)
    on_chip = lax.ppermute(pack(odd == 0), "gx", on_chip_pairs)
    arrived = lax.all_to_all(source_store, "gx", split_axis=2, concat_axis=3, tiled=True)

    f32 = jnp.float32
    ext, wide = rows + 2 * REACH, rows + 2 * HALO
    vmem = pl.BlockSpec(memory_space=pltpu.VMEM)
    smem = pl.BlockSpec(memory_space=pltpu.SMEM)
    plane = (width, depth)
    padded = (width + 2 * YPAD, depth)
    steps_scratch = [
        pltpu.VMEM((wide,) + plane, f32),
        pltpu.VMEM((wide,) + plane, f32),
        pltpu.VMEM((wide,) + plane, f32),
        pltpu.VMEM((wide,) + plane, f32),
        pltpu.VMEM((ext,) + padded, f32),
        pltpu.VMEM((ext,) + plane, f32),
    ]
    wave_scratch = [pltpu.VMEM((wide,) + padded, f32), pltpu.VMEM((wide,) + plane, f32)]
    cells = rows * width * depth
    limit = 60 * 1024 * 1024
    now, mid, flux, coeffs = pl.pallas_call(
        early_kernel,
        out_shape=(
            jax.ShapeDtypeStruct((2, rows) + plane, f32),
            jax.ShapeDtypeStruct((2, ext) + plane, f32),
            jax.ShapeDtypeStruct((3, rows) + plane, f32),
            jax.ShapeDtypeStruct((5, ext) + plane, f32),
        ),
        in_specs=[vmem] * 11,
        out_specs=(vmem,) * 4,
        scratch_shapes=wave_scratch + [pltpu.VMEM((2, ext) + plane, f32)] + steps_scratch,
        compiler_params=pltpu.CompilerParams(vmem_limit_bytes=limit),
        cost_estimate=pl.CostEstimate(flops=600 * cells, bytes_accessed=120 * cells, transcendentals=0),
        name="early",
    )(
        wave_now,
        wave_prev,
        speed_term,
        thomsen_epsilon,
        thomsen_delta,
        tilt_angle,
        on_chip,
        off_chip,
        receiver_row,
        receiver_column,
        receiver_traces,
    )

    def sides(x, tail):
        if rows == HALO:
            return x
        return lax.dynamic_slice_in_dim(x, jnp.where(tail, rows - HALO, 0), HALO, axis=1)

    off_chip = lax.ppermute(sides(now, odd == 1), "gx", off_chip_pairs)
    on_chip = lax.ppermute(sides(now, odd == 0), "gx", on_chip_pairs)
    return pl.pallas_call(
        late_kernel,
        out_shape=(
            jax.ShapeDtypeStruct((NBIN, rows) + plane, jnp.bfloat16),
            jax.ShapeDtypeStruct((2, rows) + plane, f32),
        ),
        in_specs=[vmem] * 10 + [smem],
        out_specs=(vmem, vmem),
        scratch_shapes=wave_scratch + steps_scratch,
        compiler_params=pltpu.CompilerParams(vmem_limit_bytes=limit),
        cost_estimate=pl.CostEstimate(flops=700 * cells, bytes_accessed=120 * cells, transcendentals=0),
        name="late",
    )(
        now,
        mid,
        flux,
        coeffs,
        on_chip,
        off_chip,
        receiver_row,
        receiver_column,
        receiver_traces,
        arrived,
        angle_table,
    )


def solution(mesh):
    placed = (
        P("shot", "gx", None, None),
        P("shot", "gx", None, None),
        P("gx", None, None),
        P("gx", None, None),
        P("gx", None, None),
        P("gx", None, None),
        P("shot", None, None, "gx", None),
        P("shot"),
        P("shot"),
        P("shot", None),
        P(),
    )
    return jax.shard_map(
        local,
        mesh=mesh,
        in_specs=placed,
        out_specs=(P("shot", "gx", None, None), P("shot", "gx", None, None)),
        check_vma=False,
    )
```

time: 371 us -> 43.2 us (0.12); the launches traced: 364 us -> 42.6 us
  local copies, waits for them, and re-layouts: 196 us -> 9.18 us
  other arithmetic: 124 us -> 0 us
  starting transfers between devices: 30.9 us -> 15.5 us
  Pallas kernels: 0 us -> 7.9 us
    slice x88 -> x0, local copies, waits for them, and re-layouts: 132 us -> none  [the longest x50 74.5 us: window(): lax.slice_in_dim(array_in, begin_at, begin_at + extent, axis=direction)]
    add x14 -> x0, other arithmetic: 60.2 us -> none  [the longest x4 26.4 us: first_along(): summed + first_coeffs[offset - 1] * (moved(field, direction, offset) - mo...]
    unnamed x278 -> x28, local copies, waits for them, and re-layouts: 39.4 us -> 8.28 us
    another operation x21 -> x0, other arithmetic: 30.1 us -> none  [advance(): return (jnp.stack([p_next, q_next]), (slope_x, slope_y, slope_z))]
    ppermute x8 -> x4, starting transfers between devices: 24.4 us -> 8.06 us  [the longest x1 4.39 us: local(): off_chip = lax.ppermute(sides(now, odd == 1), 'gx', off_chip_pairs)]
    mul x5 -> x0, other arithmetic: 13.1 us -> none  [the longest x2 9.83 us: angle_image(): scaled = (cosine + 1.0) * (0.5 * (FINE - 1))]
    concatenate x8 -> x0, other arithmetic: 9.19 us -> none  [padded_2(): jnp.concatenate([lax.ppermute(tail, axis, [(i, (i + 1) % count) for i in...]
    pallas_call x0 -> x2, Pallas kernels: none -> 7.9 us  [the longest x1 4.14 us: local(): pl.pallas_call(late_kernel, out_shape=(jax.ShapeDtypeStruct((NBIN, rows)...]
  transfers between devices with their start and end apart: 9 -> 5, of which waited for: 3 -> 2; matrix products, arithmetic and copies ran while one was open for 62% -> 2% of each run, Pallas kernels for 0% -> 9%
where the time goes in v1:
time: 43.2 us; the launch traced here: 42.6 us
  starting transfers between devices  15.5 us (36%)
  waiting for transfers between devices  9.31 us (22%)
  local copies, waits for them, and re-layouts  9.18 us (21%)
  Pallas kernels  7.9 us (18%)
  between operations  0.75 us (2%)
    unnamed x28, local copies, waits for them, and re-layouts  8.28 us
    all_to_all x1, starting transfers between devices, local(): lax.all_to_all(source_store, 'gx', split_axis=2, concat_axis=3, tiled=True)  7.44 us
    ppermute x1, waiting for transfers between devices, local(): off_chip = lax.ppermute(pack(odd == 1), 'gx', off_chip_pairs)  7.43 us
    ppermute x1, starting transfers between devices, local(): off_chip = lax.ppermute(sides(now, odd == 1), 'gx', off_chip_pairs)  4.39 us
    pallas_call x1, Pallas kernels, local(): pl.pallas_call(late_kernel, out_shape=(jax.ShapeDtypeStruct((NBIN, rows)...  4.14 us
    pallas_call x1, Pallas kernels, local(): pl.pallas_call(early_kernel, out_shape=(jax.ShapeDtypeStruct((2, rows) +...  3.76 us
    ppermute x1, starting transfers between devices, local(): off_chip = lax.ppermute(pack(odd == 1), 'gx', off_chip_pairs)  3.53 us
    ppermute x1, waiting for transfers between devices, local(): off_chip = lax.ppermute(sides(now, odd == 1), 'gx', off_chip_pairs)  1.87 us
  transfers between devices with their start and end apart: 5, of which 2 were waited for; matrix products, arithmetic and copies ran while one was open for 2% of the time, Pallas kernels for 9%

profile of v1, /device:TPU:1, one launch (start us, length us, event | category | flops | bytes accessed | tf_op | source)
XLA Modules:
  0.0 42.6 jit_solution(11587932930268876229)
XLA Ops:
  0.6 1.9 %copy.15 = bf16[2,4,128,1,128]{4,1,0,3,2:T(4,128)(2,1)} copy(bf16[2,4,128,1,128]{4,2,3,1,0:T(8,128)(2,1)} %param.17) | data formatting | bytes 524288 | tf_op args[6]
  2.5 0.0 copy-start
  2.5 7.4 %all-to-all-start = ((bf16[2,4,128,1,128]{4,1,0,3,2:T(4,128)(2,1)}), bf16[2,4,128,1,128]{4,1,0,3,2:T(4,128)(2,1)S(1)}, u32[]{:S(2)}, u32[]{:S(2)}) async-start(bf16[2,4,128,1,128]{4,1,0,3,2:T(4,128)(2,1)} %copy.15), calls=%async_computation | async-start | bytes 524288 | tf_op jit(solution)/shard_map/all_to_all | solution.py:410
  9.9 0.0 copy-done
  10.0 0.0 copy-start.1
  10.0 0.9 %copy-done.1 = f32[2,8,16,128]{3,2,1,0:T(8,128)S(1)} copy-done((f32[2,8,16,128]{3,2,1,0:T(8,128)S(1)}, f32[2,8,16,128]{3,2,1,0:T(8,128)}, u32[]{:S(2)}) %copy-start.1) | copy-done | bytes 131096
  10.9 0.0 copy-start.4
  10.9 0.8 %copy-done.4 = f32[8,16,128]{2,1,0:T(8,128)S(1)} copy-done((f32[8,16,128]{2,1,0:T(8,128)S(1)}, f32[8,16,128]{2,1,0:T(8,128)}, u32[]{:S(2)}) %copy-start.4) | copy-done | bytes 65560
  11.7 0.0 copy-start.5
  11.7 0.8 %copy-done.5 = f32[8,16,128]{2,1,0:T(8,128)S(1)} copy-done((f32[8,16,128]{2,1,0:T(8,128)S(1)}, f32[8,16,128]{2,1,0:T(8,128)}, u32[]{:S(2)}) %copy-start.5) | copy-done | bytes 65560
  12.6 0.0 copy-start.6
  12.6 0.8 %copy-done.6 = f32[8,16,128]{2,1,0:T(8,128)S(1)} copy-done((f32[8,16,128]{2,1,0:T(8,128)S(1)}, f32[8,16,128]{2,1,0:T(8,128)}, u32[]{:S(2)}) %copy-start.6) | copy-done | bytes 65560
  13.4 0.0 copy-start.7
  13.4 0.8 %copy-done.7 = f32[8,16,128]{2,1,0:T(8,128)S(1)} copy-done((f32[8,16,128]{2,1,0:T(8,128)S(1)}, f32[8,16,128]{2,1,0:T(8,128)}, u32[]{:S(2)}) %copy-start.7) | copy-done | bytes 65560
  14.3 3.5 %collective-permute-start.1 = (f32[40,16,128]{2,1,0:T(8,128)S(1)}, f32[40,16,128]{2,1,0:T(8,128)S(1)}, u32[]{:S(2)}, u32[]{:S(2)}) collective-permute-start(f32[40,16,128]{2,1,0:T(8,128)S(1)} %get-tuple-element.12), channel_id=1, source_target_pairs={{1,2},{3,4},{5,6},{7,8},{9,10},{11,12},{13,14},{2,1},{4,3},{6,5},{... | collective-permute-start | bytes 983048 | tf_op jit(solution)/shard_map/ppermute | solution.py:408
  17.8 0.1 collective-permute-start
  17.9 7.4 %collective-permute-done.1.off_chip = f32[40,16,128]{2,1,0:T(8,128)S(1)} collective-permute-done((f32[40,16,128]{2,1,0:T(8,128)S(1)}, f32[40,16,128]{2,1,0:T(8,128)S(1)}, u32[]{:S(2)}, u32[]{:S(2)}) %collective-permute-start.1) | collective-permute-done | bytes 327712 | tf_op jit(solution)/shard_map/ppermute | solution.py:408
  25.3 0.0 copy-start.2
  25.3 0.0 collective-permute-done.on_chip
  25.3 0.7 %copy-done.2 = f32[40,16,128]{2,1,0:T(8,128)} copy-done((f32[40,16,128]{2,1,0:T(8,128)}, f32[40,16,128]{2,1,0:T(8,128)S(1)}, u32[]{:S(2)}) %copy-start.2) | copy-done | bytes 327704
  26.0 0.0 copy-start.3
  26.0 0.7 %copy-done.3 = f32[40,16,128]{2,1,0:T(8,128)} copy-done((f32[40,16,128]{2,1,0:T(8,128)}, f32[40,16,128]{2,1,0:T(8,128)S(1)}, u32[]{:S(2)}) %copy-start.3) | copy-done | bytes 327704
  26.8 3.8 %early.1 = (f32[2,8,16,128]{3,2,1,0:T(8,128)}, f32[2,16,16,128]{3,2,1,0:T(8,128)}, f32[3,8,16,128]{3,2,1,0:T(8,128)}, f32[5,16,16,128]{3,2,1,0:T(8,128)}) custom-call(f32[2,8,16,128]{3,2,1,0:T(8,128)} %now.1, f32[2,8,16,128]{3,2,1,0:T(8,128)} %prev.1, f32[8,16,128]{2,1,0:T(8,128)} %speed.1, f32[8,16,128]{2,1,0:T(8,128)} %epsilon.1, f32[8,16,128]{2,1,0:T(8,128)} %delta.1, ...), custom_call_target="tpu_custom_call" | custom-call | flops 9830400 | bytes 1966080 | tf_op jit(solution)/shard_map/early/pallas_call | solution.py:429
  30.5 4.4 %collective-permute-start.3 = (f32[2,8,16,128]{3,2,1,0:T(8,128)}, f32[2,8,16,128]{3,2,1,0:T(8,128)S(1)}, u32[]{:S(2)}, u32[]{:S(2)}) collective-permute-start(f32[2,8,16,128]{3,2,1,0:T(8,128)} %get-tuple-element.6.now), channel_id=1, source_target_pairs={{1,2},{3,4},{5,6},{7,8},{9,10},{11,12},{13,14},{2,1},{4,3},{6,5},{... | collective-permute-start | bytes 393224 | tf_op jit(solution)/shard_map/ppermute | solution.py:462
  34.9 0.1 collective-permute-start.2
  35.0 0.0 all-to-all-done
  35.0 0.9 %copy.21 = bf16[2,4,16,8,1,128]{5,2,3,1,0,4:T(8,128)(2,1)} copy(bf16[2,4,16,8,1,128]{5,1,0,3,2,4:T(4,128)(2,1)S(1)} %bitcast.9) | data formatting | bytes 524288 | tf_op jit(solution)/shard_map/all_to_all | solution.py:410
  35.9 1.9 %collective-permute-done.3.off_chip = f32[2,8,16,128]{3,2,1,0:T(8,128)S(1)} collective-permute-done((f32[2,8,16,128]{3,2,1,0:T(8,128)}, f32[2,8,16,128]{3,2,1,0:T(8,128)S(1)}, u32[]{:S(2)}, u32[]{:S(2)}) %collective-permute-start.3) | collective-permute-done | bytes 131104 | tf_op jit(solution)/shard_map/ppermute | solution.py:462
  37.8 0.0 copy-start.8
  37.8 0.0 collective-permute-done.2.on_chip
  37.8 0.0 copy-start.9
  37.8 0.6 %copy-done.8 = f32[2,8,16,128]{3,2,1,0:T(8,128)} copy-done((f32[2,8,16,128]{3,2,1,0:T(8,128)}, f32[2,8,16,128]{3,2,1,0:T(8,128)S(1)}, u32[]{:S(2)}) %copy-start.8) | copy-done | bytes 131096
  38.4 0.1 copy-done.9
  38.5 4.1 %late.1 = (bf16[8,8,16,128]{3,2,1,0:T(8,128)(2,1)}, f32[2,8,16,128]{3,2,1,0:T(8,128)}) custom-call(f32[2,8,16,128]{3,2,1,0:T(8,128)} %get-tuple-element.6.now, f32[2,16,16,128]{3,2,1,0:T(8,128)} %get-tuple-element.7.mid, f32[3,8,16,128]{3,2,1,0:T(8,128)} %get-tuple-element.8.flux, f32[5,16,16,128]{3,2,1,0:T(8,128)} %get-tuple-element.9.coeffs, ...), custom_call_target="tpu_custom_call" | custom-call | flops 11468800 | bytes 1966080 | tf_op jit(solution)/shard_map/late/pallas_call | solution.py:464
  (9 shorter events, 0.1 us)
Async XLA Ops:
  2.5 7.4 %copy-start = (f32[2,8,16,128]{3,2,1,0:T(8,128)S(1)}, f32[2,8,16,128]{3,2,1,0:T(8,128)}, u32[]{:S(2)}) copy-start(f32[2,8,16,128]{3,2,1,0:T(8,128)} %now.1) | copy-start | bytes 393220
  2.5 32.5 %all-to-all-start = ((bf16[2,4,128,1,128]{4,1,0,3,2:T(4,128)(2,1)}), bf16[2,4,128,1,128]{4,1,0,3,2:T(4,128)(2,1)S(1)}, u32[]{:S(2)}, u32[]{:S(2)}) async-start(bf16[2,4,128,1,128]{4,1,0,3,2:T(4,128)(2,1)} %copy.15), calls=%async_computation | async-start | bytes 524288 | tf_op jit(solution)/shard_map/all_to_all | solution.py:410
  10.0 0.9 %copy-start.1 = (f32[2,8,16,128]{3,2,1,0:T(8,128)S(1)}, f32[2,8,16,128]{3,2,1,0:T(8,128)}, u32[]{:S(2)}) copy-start(f32[2,8,16,128]{3,2,1,0:T(8,128)} %prev.1) | copy-start | bytes 393220
  10.9 0.8 %copy-start.4 = (f32[8,16,128]{2,1,0:T(8,128)S(1)}, f32[8,16,128]{2,1,0:T(8,128)}, u32[]{:S(2)}) copy-start(f32[8,16,128]{2,1,0:T(8,128)} %speed.1) | copy-start | bytes 196612
  11.7 0.8 %copy-start.5 = (f32[8,16,128]{2,1,0:T(8,128)S(1)}, f32[8,16,128]{2,1,0:T(8,128)}, u32[]{:S(2)}) copy-start(f32[8,16,128]{2,1,0:T(8,128)} %epsilon.1) | copy-start | bytes 196612
  12.6 0.8 %copy-start.6 = (f32[8,16,128]{2,1,0:T(8,128)S(1)}, f32[8,16,128]{2,1,0:T(8,128)}, u32[]{:S(2)}) copy-start(f32[8,16,128]{2,1,0:T(8,128)} %delta.1) | copy-start | bytes 196612
  13.4 0.8 %copy-start.7 = (f32[8,16,128]{2,1,0:T(8,128)S(1)}, f32[8,16,128]{2,1,0:T(8,128)}, u32[]{:S(2)}) copy-start(f32[8,16,128]{2,1,0:T(8,128)} %tilt.1) | copy-start | bytes 196612
  14.3 11.0 %collective-permute-start.1 = (f32[40,16,128]{2,1,0:T(8,128)S(1)}, f32[40,16,128]{2,1,0:T(8,128)S(1)}, u32[]{:S(2)}, u32[]{:S(2)}) collective-permute-start(f32[40,16,128]{2,1,0:T(8,128)S(1)} %get-tuple-element.12), channel_id=1, source_target_pairs={{1,2},{3,4},{5,6},{7,8},{9,10},{11,12},{13,14},{2,1},{4,3},{6,5},{... | collective-permute-start | bytes 983048 | tf_op jit(solution)/shard_map/ppermute | solution.py:408
  17.8 7.5 %collective-permute-start = (f32[40,16,128]{2,1,0:T(8,128)S(1)}, f32[40,16,128]{2,1,0:T(8,128)S(1)}, u32[]{:S(2)}, u32[]{:S(2)}) collective-permute-start(f32[40,16,128]{2,1,0:T(8,128)S(1)} %get-tuple-element.13), channel_id=1, source_target_pairs={{0,1},{1,0},{2,3},{3,2},{4,5},{5,4},{6,7},{7,6},{8,9},{9,8},{10,11... | collective-permute-start | bytes 983048 | tf_op jit(solution)/shard_map/ppermute | solution.py:409
  25.3 0.7 %copy-start.2 = (f32[40,16,128]{2,1,0:T(8,128)}, f32[40,16,128]{2,1,0:T(8,128)S(1)}, u32[]{:S(2)}) copy-start(f32[40,16,128]{2,1,0:T(8,128)S(1)} %collective-permute-done.1.off_chip) | copy-start | bytes 983044
  26.0 0.7 %copy-start.3 = (f32[40,16,128]{2,1,0:T(8,128)}, f32[40,16,128]{2,1,0:T(8,128)S(1)}, u32[]{:S(2)}) copy-start(f32[40,16,128]{2,1,0:T(8,128)S(1)} %collective-permute-done.on_chip) | copy-start | bytes 983044
  30.5 7.2 %collective-permute-start.3 = (f32[2,8,16,128]{3,2,1,0:T(8,128)}, f32[2,8,16,128]{3,2,1,0:T(8,128)S(1)}, u32[]{:S(2)}, u32[]{:S(2)}) collective-permute-start(f32[2,8,16,128]{3,2,1,0:T(8,128)} %get-tuple-element.6.now), channel_id=1, source_target_pairs={{1,2},{3,4},{5,6},{7,8},{9,10},{11,12},{13,14},{2,1},{4,3},{6,5},{... | collective-permute-start | bytes 393224 | tf_op jit(solution)/shard_map/ppermute | solution.py:462
  34.9 2.9 %collective-permute-start.2 = (f32[2,8,16,128]{3,2,1,0:T(8,128)}, f32[2,8,16,128]{3,2,1,0:T(8,128)S(1)}, u32[]{:S(2)}, u32[]{:S(2)}) collective-permute-start(f32[2,8,16,128]{3,2,1,0:T(8,128)} %get-tuple-element.6.now), channel_id=1, source_target_pairs={{0,1},{1,0},{2,3},{3,2},{4,5},{5,4},{6,7},{7,6},{8,9},{9,8},{10,11... | collective-permute-start | bytes 393224 | tf_op jit(solution)/shard_map/ppermute | solution.py:463
  37.8 0.7 %copy-start.8 = (f32[2,8,16,128]{3,2,1,0:T(8,128)}, f32[2,8,16,128]{3,2,1,0:T(8,128)S(1)}, u32[]{:S(2)}) copy-start(f32[2,8,16,128]{3,2,1,0:T(8,128)S(1)} %collective-permute-done.3.off_chip) | copy-start | bytes 393220
  37.8 0.7 %copy-start.9 = (f32[2,8,16,128]{3,2,1,0:T(8,128)}, f32[2,8,16,128]{3,2,1,0:T(8,128)S(1)}, u32[]{:S(2)}) copy-start(f32[2,8,16,128]{3,2,1,0:T(8,128)S(1)} %collective-permute-done.2.on_chip) | copy-start | bytes 393220

commit v2 on v1

--- a/solution.py
+++ b/solution.py
@@ -1,5 +1,3 @@
-import functools
-
 import jax
 import jax.numpy as jnp
 from jax import lax
@@ -7,8 +5,7 @@
 from jax.experimental.pallas import tpu as pltpu
 from jax.sharding import PartitionSpec as P
 
-STEPS = 4
-IMAGE_EVERY = 2
+
 NBIN = 8
 REC_DEPTH = 2
 REACH = 4
@@ -198,6 +195,34 @@
         lambda row: injected(flat, traces, t + 1, row + REACH, width),
         emit,
     )
+
+
+def pack_kernel(now, prev, speed, epsilon, delta, tilt, far, near, sems):
+    rows = now.shape[1]
+    odd = lax.rem(lax.axis_index("gx"), 2)
+    copies = []
+
+    def copy(src, dst):
+        copies.append(pltpu.make_async_copy(src, dst, sems.at[len(copies)]))
+        copies[-1].start()
+
+    for out, tail in ((far, odd), (near, 1 - odd)):
+        wave_at = tail * (rows - HALO)
+        edge_at = tail * (rows - REACH)
+        for f in range(2):
+            copy(now.at[f, pl.ds(wave_at, HALO)], out.at[pl.ds(f * HALO, HALO)])
+        for f in range(2):
+            copy(
+                prev.at[f, pl.ds(edge_at, REACH)],
+                out.at[pl.ds(2 * HALO + f * REACH, REACH)],
+            )
+        for m, field in enumerate((speed, epsilon, delta, tilt)):
+            copy(
+                field.at[pl.ds(edge_at, REACH)],
+                out.at[pl.ds(2 * HALO + (2 + m) * REACH, REACH)],
+            )
+    for one in copies:
+        one.wait()
 
 
 def early_kernel(
@@ -394,21 +419,6 @@
     off_chip_pairs = [(i, i + 1) for i in range(1, count - 1, 2)]
     off_chip_pairs = off_chip_pairs + [(b, a) for a, b in off_chip_pairs]
 
-    def pack(tail):
-        def edge(x, n, dim):
-            return lax.dynamic_slice_in_dim(x, jnp.where(tail, rows - n, 0), n, axis=dim)
-
-        wave = wave_now if rows == HALO else edge(wave_now, HALO, 1)
-        parts = [wave.reshape(2 * HALO, width, depth)]
-        parts.append(edge(wave_prev, REACH, 1).reshape(2 * REACH, width, depth))
-        for x in (speed_term, thomsen_epsilon, thomsen_delta, tilt_angle):
-            parts.append(edge(x, REACH, 0))
-        return jnp.concatenate(parts, axis=0)
-
-    off_chip = lax.ppermute(pack(odd == 1), "gx", off_chip_pairs)
-    on_chip = lax.ppermute(pack(odd == 0), "gx", on_chip_pairs)
-    arrived = lax.all_to_all(source_store, "gx", split_axis=2, concat_axis=3, tiled=True)
-
     f32 = jnp.float32
     ext, wide = rows + 2 * REACH, rows + 2 * HALO
     vmem = pl.BlockSpec(memory_space=pltpu.VMEM)
@@ -425,7 +435,33 @@
     ]
     wave_scratch = [pltpu.VMEM((wide,) + padded, f32), pltpu.VMEM((wide,) + plane, f32)]
     cells = rows * width * depth
-    limit = 60 * 1024 * 1024
+    plane_bytes = 4 * width * depth
+
+    def limit(planes):
+        return 4 * 1024 * 1024 + planes * plane_bytes
+
+    packed = jax.ShapeDtypeStruct((2 * HALO + 6 * REACH,) + plane, f32)
+    medium = (speed_term, thomsen_epsilon, thomsen_delta, tilt_angle)
+    in_hbm = pl.BlockSpec(memory_space=pltpu.HBM)
+    far_pack, near_pack = pl.pallas_call(
+        pack_kernel,
+        out_shape=(packed, packed),
+        in_specs=[in_hbm] * 6,
+        out_specs=(vmem, vmem),
+        scratch_shapes=[pltpu.SemaphoreType.DMA((16,))],
+        compiler_params=pltpu.CompilerParams(vmem_limit_bytes=limit(80)),
+        name="pack",
+    )(
+        *[
+            pltpu.with_memory_space_constraint(x, pltpu.HBM)
+            for x in (wave_now, wave_prev, *medium)
+        ]
+    )
+    off_chip = lax.ppermute(far_pack, "gx", off_chip_pairs)
+    on_chip = lax.ppermute(near_pack, "gx", on_chip_pairs)
+    arrived = lax.all_to_all(
+        source_store, "gx", split_axis=2, concat_axis=3, tiled=True
+    )
     now, mid, flux, coeffs = pl.pallas_call(
         early_kernel,
         out_shape=(
@@ -437,16 +473,13 @@
         in_specs=[vmem] * 11,
         out_specs=(vmem,) * 4,
         scratch_shapes=wave_scratch + [pltpu.VMEM((2, ext) + plane, f32)] + steps_scratch,
-        compiler_params=pltpu.CompilerParams(vmem_limit_bytes=limit),
+        compiler_params=pltpu.CompilerParams(vmem_limit_bytes=limit(26 * wide)),
         cost_estimate=pl.CostEstimate(flops=600 * cells, bytes_accessed=120 * cells, transcendentals=0),
         name="early",
     )(
         wave_now,
         wave_prev,
-        speed_term,
-        thomsen_epsilon,
-        thomsen_delta,
-        tilt_angle,
+        *medium,
         on_chip,
         off_chip,
         receiver_row,
@@ -470,7 +503,7 @@
         in_specs=[vmem] * 10 + [smem],
         out_specs=(vmem, vmem),
         scratch_shapes=wave_scratch + steps_scratch,
-        compiler_params=pltpu.CompilerParams(vmem_limit_bytes=limit),
+        compiler_params=pltpu.CompilerParams(vmem_limit_bytes=limit(26 * wide)),
         cost_estimate=pl.CostEstimate(flops=700 * cells, bytes_accessed=120 * cells, transcendentals=0),
         name="late",
     )(

time: 43.2 us -> 36.2 us (0.84)
  local copies, waits for them, and re-layouts: 9.18 us -> 2.74 us
  Pallas kernels: 7.9 us -> 6.35 us
  waiting for transfers between devices: 9.31 us -> 10.5 us
    unnamed x28 -> x21, local copies, waits for them, and re-layouts: 8.28 us -> 2.57 us
    pallas_call x1, Pallas kernels: 3.76 us -> 1.84 us  [local(): pl.pallas_call(early_kernel, out_shape=(jax.ShapeDtypeStruct((2, rows) +...]
    pallas_call x0 -> x1, Pallas kernels: none -> 1.27 us  [local(): pl.pallas_call(pack_kernel, out_shape=(packed, packed), in_specs=[in_hbm]...]
    pallas_call x1, Pallas kernels: 4.14 us -> 3.24 us  [local(): pl.pallas_call(late_kernel, out_shape=(jax.ShapeDtypeStruct((NBIN, rows)...]
    all_to_all x1, local copies, waits for them, and re-layouts: 0.89 us -> 0.18 us  [local(): lax.all_to_all(source_store, 'gx', split_axis=2, concat_axis=3, tiled=True)]
    ppermute x2, waiting for transfers between devices: 7.43 us -> 8.11 us  [the longest x1 8.1 us: local(): off_chip = lax.ppermute(far_pack, 'gx', off_chip_pairs)]
    ppermute x1, waiting for transfers between devices: 1.87 us -> 2.37 us  [local(): off_chip = lax.ppermute(sides(now, odd == 1), 'gx', off_chip_pairs)]
  transfers between devices with their start and end apart: 5 -> 5, of which waited for: 2 -> 2; matrix products, arithmetic and copies ran while one was open for 2% -> 0% of each run, Pallas kernels for 9% -> 9%
where the time goes in v2:
time: 36.2 us; the launch traced here: 35.9 us
  starting transfers between devices  15.5 us (43%)
  waiting for transfers between devices  10.5 us (29%)
  Pallas kernels  6.35 us (18%)
  local copies, waits for them, and re-layouts  2.74 us (8%)
  between operations  0.81 us (2%)
    ppermute x1, waiting for transfers between devices, local(): off_chip = lax.ppermute(far_pack, 'gx', off_chip_pairs)  8.1 us
    all_to_all x1, starting transfers between devices, local(): lax.all_to_all(source_store, 'gx', split_axis=2, concat_axis=3, tiled=True)  7.31 us
    ppermute x1, starting transfers between devices, local(): off_chip = lax.ppermute(sides(now, odd == 1), 'gx', off_chip_pairs)  4.4 us
    ppermute x1, starting transfers between devices, local(): off_chip = lax.ppermute(far_pack, 'gx', off_chip_pairs)  3.54 us
    pallas_call x1, Pallas kernels, local(): pl.pallas_call(late_kernel, out_shape=(jax.ShapeDtypeStruct((NBIN, rows)...  3.24 us
    unnamed x21, local copies, waits for them, and re-layouts  2.57 us
    ppermute x1, waiting for transfers between devices, local(): off_chip = lax.ppermute(sides(now, odd == 1), 'gx', off_chip_pairs)  2.37 us
    pallas_call x1, Pallas kernels, local(): pl.pallas_call(early_kernel, out_shape=(jax.ShapeDtypeStruct((2, rows) +...  1.84 us
  transfers between devices with their start and end apart: 5, of which 2 were waited for; matrix products, arithmetic and copies ran while one was open for 0% of the time, Pallas kernels for 9%

profile of v2, /device:TPU:1, one launch (start us, length us, event | category | flops | bytes accessed | tf_op | source)
XLA Modules:
  0.0 35.9 jit_solution(3655262319449603411)
XLA Ops:
  0.6 1.9 %copy.15 = bf16[2,4,128,1,128]{4,1,0,3,2:T(4,128)(2,1)} copy(bf16[2,4,128,1,128]{4,2,3,1,0:T(8,128)(2,1)} %param.17) | data formatting | bytes 524288 | tf_op args[6]
  2.5 7.3 %all-to-all-start = ((bf16[2,4,128,1,128]{4,1,0,3,2:T(4,128)(2,1)}), bf16[2,4,128,1,128]{4,1,0,3,2:T(4,128)(2,1)S(1)}, u32[]{:S(2)}, u32[]{:S(2)}) async-start(bf16[2,4,128,1,128]{4,1,0,3,2:T(4,128)(2,1)} %copy.15), calls=%async_computation | async-start | bytes 524288 | tf_op jit(solution)/shard_map/all_to_all | solution.py:462
  9.8 0.0 copy-start
  9.8 0.0 copy-start.1
  9.8 0.0 copy-start.2
  9.8 0.0 copy-start.3
  9.8 0.0 copy-start.4
  9.9 0.0 copy-start.5
  9.9 1.3 %pack.1 = (f32[40,16,128]{2,1,0:T(8,128)S(1)}, f32[40,16,128]{2,1,0:T(8,128)S(1)}) custom-call(f32[2,8,16,128]{3,2,1,0:T(8,128)} %now.3, f32[2,8,16,128]{3,2,1,0:T(8,128)} %prev.3, f32[8,16,128]{2,1,0:T(8,128)} %speed.3, f32[8,16,128]{2,1,0:T(8,128)} %epsilon.3, f32[8,16,128]{2,1,0:T(8,128)} %delta.3, f32[8,16,128]{2,1,0:T(8,128)} %tilt.3), custom_call_target="tpu_custom_call" | custom-call | tf_op jit(solution)/shard_map/pack/pallas_call | solution.py:446
  11.1 0.0 copy-start.6
  11.2 0.0 copy-start.7
  11.2 0.0 copy-start.8
  11.2 0.2 collective-permute-start
  11.4 3.5 %collective-permute-start.1 = (f32[40,16,128]{2,1,0:T(8,128)S(1)}, f32[40,16,128]{2,1,0:T(8,128)S(1)}, u32[]{:S(2)}, u32[]{:S(2)}) collective-permute-start(f32[40,16,128]{2,1,0:T(8,128)S(1)} %get-tuple-element.9), channel_id=1, source_target_pairs={{1,2},{3,4},{5,6},{7,8},{9,10},{11,12},{13,14},{2,1},{4,3},{6,5},{... | collective-permute-start | bytes 983048 | tf_op jit(solution)/shard_map/ppermute | solution.py:460
  14.9 0.0 collective-permute-done.on_chip
  14.9 8.1 %collective-permute-done.1.off_chip = f32[40,16,128]{2,1,0:T(8,128)S(1)} collective-permute-done((f32[40,16,128]{2,1,0:T(8,128)S(1)}, f32[40,16,128]{2,1,0:T(8,128)S(1)}, u32[]{:S(2)}, u32[]{:S(2)}) %collective-permute-start.1) | collective-permute-done | bytes 327712 | tf_op jit(solution)/shard_map/ppermute | solution.py:460
  23.0 0.0 copy-done
  23.0 0.0 copy-done.1
  23.0 0.0 copy-done.2
  23.0 0.0 copy-done.3
  23.0 0.0 copy-done.4
  23.0 0.0 copy-done.5
  23.0 0.0 copy-done.6
  23.1 0.0 copy-done.7
  23.1 0.0 copy-done.8
  23.1 1.8 %early.1 = (f32[2,8,16,128]{3,2,1,0:T(8,128)S(1)}, f32[2,16,16,128]{3,2,1,0:T(8,128)S(1)}, f32[3,8,16,128]{3,2,1,0:T(8,128)S(1)}, f32[5,16,16,128]{3,2,1,0:T(8,128)S(1)}) custom-call(f32[2,8,16,128]{3,2,1,0:T(8,128)S(1)} %copy-done, f32[2,8,16,128]{3,2,1,0:T(8,128)S(1)} %copy-done.1, f32[8,16,128]{2,1,0:T(8,128)S(1)} %copy-done.2, ...), custom_call_target="tpu_custom_call" | custom-call | flops 9830400 | bytes 1966080 | tf_op jit(solution)/shard_map/early/pallas_call | solution.py:465
  24.9 4.4 %collective-permute-start.3 = (f32[2,8,16,128]{3,2,1,0:T(8,128)S(1)}, f32[2,8,16,128]{3,2,1,0:T(8,128)S(1)}, u32[]{:S(2)}, u32[]{:S(2)}) collective-permute-start(f32[2,8,16,128]{3,2,1,0:T(8,128)S(1)} %get-tuple-element.10.now), channel_id=1, source_target_pairs={{1,2},{3,4},{5,6},{7,8},{9,10},{11,12},{13,14},{2,1},{4,3},{6,5},{... | collective-permute-start | bytes 393224 | tf_op jit(solution)/shard_map/ppermute | solution.py:495
  29.3 0.1 collective-permute-start.2
  29.4 0.0 all-to-all-done
  29.4 0.2 copy.21
  29.6 2.4 %collective-permute-done.3.off_chip = f32[2,8,16,128]{3,2,1,0:T(8,128)S(1)} collective-permute-done((f32[2,8,16,128]{3,2,1,0:T(8,128)S(1)}, f32[2,8,16,128]{3,2,1,0:T(8,128)S(1)}, u32[]{:S(2)}, u32[]{:S(2)}) %collective-permute-start.3) | collective-permute-done | bytes 131104 | tf_op jit(solution)/shard_map/ppermute | solution.py:495
  32.0 0.0 collective-permute-done.2.on_chip
  32.0 0.0 copy-start.9
  32.0 0.7 %copy-done.9 = s32[32]{0:T(128)S(1)} copy-done((s32[32]{0:T(128)S(1)}, s32[32]{0:T(128)}, u32[]{:S(2)}) %copy-start.9) | copy-done | bytes 152
  32.6 3.2 %late.1 = (bf16[8,8,16,128]{3,2,1,0:T(8,128)(2,1)}, f32[2,8,16,128]{3,2,1,0:T(8,128)}) custom-call(f32[2,8,16,128]{3,2,1,0:T(8,128)S(1)} %get-tuple-element.10.now, f32[2,16,16,128]{3,2,1,0:T(8,128)S(1)} %get-tuple-element.11.mid, f32[3,8,16,128]{3,2,1,0:T(8,128)S(1)} %get-tuple-element.12.flux, f32[5,16,16,128]{3,2,1,0:T(8,128)S(1)} %get-tuple-element.13.coeffs, ...), custom_call_target="tpu_custom_call" | custom-call | flops 11468800 | bytes 1966080 | tf_op jit(solution)/shard_map/late/pallas_call | solution.py:497
Async XLA Ops:
  2.5 26.9 %all-to-all-start = ((bf16[2,4,128,1,128]{4,1,0,3,2:T(4,128)(2,1)}), bf16[2,4,128,1,128]{4,1,0,3,2:T(4,128)(2,1)S(1)}, u32[]{:S(2)}, u32[]{:S(2)}) async-start(bf16[2,4,128,1,128]{4,1,0,3,2:T(4,128)(2,1)} %copy.15), calls=%async_computation | async-start | bytes 524288 | tf_op jit(solution)/shard_map/all_to_all | solution.py:462
  9.8 13.2 %copy-start = (f32[2,8,16,128]{3,2,1,0:T(8,128)S(1)}, f32[2,8,16,128]{3,2,1,0:T(8,128)}, u32[]{:S(2)}) copy-start(f32[2,8,16,128]{3,2,1,0:T(8,128)} %now.3) | copy-start | bytes 393220
  9.8 13.2 %copy-start.1 = (f32[2,8,16,128]{3,2,1,0:T(8,128)S(1)}, f32[2,8,16,128]{3,2,1,0:T(8,128)}, u32[]{:S(2)}) copy-start(f32[2,8,16,128]{3,2,1,0:T(8,128)} %prev.3) | copy-start | bytes 393220
  9.8 13.2 %copy-start.2 = (f32[8,16,128]{2,1,0:T(8,128)S(1)}, f32[8,16,128]{2,1,0:T(8,128)}, u32[]{:S(2)}) copy-start(f32[8,16,128]{2,1,0:T(8,128)} %speed.3) | copy-start | bytes 196612
  9.8 13.2 %copy-start.3 = (f32[8,16,128]{2,1,0:T(8,128)S(1)}, f32[8,16,128]{2,1,0:T(8,128)}, u32[]{:S(2)}) copy-start(f32[8,16,128]{2,1,0:T(8,128)} %epsilon.3) | copy-start | bytes 196612
  9.8 13.2 %copy-start.4 = (f32[8,16,128]{2,1,0:T(8,128)S(1)}, f32[8,16,128]{2,1,0:T(8,128)}, u32[]{:S(2)}) copy-start(f32[8,16,128]{2,1,0:T(8,128)} %delta.3) | copy-start | bytes 196612
  9.9 13.2 %copy-start.5 = (f32[8,16,128]{2,1,0:T(8,128)S(1)}, f32[8,16,128]{2,1,0:T(8,128)}, u32[]{:S(2)}) copy-start(f32[8,16,128]{2,1,0:T(8,128)} %tilt.3) | copy-start | bytes 196612
  11.1 11.9 %copy-start.6 = (f32[4,128]{1,0:T(4,128)S(1)}, f32[4,128]{1,0:T(4,128)}, u32[]{:S(2)}) copy-start(f32[4,128]{1,0:T(4,128)} %traces.3) | copy-start | bytes 6148
  11.2 11.9 %copy-start.7 = (s32[128]{0:T(128)S(1)}, s32[128]{0:T(128)}, u32[]{:S(2)}) copy-start(s32[128]{0:T(128)} %receiver_row.3) | copy-start | bytes 1540
  11.2 11.9 %copy-start.8 = (s32[128]{0:T(128)S(1)}, s32[128]{0:T(128)}, u32[]{:S(2)}) copy-start(s32[128]{0:T(128)} %receiver_column.3) | copy-start | bytes 1540
  11.2 3.7 %collective-permute-start = (f32[40,16,128]{2,1,0:T(8,128)S(1)}, f32[40,16,128]{2,1,0:T(8,128)S(1)}, u32[]{:S(2)}, u32[]{:S(2)}) collective-permute-start(f32[40,16,128]{2,1,0:T(8,128)S(1)} %get-tuple-element.8), channel_id=1, source_target_pairs={{0,1},{1,0},{2,3},{3,2},{4,5},{5,4},{6,7},{7,6},{8,9},{9,8},{10,11... | collective-permute-start | bytes 983048 | tf_op jit(solution)/shard_map/ppermute | solution.py:461
  11.4 11.7 %collective-permute-start.1 = (f32[40,16,128]{2,1,0:T(8,128)S(1)}, f32[40,16,128]{2,1,0:T(8,128)S(1)}, u32[]{:S(2)}, u32[]{:S(2)}) collective-permute-start(f32[40,16,128]{2,1,0:T(8,128)S(1)} %get-tuple-element.9), channel_id=1, source_target_pairs={{1,2},{3,4},{5,6},{7,8},{9,10},{11,12},{13,14},{2,1},{4,3},{6,5},{... | collective-permute-start | bytes 983048 | tf_op jit(solution)/shard_map/ppermute | solution.py:460
  24.9 7.0 %collective-permute-start.3 = (f32[2,8,16,128]{3,2,1,0:T(8,128)S(1)}, f32[2,8,16,128]{3,2,1,0:T(8,128)S(1)}, u32[]{:S(2)}, u32[]{:S(2)}) collective-permute-start(f32[2,8,16,128]{3,2,1,0:T(8,128)S(1)} %get-tuple-element.10.now), channel_id=1, source_target_pairs={{1,2},{3,4},{5,6},{7,8},{9,10},{11,12},{13,14},{2,1},{4,3},{6,5},{... | collective-permute-start | bytes 393224 | tf_op jit(solution)/shard_map/ppermute | solution.py:495
  29.3 2.6 %collective-permute-start.2 = (f32[2,8,16,128]{3,2,1,0:T(8,128)S(1)}, f32[2,8,16,128]{3,2,1,0:T(8,128)S(1)}, u32[]{:S(2)}, u32[]{:S(2)}) collective-permute-start(f32[2,8,16,128]{3,2,1,0:T(8,128)S(1)} %get-tuple-element.10.now), channel_id=1, source_target_pairs={{0,1},{1,0},{2,3},{3,2},{4,5},{5,4},{6,7},{7,6},{8,9},{9,8},{10,11... | collective-permute-start | bytes 393224 | tf_op jit(solution)/shard_map/ppermute | solution.py:496
  32.0 0.7 %copy-start.9 = (s32[32]{0:T(128)S(1)}, s32[32]{0:T(128)}, u32[]{:S(2)}) copy-start(s32[32]{0:T(128)} %table.1) | copy-start | bytes 388

commit v3 on v2

v3 whole, which is shorter than its diff:
```python
import jax
import jax.numpy as jnp
import numpy as np
from jax import lax
from jax.experimental import pallas as pl
from jax.experimental.pallas import tpu as pltpu
from jax.sharding import PartitionSpec as P


STEPS = 4
NBIN = 8
REC_DEPTH = 2
REACH = 4
HALO = 2 * REACH
YPAD = 8

SECOND = (-205.0 / 72.0, 8.0 / 5.0, -1.0 / 5.0, 8.0 / 315.0, -1.0 / 560.0)
FIRST = (4.0 / 5.0, -1.0 / 5.0, 4.0 / 105.0, -1.0 / 280.0)


def each_row(count, width, body):
    if width <= 16:
        for row in range(count):
            body(row)
    else:
        lax.fori_loop(0, count, lambda row, carry: (body(row), carry)[1], 0)


def each_chunk(count, width, body):
    size = max(1, min(count, 512 // width))
    while count % size:
        size -= 1
    if count // size <= 2:
        for start in range(0, count, size):
            body(start, size)
    else:
        lax.fori_loop(0, count // size, lambda i, carry: (body(i * size, size), carry)[1], 0)


def second(centre, pairs):
    total = SECOND[0] * centre
    for k in range(1, 5):
        plus, minus = pairs(k)
        total = total + SECOND[k] * (plus + minus)
    return total


def first(pairs):
    total = None
    for k in range(1, 5):
        plus, minus = pairs(k)
        term = FIRST[k - 1] * (plus - minus)
        total = term if total is None else total + term
    return total


def depth_matrices(depth):
    eye = [np.eye(depth, k=k, dtype=np.float64) for k in range(-4, 5)]
    slope = sum(np.float32(FIRST[k - 1]) * (eye[4 - k] - eye[4 + k]) for k in range(1, 5))
    curve = np.float32(SECOND[0]) * eye[4] + sum(
        np.float32(SECOND[k]) * (eye[4 - k] + eye[4 + k]) for k in range(1, 5)
    )
    rest = np.concatenate([slope, curve], axis=1).astype(np.float32)
    parts = []
    for _ in range(3):
        parts.append(rest.astype(jnp.bfloat16))
        rest = rest - parts[-1].astype(np.float32)
    return np.stack(parts)


def depth_diffs(field, matrices):
    depth = field.shape[1]
    high = field.astype(jnp.bfloat16)
    rest = field - high.astype(jnp.float32)
    middle = rest.astype(jnp.bfloat16)
    low = (rest - middle.astype(jnp.float32)).astype(jnp.bfloat16)
    m_high, m_middle, m_low = matrices[0], matrices[1], matrices[2]

    def product(left, top, bottom):
        return jnp.dot(
            left, jnp.concatenate([top, bottom], axis=0), preferred_element_type=jnp.float32
        )

    upper = jnp.concatenate([high, middle], axis=1)
    lower = jnp.concatenate([high, low], axis=1)
    both = (
        product(lower, m_low, m_high)
        + product(upper, m_middle, m_middle)
        + product(upper, m_high, m_high)
    )
    return both[:, :depth], both[:, depth:]


def depth_rows(read, slope, curve, begin, count, width, matrices, shift=0):
    def chunk(start, size):
        field = read(begin + start, size)
        depth = field.shape[-1]
        s, c = depth_diffs(field.reshape(size * width, depth), matrices)
        slope[pl.ds(begin + shift + start, size)] = s.reshape(size, width, depth)
        curve[pl.ds(begin + shift + start, size)] = c.reshape(size, width, depth)

    each_chunk(count, width, chunk)


def sine_terms(angle):
    half = 0.5 * angle
    sq = half * half
    s = 1.0
    for n in (12 * 13, 10 * 11, 8 * 9, 6 * 7, 4 * 5, 2 * 3):
        s = 1.0 - sq * s * (1.0 / n)
    s = s * half
    c = 1.0
    for n in (13 * 14, 11 * 12, 9 * 10, 7 * 8, 5 * 6, 3 * 4, 1 * 2):
        c = 1.0 - sq * c * (1.0 / n)
    sine = 2.0 * s * c
    cosine = 1.0 - 2.0 * s * s
    return sine * sine, 2.0 * sine * cosine


def derive(coeffs, at, s, e, d, a):
    coeffs[0, at] = s
    coeffs[1, at] = s * (1.0 + 2.0 * e)
    coeffs[2, at] = s * jnp.sqrt(1.0 + 2.0 * d)
    coeffs[3, at], coeffs[4, at] = sine_terms(a)


def receivers(row_ref, column_ref, rows, width):
    begin = lax.axis_index("gx") * rows - REACH
    count = row_ref.shape[0]
    local_row = row_ref[...].reshape(1, count) - begin
    inside = (local_row >= 0) & (local_row < rows + 2 * REACH)
    return jnp.where(inside, local_row * width + column_ref[...].reshape(1, count), -1)


def time_step(rows, width, fields, earlier, coeffs, slopes, curves, inject, emit):
    p, q = fields
    slope_p, slope_q = slopes
    curve_p, curve_q = curves
    inner = slice(YPAD, YPAD + width)

    def update(row):
        at = row + REACH
        now_p = p[at, inner, :]
        now_q = q[at]
        xx_p = second(now_p, lambda k: (p[at + k, inner, :], p[at - k, inner, :]))
        xx_q = second(now_q, lambda k: (q[at + k], q[at - k]))
        xz_p = first(lambda k: (slope_p[at + k], slope_p[at - k]))
        xz_q = first(lambda k: (slope_q[at + k], slope_q[at - k]))
        yy_p = second(
            now_p,
            lambda k: (
                p[at, YPAD + k : YPAD + k + width, :],
                p[at, YPAD - k : YPAD - k + width, :],
            ),
        )
        speed, gain, mixed, sine_sq, sine_double = coeffs(row)
        tilt_p = sine_sq * (xx_p - curve_p[at]) + sine_double * xz_p
        tilt_q = sine_sq * (xx_q - curve_q[at]) + sine_double * xz_q
        across = xx_p + yy_p - tilt_p
        rotated = curve_q[at] + tilt_q
        prev_p, prev_q = earlier(row)
        next_p = 2.0 * now_p - prev_p + (gain * across + mixed * rotated)
        next_q = 2.0 * now_q - prev_q + (mixed * across + speed * rotated)
        emit(row, next_p + inject(row), next_q)

    each_row(rows, width, update)


def flux_row(row, width, p, slope_z, before):
    at = row + REACH
    now = p[at, YPAD : YPAD + width, :]
    back = before - now
    slope_x = first(
        lambda k: (p[at + k, YPAD : YPAD + width, :], p[at - k, YPAD : YPAD + width, :])
    )
    slope_y = first(
        lambda k: (p[at, YPAD + k : YPAD + k + width, :], p[at, YPAD - k : YPAD - k + width, :])
    )
    return now, (back * slope_x, back * slope_y, back * slope_z)


def image_terms(source, n, row, field, flux, offsets, emit):
    fx, fy, fz = flux
    s0, s1, s2, s3 = [source[n, c, row].astype(jnp.float32) for c in range(4)]
    dot = s1 * fx + s2 * fy + s3 * fz
    lengths = jnp.sqrt(s1 * s1 + s2 * s2 + s3 * s3) * jnp.sqrt(fx * fx + fy * fy + fz * fz)
    cosine = dot / jnp.maximum(lengths, 1.0)
    scaled = (cosine + 1.0) * offsets[NBIN + 1 : NBIN + 2, :]
    strength = s0 * field
    ramps = [
        jnp.clip(scaled - offsets[b : b + 1, :], 0.0, 1.0) * strength for b in range(NBIN + 1)
    ]
    for b in range(NBIN):
        emit(b, ramps[b] - ramps[b + 1])


def clear_pads(ref, width):
    rows, _, depth = ref.shape
    zeros = jnp.zeros((rows, YPAD, depth), jnp.float32)
    ref[:, :YPAD, :] = zeros
    ref[:, YPAD + width :, :] = zeros


def place(dst_p, dst_q, centre, sides, width):
    rows = centre.shape[1]
    inner = pl.ds(YPAD, width)
    dst_p[pl.ds(HALO, rows), inner, :] = centre[0]
    dst_q[pl.ds(HALO, rows)] = centre[1]
    for at, read in sides:
        dst_p[pl.ds(at, HALO), inner, :] = read(0, HALO)
        dst_q[pl.ds(at, HALO)] = read(HALO, HALO)


def side_starts(rows, reach):
    odd = lax.rem(lax.axis_index("gx"), 2)
    on_chip = jnp.where(odd == 1, 0, rows + reach)
    off_chip = jnp.where(odd == 1, rows + reach, 0)
    return on_chip, off_chip


def two_steps(
    t, rows, width, waves, own, first_prev, coeffs, inject, matrices, scratch, mid_emit, emit, second_prev
):
    p, q = waves
    slope_p, slope_q, curve_p, curve_q, p1, q1 = scratch
    inner = slice(YPAD, YPAD + width)
    clear_pads(p1, width)
    for dst, src in zip((slope_p, slope_q, curve_p, curve_q), own):
        dst[pl.ds(HALO, rows)] = src

    def read_p(start, size):
        return p[pl.ds(start, size), inner, :]

    def read_q(start, size):
        return q[pl.ds(start, size)]

    for begin in (0, rows + HALO):
        depth_rows(read_p, slope_p, curve_p, begin, HALO, width, matrices)
        depth_rows(read_q, slope_q, curve_q, begin, HALO, width, matrices)

    def keep(row, next_p, next_q):
        p1[row, inner, :] = next_p
        q1[row] = next_q
        mid_emit(row, next_p, next_q)

    ext = rows + 2 * REACH
    time_step(
        ext,
        width,
        waves,
        first_prev,
        lambda row: [coeffs[c, row] for c in range(5)],
        (slope_p, slope_q),
        (curve_p, curve_q),
        lambda row: inject[t, row],
        keep,
    )
    depth_rows(lambda b, n: p1[pl.ds(b, n), inner, :], slope_p, curve_p, 0, ext, width, matrices)
    depth_rows(lambda b, n: q1[pl.ds(b, n)], slope_q, curve_q, 0, ext, width, matrices)
    time_step(
        rows,
        width,
        (p1, q1),
        second_prev,
        lambda row: [coeffs[c, row + REACH] for c in range(5)],
        (slope_p, slope_q),
        (curve_p, curve_q),
        lambda row: inject[t + 1, row + REACH],
        emit,
    )


def pack_kernel(now, prev, speed, epsilon, delta, tilt, far, near, sems):
    rows = now.shape[1]
    odd = lax.rem(lax.axis_index("gx"), 2)
    copies = []

    def copy(src, dst):
        copies.append(pltpu.make_async_copy(src, dst, sems.at[len(copies)]))
        copies[-1].start()

    for out, tail in ((far, odd), (near, 1 - odd)):
        wave_at = tail * (rows - HALO)
        edge_at = tail * (rows - REACH)
        for f in range(2):
            copy(now.at[f, pl.ds(wave_at, HALO)], out.at[pl.ds(f * HALO, HALO)])
        for f in range(2):
            copy(
                prev.at[f, pl.ds(edge_at, REACH)],
                out.at[pl.ds(2 * HALO + f * REACH, REACH)],
            )
        for m, field in enumerate((speed, epsilon, delta, tilt)):
            copy(
                field.at[pl.ds(edge_at, REACH)],
                out.at[pl.ds(2 * HALO + (2 + m) * REACH, REACH)],
            )
    for one in copies:
        one.wait()


def prep_kernel(
    now,
    speed,
    epsilon,
    delta,
    tilt,
    receiver_row,
    receiver_column,
    traces,
    table,
    matrices,
    coeffs,
    inject,
    slopes,
    curves,
    offsets,
):
    rows, width, depth = speed.shape
    each_row(
        rows,
        width,
        lambda r: derive(coeffs, r, speed[r], epsilon[r], delta[r], tilt[r]),
    )
    for f in range(2):
        depth_rows(
            lambda b, n: now[f, pl.ds(b, n)], slopes.at[f], curves.at[f], 0, rows, width, matrices
        )
    flat = receivers(receiver_row, receiver_column, rows, width)

    def samples(row):
        cell = lax.broadcasted_iota(jnp.int32, (width, flat.shape[1]), 0) + row * width
        lane = lax.broadcasted_iota(jnp.int32, (width, depth), 1)
        hit = cell == flat
        for t in range(STEPS):
            column = jnp.sum(jnp.where(hit, traces[t : t + 1, :], 0.0), axis=1, keepdims=True)
            inject[t, row] = jnp.where(lane == REC_DEPTH, column, 0.0)

    each_row(rows + 2 * REACH, width, samples)
    fine = table.shape[0]
    starts = [jnp.int32(0)] * NBIN
    for f in range(fine):
        named = table[f]
        for b in range(1, NBIN):
            starts[b] = starts[b] + (named < b).astype(jnp.int32)
    values = [s.astype(jnp.float32) - 1.0 for s in starts]
    values = values + [jnp.float32(fine - 1), jnp.float32(0.5 * (fine - 1))]
    for b, value in enumerate(values):
        offsets[b : b + 1, :] = jnp.full((1, depth), value, jnp.float32)


def early_kernel(
    now,
    prev,
    on_chip,
    off_chip,
    own_coeffs,
    inject,
    slopes,
    curves,
    matrices,
    out,
    mid,
    coeffs,
    slope_out,
    p,
    q,
    prev_ext,
    *scratch,
):
    rows, width = now.shape[1], now.shape[2]
    near, far = side_starts(rows, HALO)
    clear_pads(p, width)
    place(
        p,
        q,
        now,
        (
            (near, lambda a, n: on_chip[pl.ds(a, n)]),
            (far, lambda a, n: off_chip[pl.ds(a, n)]),
        ),
        width,
    )
    near, far = side_starts(rows, REACH)
    base = 2 * HALO
    for c in range(5):
        coeffs[c, pl.ds(REACH, rows)] = own_coeffs[c]
    for f in range(2):
        prev_ext[f, pl.ds(REACH, rows)] = prev[f]
    for at, part in ((near, on_chip), (far, off_chip)):
        for f in range(2):
            prev_ext[f, pl.ds(at, REACH)] = part[pl.ds(base + f * REACH, REACH)]
        for r in range(REACH):
            derive(coeffs, at + r, *[part[base + (2 + m) * REACH + r] for m in range(4)])

    def mid_emit(row, next_p, next_q):
        mid[0, row] = next_p
        mid[1, row] = next_q

    def emit(row, next_p, next_q):
        out[0, row] = next_p
        out[1, row] = next_q

    two_steps(
        0,
        rows,
        width,
        (p, q),
        (slopes[0], slopes[1], curves[0], curves[1]),
        lambda row: (prev_ext[0, row], prev_ext[1, row]),
        coeffs,
        inject,
        matrices,
        scratch,
        mid_emit,
        emit,
        lambda row: (now[0, row], now[1, row]),
    )
    slope_out[...] = scratch[0][pl.ds(REACH, rows)]


def side_kernel(before, mid, slope_z, now, matrices, flux, slopes, curves, p1):
    rows, width = before.shape[1], before.shape[2]
    clear_pads(p1, width)
    p1[:, YPAD : YPAD + width, :] = mid[0]

    def fluxes(row):
        _, parts = flux_row(row, width, p1, slope_z[row], before[0, row])
        for a in range(3):
            flux[a, row] = parts[a]

    each_row(rows, width, fluxes)
    for f in range(2):
        depth_rows(
            lambda b, n: now[f, pl.ds(b, n)], slopes.at[f], curves.at[f], 0, rows, width, matrices
        )


def first_image_kernel(source, mid, flux, offsets, images):
    rows, width = flux.shape[1], flux.shape[2]

    def image_row(row):
        def emit(b, term):
            images[b, row] = term

        image_terms(
            source, 0, row, mid[0, row + REACH], [flux[a, row] for a in range(3)], offsets, emit
        )

    each_row(rows, width, image_row)


def late_kernel(
    now,
    mid,
    coeffs,
    on_chip,
    off_chip,
    inject,
    slopes,
    curves,
    matrices,
    source,
    offsets,
    partial_images,
    images,
    out,
    p,
    q,
    *scratch,
):
    rows, width = now.shape[1], now.shape[2]
    near, far = side_starts(rows, HALO)
    clear_pads(p, width)
    place(
        p,
        q,
        now,
        (
            (near, lambda a, n: on_chip[a // HALO]),
            (far, lambda a, n: off_chip[a // HALO]),
        ),
        width,
    )

    def emit(row, next_p, next_q):
        out[0, row] = next_p
        out[1, row] = next_q

    two_steps(
        2,
        rows,
        width,
        (p, q),
        (slopes[0], slopes[1], curves[0], curves[1]),
        lambda row: (mid[0, row], mid[1, row]),
        coeffs,
        inject,
        matrices,
        scratch,
        lambda row, next_p, next_q: None,
        emit,
        lambda row: (now[0, row], now[1, row]),
    )
    slope_z, p1 = scratch[0], scratch[4]

    def image_row(row):
        field, flux = flux_row(row, width, p1, slope_z[row + REACH], now[0, row])

        def finish(b, term):
            images[b, row] = (partial_images[b, row] + term).astype(images.dtype)

        image_terms(source, 1, row, field, flux, offsets, finish)

    each_row(rows, width, image_row)


def local(
    wave_now,
    wave_prev,
    speed_term,
    thomsen_epsilon,
    thomsen_delta,
    tilt_angle,
    source_store,
    receiver_row,
    receiver_column,
    receiver_traces,
    angle_table,
):
    _, rows, width, depth = wave_now.shape
    count = lax.axis_size("gx")
    odd = lax.rem(lax.axis_index("gx"), 2)
    on_chip_pairs = [(i, i ^ 1) for i in range(count)]
    off_chip_pairs = [(i, i + 1) for i in range(1, count - 1, 2)]
    off_chip_pairs = off_chip_pairs + [(b, a) for a, b in off_chip_pairs]

    f32 = jnp.float32
    ext, wide = rows + 2 * REACH, rows + 2 * HALO
    vmem = pl.BlockSpec(memory_space=pltpu.VMEM)
    smem = pl.BlockSpec(memory_space=pltpu.SMEM)
    in_hbm = pl.BlockSpec(memory_space=pltpu.HBM)
    plane = (width, depth)
    padded = (width + 2 * YPAD, depth)
    plane_bytes = 4 * width * depth
    line_flops = width * depth

    def planes(*lead):
        return jax.ShapeDtypeStruct(lead + plane, f32)

    def call(kernel, outs, ins, in_specs, scratch, grant, cost):
        return pl.pallas_call(
            kernel,
            out_shape=outs,
            in_specs=in_specs,
            out_specs=jax.tree.map(lambda _: vmem, outs),
            scratch_shapes=scratch,
            compiler_params=pltpu.CompilerParams(
                vmem_limit_bytes=4 * 1024 * 1024 + grant * plane_bytes
            ),
            cost_estimate=pl.CostEstimate(
                flops=cost * line_flops, bytes_accessed=cost * line_flops // 4, transcendentals=0
            ),
        )(*ins)

    step_scratch = [
        pltpu.VMEM((wide,) + plane, f32),
        pltpu.VMEM((wide,) + plane, f32),
        pltpu.VMEM((wide,) + plane, f32),
        pltpu.VMEM((wide,) + plane, f32),
        pltpu.VMEM((ext,) + padded, f32),
        pltpu.VMEM((ext,) + plane, f32),
    ]
    wave_scratch = [pltpu.VMEM((wide,) + padded, f32), pltpu.VMEM((wide,) + plane, f32)]
    medium = (speed_term, thomsen_epsilon, thomsen_delta, tilt_angle)
    matrices = jnp.asarray(depth_matrices(depth))

    packed = planes(2 * HALO + 6 * REACH)
    far_pack, near_pack = call(
        pack_kernel,
        (packed, packed),
        [
            pltpu.with_memory_space_constraint(x, pltpu.HBM)
            for x in (wave_now, wave_prev, *medium)
        ],
        [in_hbm] * 6,
        [pltpu.SemaphoreType.DMA((16,))],
        80,
        200,
    )
    off_chip = lax.ppermute(far_pack, "gx", off_chip_pairs)
    on_chip = lax.ppermute(near_pack, "gx", on_chip_pairs)
    arrived = lax.all_to_all(source_store, "gx", split_axis=2, concat_axis=3, tiled=True)
    own_coeffs, inject, slopes, curves, offsets = call(
        prep_kernel,
        (
            planes(5, rows),
            planes(STEPS, ext),
            planes(2, rows),
            planes(2, rows),
            jax.ShapeDtypeStruct((16, depth), f32),
        ),
        (wave_now, *medium, receiver_row, receiver_column, receiver_traces, angle_table, matrices),
        [vmem] * 8 + [smem, vmem],
        [],
        20 * wide,
        60 * rows,
    )
    now, mid, coeffs, slope_z = call(
        early_kernel,
        (planes(2, rows), planes(2, ext), planes(5, ext), planes(rows)),
        (wave_now, wave_prev, on_chip, off_chip, own_coeffs, inject, slopes, curves, matrices),
        [vmem] * 9,
        wave_scratch + [pltpu.VMEM((2, ext) + plane, f32)] + step_scratch,
        30 * wide,
        400 * rows,
    )

    def side(tail):
        if rows == HALO:
            return now
        return lax.dynamic_slice_in_dim(now, jnp.where(tail, rows - HALO, 0), HALO, axis=1)

    off_chip = lax.ppermute(side(odd == 1), "gx", off_chip_pairs)
    on_chip = lax.ppermute(side(odd == 0), "gx", on_chip_pairs)
    flux, slopes, curves = call(
        side_kernel,
        (planes(3, rows), planes(2, rows), planes(2, rows)),
        (wave_now, mid, slope_z, now, matrices),
        [vmem] * 5,
        [pltpu.VMEM((ext,) + padded, f32)],
        12 * wide,
        60 * rows,
    )
    partial_images = call(
        first_image_kernel,
        planes(NBIN, rows),
        (arrived, mid, flux, offsets),
        [vmem] * 4,
        [],
        16 * wide,
        60 * rows,
    )
    images, final = call(
        late_kernel,
        (jax.ShapeDtypeStruct((NBIN, rows) + plane, jnp.bfloat16), planes(2, rows)),
        (
            now,
            mid,
            coeffs,
            on_chip,
            off_chip,
            inject,
            slopes,
            curves,
            matrices,
            arrived,
            offsets,
            partial_images,
        ),
        [vmem] * 12,
        wave_scratch + step_scratch,
        34 * wide,
        500 * rows,
    )
    return images, final


def solution(mesh):
    placed = (
        P("shot", "gx", None, None),
        P("shot", "gx", None, None),
        P("gx", None, None),
        P("gx", None, None),
        P("gx", None, None),
        P("gx", None, None),
        P("shot", None, None, "gx", None),
        P("shot"),
        P("shot"),
        P("shot", None),
        P(),
    )
    return jax.shard_map(
        local,
        mesh=mesh,
        in_specs=placed,
        out_specs=(P("shot", "gx", None, None), P("shot", "gx", None, None)),
        check_vma=False,
    )
```

time: 36.2 us -> 33.7 us (0.931)
  waiting for transfers between devices: 10.5 us -> 8.71 us
  local copies, waits for them, and re-layouts: 2.74 us -> 2.09 us
  Pallas kernels: 6.35 us -> 5.92 us
    ppermute x1, waiting for transfers between devices: 8.1 us -> 6.85 us  [local(): off_chip = lax.ppermute(far_pack, 'gx', off_chip_pairs)]
    unnamed x21 -> x23, local copies, waits for them, and re-layouts: 2.57 us -> 1.92 us
    ppermute x2, waiting for transfers between devices: 2.37 us -> 1.85 us  [the longest x1 1.85 us: local(): off_chip = lax.ppermute(side(odd == 1), 'gx', off_chip_pairs)]
    pallas_call x3 -> x6, Pallas kernels: 6.35 us -> 5.92 us  [call(): pl.pallas_call(kernel, out_shape=outs, in_specs=in_specs, out_specs=jax.t...]
  transfers between devices with their start and end apart: 5 -> 5, of which waited for: 2 -> 2; matrix products, arithmetic and copies ran while one was open for 0% -> 1% of each run, Pallas kernels for 9% -> 12%
where the time goes in v3:
time: 33.7 us; the launch traced here: 33.3 us
  starting transfers between devices  15.8 us (47%)
  waiting for transfers between devices  8.71 us (26%)
  Pallas kernels  5.92 us (18%)
  local copies, waits for them, and re-layouts  2.09 us (6%)
  between operations  0.87 us (3%)
    all_to_all x1, starting transfers between devices, local(): lax.all_to_all(source_store, 'gx', split_axis=2, concat_axis=3, tiled=True)  7.44 us
    ppermute x1, waiting for transfers between devices, local(): off_chip = lax.ppermute(far_pack, 'gx', off_chip_pairs)  6.85 us
    pallas_call x6, Pallas kernels, call(): pl.pallas_call(kernel, out_shape=outs, in_specs=in_specs, out_specs=jax.t...  5.92 us
    ppermute x1, starting transfers between devices, local(): off_chip = lax.ppermute(side(odd == 1), 'gx', off_chip_pairs)  4.4 us
    ppermute x1, starting transfers between devices, local(): off_chip = lax.ppermute(far_pack, 'gx', off_chip_pairs)  3.67 us
    unnamed x23, local copies, waits for them, and re-layouts  1.92 us
    ppermute x1, waiting for transfers between devices, local(): off_chip = lax.ppermute(side(odd == 1), 'gx', off_chip_pairs)  1.85 us
  transfers between devices with their start and end apart: 5, of which 2 were waited for; matrix products, arithmetic and copies ran while one was open for 1% of the time, Pallas kernels for 12%

profile of v3, /device:TPU:1, one launch (start us, length us, event | category | flops | bytes accessed | tf_op | source)
XLA Modules:
  0.0 33.3 jit_solution(1308780310451568124)
XLA Ops:
  0.6 1.9 %copy.16 = bf16[2,4,128,1,128]{4,1,0,3,2:T(4,128)(2,1)} copy(bf16[2,4,128,1,128]{4,2,3,1,0:T(8,128)(2,1)} %param.18) | data formatting | bytes 524288 | tf_op args[6]
  2.5 0.0 copy-start.6
  2.5 7.4 %all-to-all-start = ((bf16[2,4,128,1,128]{4,1,0,3,2:T(4,128)(2,1)}), bf16[2,4,128,1,128]{4,1,0,3,2:T(4,128)(2,1)S(1)}, u32[]{:S(2)}, u32[]{:S(2)}) async-start(bf16[2,4,128,1,128]{4,1,0,3,2:T(4,128)(2,1)} %copy.16), calls=%async_computation | async-start | bytes 524288 | tf_op jit(solution)/shard_map/all_to_all | solution.py:592
  9.9 0.0 copy-start
  9.9 0.0 copy-start.1
  10.0 0.0 copy-start.3
  10.0 0.0 copy-start.4
  10.0 0.0 copy-start.5
  10.0 1.3 %shard_map.131 = (f32[40,16,128]{2,1,0:T(8,128)S(1)}, f32[40,16,128]{2,1,0:T(8,128)S(1)}) custom-call(f32[2,8,16,128]{3,2,1,0:T(8,128)} %before.1, f32[2,8,16,128]{3,2,1,0:T(8,128)} %prev.3, f32[8,16,128]{2,1,0:T(8,128)} %speed.3, f32[8,16,128]{2,1,0:T(8,128)} %epsilon.3, f32[8,16,128]{2,1,0:T(8,128)} %delta.3, f32[8,16,128]{2,1,0:T(8,128)} %tilt.3), custom_call_target="tpu_custom_call" | custom-call | flops 409600 | bytes 102400 | tf_op jit(solution)/shard_map/pallas_call | solution.py:551
  11.3 0.0 copy-start.7
  11.3 0.0 copy-start.8
  11.3 0.0 copy-start.9
  11.3 0.0 copy-start.10
  11.3 0.2 collective-permute-start
  11.5 0.0 copy-start.2
  11.5 3.7 %collective-permute-start.1 = (f32[40,16,128]{2,1,0:T(8,128)S(1)}, f32[40,16,128]{2,1,0:T(8,128)S(1)}, u32[]{:S(2)}, u32[]{:S(2)}) collective-permute-start(f32[40,16,128]{2,1,0:T(8,128)S(1)} %get-tuple-element.17), channel_id=1, source_target_pairs={{1,2},{3,4},{5,6},{7,8},{9,10},{11,12},{13,14},{2,1},{4,3},{6,5},{... | collective-permute-start | bytes 983048 | tf_op jit(solution)/shard_map/ppermute | solution.py:590
  15.2 0.0 copy-done.6
  15.2 0.0 copy-done
  15.2 0.0 copy-done.1
  15.2 0.0 copy-done.3
  15.2 0.0 copy-done.4
  15.2 0.0 copy-done.5
  15.2 0.0 copy-done.7
  15.2 0.0 copy-done.8
  15.2 0.0 copy-done.9
  15.2 0.0 copy-done.10
  15.3 1.0 %shard_map.132 = (f32[5,8,16,128]{3,2,1,0:T(8,128)S(1)}, f32[4,16,16,128]{3,2,1,0:T(8,128)S(1)}, f32[2,8,16,128]{3,2,1,0:T(8,128)S(1)}, f32[2,8,16,128]{3,2,1,0:T(8,128)S(1)}, f32[16,128]{1,0:T(8,128)S(1)}) custom-call(f32[2,8,16,128]{3,2,1,0:T(8,128)S(1)} %copy-done.1, f32[8,16,128]{2,1,0:T(8,128)S(1)} %copy-done.3, f32[8,16,128]{2,1,0:T(8,128)S(1)} %copy-done.4, ...), custom_call_target="tpu_custom_call" | custom-call | flops 983040 | bytes 245760 | tf_op jit(solution)/shard_map/pallas_call | solution.py:551
  16.3 0.0 collective-permute-done.on_chip
  16.3 6.9 %collective-permute-done.1.off_chip = f32[40,16,128]{2,1,0:T(8,128)S(1)} collective-permute-done((f32[40,16,128]{2,1,0:T(8,128)S(1)}, f32[40,16,128]{2,1,0:T(8,128)S(1)}, u32[]{:S(2)}, u32[]{:S(2)}) %collective-permute-start.1) | collective-permute-done | bytes 327712 | tf_op jit(solution)/shard_map/ppermute | solution.py:590
  23.2 0.0 copy-done.2
  23.2 1.1 %shard_map.133 = (f32[2,8,16,128]{3,2,1,0:T(8,128)S(1)}, f32[2,16,16,128]{3,2,1,0:T(8,128)S(1)}, f32[5,16,16,128]{3,2,1,0:T(8,128)S(1)}, f32[8,16,128]{2,1,0:T(8,128)S(1)}) custom-call(f32[2,8,16,128]{3,2,1,0:T(8,128)S(1)} %copy-done.1, f32[2,8,16,128]{3,2,1,0:T(8,128)S(1)} %copy-done.2, f32[40,16,128]{2,1,0:T(8,128)S(1)} %collective-permute-done.on_chip, ...), custom_call_target="tpu_custom_call" | custom-call | flops 6553600 | bytes 1638400 | tf_op jit(solution)/shard_map/pallas_call | solution.py:551
  24.3 4.4 %collective-permute-start.3 = (f32[2,8,16,128]{3,2,1,0:T(8,128)S(1)}, f32[2,8,16,128]{3,2,1,0:T(8,128)S(1)}, u32[]{:S(2)}, u32[]{:S(2)}) collective-permute-start(f32[2,8,16,128]{3,2,1,0:T(8,128)S(1)} %get-tuple-element.22.now), channel_id=1, source_target_pairs={{1,2},{3,4},{5,6},{7,8},{9,10},{11,12},{13,14},{2,1},{4,3},{6,5},{... | collective-permute-start | bytes 393224 | tf_op jit(solution)/shard_map/ppermute | solution.py:623
  28.7 0.1 collective-permute-start.2
  28.8 0.3 shard_map.134
  29.1 0.0 all-to-all-done
  29.2 0.2 copy.22
  29.3 0.2 shard_map.135.partial_images
  29.5 1.8 %collective-permute-done.3.off_chip = f32[2,8,16,128]{3,2,1,0:T(8,128)S(1)} collective-permute-done((f32[2,8,16,128]{3,2,1,0:T(8,128)S(1)}, f32[2,8,16,128]{3,2,1,0:T(8,128)S(1)}, u32[]{:S(2)}, u32[]{:S(2)}) %collective-permute-start.3) | collective-permute-done | bytes 131104 | tf_op jit(solution)/shard_map/ppermute | solution.py:623
  31.4 0.0 collective-permute-done.2.on_chip
  31.4 2.0 %shard_map.136 = (bf16[8,8,16,128]{3,2,1,0:T(8,128)(2,1)}, f32[2,8,16,128]{3,2,1,0:T(8,128)}) custom-call(f32[2,8,16,128]{3,2,1,0:T(8,128)S(1)} %get-tuple-element.22.now, f32[2,16,16,128]{3,2,1,0:T(8,128)S(1)} %get-tuple-element.23.mid, f32[5,16,16,128]{3,2,1,0:T(8,128)S(1)} %get-tuple-element.24.coeffs, ...), custom_call_target="tpu_custom_call" | custom-call | flops 8192000 | bytes 2048000 | tf_op jit(solution)/shard_map/pallas_call | solution.py:551
Async XLA Ops:
  2.5 12.7 %copy-start.6 = (f32[8,16,128]{2,1,0:T(8,128)S(1)}, f32[8,16,128]{2,1,0:T(8,128)}, u32[]{:S(2)}) copy-start(f32[8,16,128]{2,1,0:T(8,128)} %tilt.3) | copy-start | bytes 196612
  2.5 26.7 %all-to-all-start = ((bf16[2,4,128,1,128]{4,1,0,3,2:T(4,128)(2,1)}), bf16[2,4,128,1,128]{4,1,0,3,2:T(4,128)(2,1)S(1)}, u32[]{:S(2)}, u32[]{:S(2)}) async-start(bf16[2,4,128,1,128]{4,1,0,3,2:T(4,128)(2,1)} %copy.16), calls=%async_computation | async-start | bytes 524288 | tf_op jit(solution)/shard_map/all_to_all | solution.py:592
  9.9 5.2 %copy-start = (bf16[3,128,256]{2,1,0:T(8,128)(2,1)S(1)}, bf16[3,128,256]{2,1,0:T(8,128)(2,1)}, u32[]{:S(2)}) copy-start(bf16[3,128,256]{2,1,0:T(8,128)(2,1)} %constant.2.clone.matrices) | copy-start | bytes 589828
  9.9 5.2 %copy-start.1 = (f32[2,8,16,128]{3,2,1,0:T(8,128)S(1)}, f32[2,8,16,128]{3,2,1,0:T(8,128)}, u32[]{:S(2)}) copy-start(f32[2,8,16,128]{3,2,1,0:T(8,128)} %before.1) | copy-start | bytes 393220
  10.0 5.2 %copy-start.3 = (f32[8,16,128]{2,1,0:T(8,128)S(1)}, f32[8,16,128]{2,1,0:T(8,128)}, u32[]{:S(2)}) copy-start(f32[8,16,128]{2,1,0:T(8,128)} %speed.3) | copy-start | bytes 196612
  10.0 5.2 %copy-start.4 = (f32[8,16,128]{2,1,0:T(8,128)S(1)}, f32[8,16,128]{2,1,0:T(8,128)}, u32[]{:S(2)}) copy-start(f32[8,16,128]{2,1,0:T(8,128)} %epsilon.3) | copy-start | bytes 196612
  10.0 5.2 %copy-start.5 = (f32[8,16,128]{2,1,0:T(8,128)S(1)}, f32[8,16,128]{2,1,0:T(8,128)}, u32[]{:S(2)}) copy-start(f32[8,16,128]{2,1,0:T(8,128)} %delta.3) | copy-start | bytes 196612
  11.3 4.0 %copy-start.7 = (f32[4,128]{1,0:T(4,128)S(1)}, f32[4,128]{1,0:T(4,128)}, u32[]{:S(2)}) copy-start(f32[4,128]{1,0:T(4,128)} %traces.1) | copy-start | bytes 6148
  11.3 4.0 %copy-start.8 = (s32[128]{0:T(128)S(1)}, s32[128]{0:T(128)}, u32[]{:S(2)}) copy-start(s32[128]{0:T(128)} %receiver_row.1) | copy-start | bytes 1540
  11.3 4.0 %copy-start.9 = (s32[128]{0:T(128)S(1)}, s32[128]{0:T(128)}, u32[]{:S(2)}) copy-start(s32[128]{0:T(128)} %receiver_column.1) | copy-start | bytes 1540
  11.3 4.0 %copy-start.10 = (s32[32]{0:T(128)S(1)}, s32[32]{0:T(128)}, u32[]{:S(2)}) copy-start(s32[32]{0:T(128)} %table.1) | copy-start | bytes 388
  11.3 5.0 %collective-permute-start = (f32[40,16,128]{2,1,0:T(8,128)S(1)}, f32[40,16,128]{2,1,0:T(8,128)S(1)}, u32[]{:S(2)}, u32[]{:S(2)}) collective-permute-start(f32[40,16,128]{2,1,0:T(8,128)S(1)} %get-tuple-element.16), channel_id=1, source_target_pairs={{0,1},{1,0},{2,3},{3,2},{4,5},{5,4},{6,7},{7,6},{8,9},{9,8},{10,11... | collective-permute-start | bytes 983048 | tf_op jit(solution)/shard_map/ppermute | solution.py:591
  11.5 11.7 %copy-start.2 = (f32[2,8,16,128]{3,2,1,0:T(8,128)S(1)}, f32[2,8,16,128]{3,2,1,0:T(8,128)}, u32[]{:S(2)}) copy-start(f32[2,8,16,128]{3,2,1,0:T(8,128)} %prev.3) | copy-start | bytes 393220
  11.5 11.7 %collective-permute-start.1 = (f32[40,16,128]{2,1,0:T(8,128)S(1)}, f32[40,16,128]{2,1,0:T(8,128)S(1)}, u32[]{:S(2)}, u32[]{:S(2)}) collective-permute-start(f32[40,16,128]{2,1,0:T(8,128)S(1)} %get-tuple-element.17), channel_id=1, source_target_pairs={{1,2},{3,4},{5,6},{7,8},{9,10},{11,12},{13,14},{2,1},{4,3},{6,5},{... | collective-permute-start | bytes 983048 | tf_op jit(solution)/shard_map/ppermute | solution.py:590
  24.3 7.0 %collective-permute-start.3 = (f32[2,8,16,128]{3,2,1,0:T(8,128)S(1)}, f32[2,8,16,128]{3,2,1,0:T(8,128)S(1)}, u32[]{:S(2)}, u32[]{:S(2)}) collective-permute-start(f32[2,8,16,128]{3,2,1,0:T(8,128)S(1)} %get-tuple-element.22.now), channel_id=1, source_target_pairs={{1,2},{3,4},{5,6},{7,8},{9,10},{11,12},{13,14},{2,1},{4,3},{6,5},{... | collective-permute-start | bytes 393224 | tf_op jit(solution)/shard_map/ppermute | solution.py:623
  28.7 2.6 %collective-permute-start.2 = (f32[2,8,16,128]{3,2,1,0:T(8,128)S(1)}, f32[2,8,16,128]{3,2,1,0:T(8,128)S(1)}, u32[]{:S(2)}, u32[]{:S(2)}) collective-permute-start(f32[2,8,16,128]{3,2,1,0:T(8,128)S(1)} %get-tuple-element.22.now), channel_id=1, source_target_pairs={{0,1},{1,0},{2,3},{3,2},{4,5},{5,4},{6,7},{7,6},{8,9},{9,8},{10,11... | collective-permute-start | bytes 393224 | tf_op jit(solution)/shard_map/ppermute | solution.py:624

commit v4 on v3

--- a/solution.py
+++ b/solution.py
@@ -218,6 +218,11 @@
     return on_chip, off_chip
 
 
+def has_far_side():
+    at = lax.axis_index("gx")
+    return (at > 0) & (at < lax.axis_size("gx") - 1)
+
+
 def two_steps(
     t, rows, width, waves, own, first_prev, coeffs, inject, matrices, scratch, mid_emit, emit, second_prev
 ):
@@ -369,6 +374,7 @@
 ):
     rows, width = now.shape[1], now.shape[2]
     near, far = side_starts(rows, HALO)
+    inside = has_far_side()
     clear_pads(p, width)
     place(
         p,
@@ -376,7 +382,7 @@
         now,
         (
             (near, lambda a, n: on_chip[pl.ds(a, n)]),
-            (far, lambda a, n: off_chip[pl.ds(a, n)]),
+            (far, lambda a, n: jnp.where(inside, off_chip[pl.ds(a, n)], 0.0)),
         ),
         width,
     )
@@ -386,11 +392,16 @@
         coeffs[c, pl.ds(REACH, rows)] = own_coeffs[c]
     for f in range(2):
         prev_ext[f, pl.ds(REACH, rows)] = prev[f]
-    for at, part in ((near, on_chip), (far, off_chip)):
+    for at, part, real in ((near, on_chip, True), (far, off_chip, inside)):
+
+        def only_real(value, real=real):
+            return value if real is True else jnp.where(real, value, 0.0)
+
         for f in range(2):
-            prev_ext[f, pl.ds(at, REACH)] = part[pl.ds(base + f * REACH, REACH)]
+            prev_ext[f, pl.ds(at, REACH)] = only_real(part[pl.ds(base + f * REACH, REACH)])
         for r in range(REACH):
-            derive(coeffs, at + r, *[part[base + (2 + m) * REACH + r] for m in range(4)])
+            fields = [part[base + (2 + m) * REACH + r] for m in range(4)]
+            derive(coeffs, at + r, only_real(fields[0]), *fields[1:])
 
     def mid_emit(row, next_p, next_q):
         mid[0, row] = next_p
@@ -470,6 +481,7 @@
 ):
     rows, width = now.shape[1], now.shape[2]
     near, far = side_starts(rows, HALO)
+    inside = has_far_side()
     clear_pads(p, width)
     place(
         p,
@@ -477,7 +489,7 @@
         now,
         (
             (near, lambda a, n: on_chip[a // HALO]),
-            (far, lambda a, n: off_chip[a // HALO]),
+            (far, lambda a, n: jnp.where(inside, off_chip[a // HALO], 0.0)),
         ),
         width,
     )
@@ -531,8 +543,16 @@
     count = lax.axis_size("gx")
     odd = lax.rem(lax.axis_index("gx"), 2)
     on_chip_pairs = [(i, i ^ 1) for i in range(count)]
-    off_chip_pairs = [(i, i + 1) for i in range(1, count - 1, 2)]
-    off_chip_pairs = off_chip_pairs + [(b, a) for a, b in off_chip_pairs]
+    both_axes = ("shot", "gx")
+    shots = lax.axis_size("shot")
+    off_chip_pairs = []
+    for shot in range(shots):
+        at = shot * count
+        for i in range(1, count - 1, 2):
+            off_chip_pairs += [(at + i, at + i + 1), (at + i + 1, at + i)]
+        other = ((shot + 1) % shots) * count
+        if shots > 1:
+            off_chip_pairs += [(at, other), (at + count - 1, other + count - 1)]
 
     f32 = jnp.float32
     ext, wide = rows + 2 * REACH, rows + 2 * HALO
@@ -587,7 +607,7 @@
         80,
         200,
     )
-    off_chip = lax.ppermute(far_pack, "gx", off_chip_pairs)
+    off_chip = lax.ppermute(far_pack, both_axes, off_chip_pairs)
     on_chip = lax.ppermute(near_pack, "gx", on_chip_pairs)
     arrived = lax.all_to_all(source_store, "gx", split_axis=2, concat_axis=3, tiled=True)
     own_coeffs, inject, slopes, curves, offsets = call(
@@ -620,7 +640,7 @@
             return now
         return lax.dynamic_slice_in_dim(now, jnp.where(tail, rows - HALO, 0), HALO, axis=1)
 
-    off_chip = lax.ppermute(side(odd == 1), "gx", off_chip_pairs)
+    off_chip = lax.ppermute(side(odd == 1), both_axes, off_chip_pairs)
     on_chip = lax.ppermute(side(odd == 0), "gx", on_chip_pairs)
     flux, slopes, curves = call(
         side_kernel,

time: 33.7 us -> 30.8 us (0.914)
  starting transfers between devices: 15.8 us -> 11.8 us
  waiting for transfers between devices: 8.71 us -> 9.68 us
    ppermute x2, starting transfers between devices: 8.07 us -> 4.19 us  [the longest x1 2.55 us: local(): off_chip = lax.ppermute(side(odd == 1), both_axes, off_chip_pairs)]
    ppermute x2, waiting for transfers between devices: 8.7 us -> 9.67 us  [the longest x1 7.73 us: local(): off_chip = lax.ppermute(far_pack, both_axes, off_chip_pairs)]
  transfers between devices with their start and end apart: 5 -> 5, of which waited for: 2 -> 2; matrix products, arithmetic and copies ran while one was open for 1% -> 1% of each run, Pallas kernels for 12% -> 13%
where the time goes in v4:
time: 30.8 us; the launch traced here: 30.3 us
  starting transfers between devices  11.8 us (38%)
  waiting for transfers between devices  9.68 us (31%)
  Pallas kernels  5.93 us (19%)
  local copies, waits for them, and re-layouts  2.09 us (7%)
  between operations  0.82 us (3%)
    ppermute x1, waiting for transfers between devices, local(): off_chip = lax.ppermute(far_pack, both_axes, off_chip_pairs)  7.73 us
    all_to_all x1, starting transfers between devices, local(): lax.all_to_all(source_store, 'gx', split_axis=2, concat_axis=3, tiled=True)  7.44 us
    pallas_call x6, Pallas kernels, call(): pl.pallas_call(kernel, out_shape=outs, in_specs=in_specs, out_specs=jax.t...  5.93 us
    ppermute x1, starting transfers between devices, local(): off_chip = lax.ppermute(side(odd == 1), both_axes, off_chip_pairs)  2.55 us
    ppermute x1, waiting for transfers between devices, local(): off_chip = lax.ppermute(side(odd == 1), both_axes, off_chip_pairs)  1.94 us
    unnamed x23, local copies, waits for them, and re-layouts  1.92 us
    ppermute x1, starting transfers between devices, local(): off_chip = lax.ppermute(far_pack, both_axes, off_chip_pairs)  1.64 us
  transfers between devices with their start and end apart: 5, of which 2 were waited for; matrix products, arithmetic and copies ran while one was open for 1% of the time, Pallas kernels for 13%

profile of v4, /device:TPU:1, one launch (start us, length us, event | category | flops | bytes accessed | tf_op | source)
XLA Modules:
  0.0 30.3 jit_solution(10110155586389397638)
XLA Ops:
  0.6 1.9 %copy.16 = bf16[2,4,128,1,128]{4,1,0,3,2:T(4,128)(2,1)} copy(bf16[2,4,128,1,128]{4,2,3,1,0:T(8,128)(2,1)} %param.18) | data formatting | bytes 524288 | tf_op args[6]
  2.5 0.0 copy-start.6
  2.5 7.4 %all-to-all-start = ((bf16[2,4,128,1,128]{4,1,0,3,2:T(4,128)(2,1)}), bf16[2,4,128,1,128]{4,1,0,3,2:T(4,128)(2,1)S(1)}, u32[]{:S(2)}, u32[]{:S(2)}) async-start(bf16[2,4,128,1,128]{4,1,0,3,2:T(4,128)(2,1)} %copy.16), calls=%async_computation | async-start | bytes 524288 | tf_op jit(solution)/shard_map/all_to_all | solution.py:612
  9.9 0.0 copy-start
  9.9 0.0 copy-start.1
  10.0 0.0 copy-start.3
  10.0 0.0 copy-start.4
  10.0 0.0 copy-start.5
  10.0 1.3 %shard_map.131 = (f32[40,16,128]{2,1,0:T(8,128)S(1)}, f32[40,16,128]{2,1,0:T(8,128)S(1)}) custom-call(f32[2,8,16,128]{3,2,1,0:T(8,128)} %before.1, f32[2,8,16,128]{3,2,1,0:T(8,128)} %prev.3, f32[8,16,128]{2,1,0:T(8,128)} %speed.3, f32[8,16,128]{2,1,0:T(8,128)} %epsilon.3, f32[8,16,128]{2,1,0:T(8,128)} %delta.3, f32[8,16,128]{2,1,0:T(8,128)} %tilt.3), custom_call_target="tpu_custom_call" | custom-call | flops 409600 | bytes 102400 | tf_op jit(solution)/shard_map/pallas_call | solution.py:571
  11.3 0.0 copy-start.7
  11.3 0.0 copy-start.8
  11.3 0.0 copy-start.9
  11.3 0.0 copy-start.10
  11.3 0.2 collective-permute-start
  11.5 0.0 copy-start.2
  11.5 1.6 %collective-permute-start.1 = (f32[40,16,128]{2,1,0:T(8,128)S(1)}, f32[40,16,128]{2,1,0:T(8,128)S(1)}, u32[]{:S(2)}, u32[]{:S(2)}) collective-permute-start(f32[40,16,128]{2,1,0:T(8,128)S(1)} %get-tuple-element.17), channel_id=1, source_target_pairs={{1,2},{2,1},{3,4},{4,3},{5,6},{6,5},{7,8},{8,7},{9,10},{10,9},{11,... | collective-permute-start | bytes 983048 | tf_op jit(solution)/shard_map/ppermute | solution.py:610
  13.1 0.0 copy-done.6
  13.1 0.0 copy-done
  13.1 0.0 copy-done.1
  13.1 0.0 copy-done.3
  13.1 0.0 copy-done.4
  13.1 0.0 copy-done.5
  13.2 0.0 copy-done.7
  13.2 0.0 copy-done.8
  13.2 0.0 copy-done.9
  13.2 0.0 copy-done.10
  13.2 1.0 %shard_map.132 = (f32[5,8,16,128]{3,2,1,0:T(8,128)S(1)}, f32[4,16,16,128]{3,2,1,0:T(8,128)S(1)}, f32[2,8,16,128]{3,2,1,0:T(8,128)S(1)}, f32[2,8,16,128]{3,2,1,0:T(8,128)S(1)}, f32[16,128]{1,0:T(8,128)S(1)}) custom-call(f32[2,8,16,128]{3,2,1,0:T(8,128)S(1)} %copy-done.1, f32[8,16,128]{2,1,0:T(8,128)S(1)} %copy-done.3, f32[8,16,128]{2,1,0:T(8,128)S(1)} %copy-done.4, ...), custom_call_target="tpu_custom_call" | custom-call | flops 983040 | bytes 245760 | tf_op jit(solution)/shard_map/pallas_call | solution.py:571
  14.2 0.0 collective-permute-done.on_chip
  14.3 7.7 %collective-permute-done.1.off_chip = f32[40,16,128]{2,1,0:T(8,128)S(1)} collective-permute-done((f32[40,16,128]{2,1,0:T(8,128)S(1)}, f32[40,16,128]{2,1,0:T(8,128)S(1)}, u32[]{:S(2)}, u32[]{:S(2)}) %collective-permute-start.1) | collective-permute-done | bytes 327712 | tf_op jit(solution)/shard_map/ppermute | solution.py:610
  22.0 0.0 copy-done.2
  22.0 1.1 %shard_map.133 = (f32[2,8,16,128]{3,2,1,0:T(8,128)S(1)}, f32[2,16,16,128]{3,2,1,0:T(8,128)S(1)}, f32[5,16,16,128]{3,2,1,0:T(8,128)S(1)}, f32[8,16,128]{2,1,0:T(8,128)S(1)}) custom-call(f32[2,8,16,128]{3,2,1,0:T(8,128)S(1)} %copy-done.1, f32[2,8,16,128]{3,2,1,0:T(8,128)S(1)} %copy-done.2, f32[40,16,128]{2,1,0:T(8,128)S(1)} %collective-permute-done.on_chip, ...), custom_call_target="tpu_custom_call" | custom-call | flops 6553600 | bytes 1638400 | tf_op jit(solution)/shard_map/pallas_call | solution.py:571
  23.1 2.5 %collective-permute-start.3 = (f32[2,8,16,128]{3,2,1,0:T(8,128)S(1)}, f32[2,8,16,128]{3,2,1,0:T(8,128)S(1)}, u32[]{:S(2)}, u32[]{:S(2)}) collective-permute-start(f32[2,8,16,128]{3,2,1,0:T(8,128)S(1)} %get-tuple-element.22.now), channel_id=1, source_target_pairs={{1,2},{2,1},{3,4},{4,3},{5,6},{6,5},{7,8},{8,7},{9,10},{10,9},{11,... | collective-permute-start | bytes 393224 | tf_op jit(solution)/shard_map/ppermute | solution.py:643
  25.7 0.0 collective-permute-start.2
  25.7 0.3 %shard_map.134 = (f32[3,8,16,128]{3,2,1,0:T(8,128)S(1)}, f32[2,8,16,128]{3,2,1,0:T(8,128)S(1)}, f32[2,8,16,128]{3,2,1,0:T(8,128)S(1)}) custom-call(f32[2,8,16,128]{3,2,1,0:T(8,128)S(1)} %copy-done.1, f32[2,16,16,128]{3,2,1,0:T(8,128)S(1)} %get-tuple-element.23.mid, f32[8,16,128]{2,1,0:T(8,128)S(1)} %get-tuple-element.25.slope_z, ...), custom_call_target="tpu_custom_call" | custom-call | flops 983040 | bytes 245760 | tf_op jit(solution)/shard_map/pallas_call | solution.py:571
  26.0 0.0 all-to-all-done
  26.0 0.2 copy.22
  26.2 0.2 shard_map.135.partial_images
  26.4 1.9 %collective-permute-done.3.off_chip = f32[2,8,16,128]{3,2,1,0:T(8,128)S(1)} collective-permute-done((f32[2,8,16,128]{3,2,1,0:T(8,128)S(1)}, f32[2,8,16,128]{3,2,1,0:T(8,128)S(1)}, u32[]{:S(2)}, u32[]{:S(2)}) %collective-permute-start.3) | collective-permute-done | bytes 131104 | tf_op jit(solution)/shard_map/ppermute | solution.py:643
  28.4 0.0 collective-permute-done.2.on_chip
  28.4 2.0 %shard_map.136 = (bf16[8,8,16,128]{3,2,1,0:T(8,128)(2,1)}, f32[2,8,16,128]{3,2,1,0:T(8,128)}) custom-call(f32[2,8,16,128]{3,2,1,0:T(8,128)S(1)} %get-tuple-element.22.now, f32[2,16,16,128]{3,2,1,0:T(8,128)S(1)} %get-tuple-element.23.mid, f32[5,16,16,128]{3,2,1,0:T(8,128)S(1)} %get-tuple-element.24.coeffs, ...), custom_call_target="tpu_custom_call" | custom-call | flops 8192000 | bytes 2048000 | tf_op jit(solution)/shard_map/pallas_call | solution.py:571
Async XLA Ops:
  2.5 10.6 %copy-start.6 = (f32[8,16,128]{2,1,0:T(8,128)S(1)}, f32[8,16,128]{2,1,0:T(8,128)}, u32[]{:S(2)}) copy-start(f32[8,16,128]{2,1,0:T(8,128)} %tilt.3) | copy-start | bytes 196612
  2.5 23.5 %all-to-all-start = ((bf16[2,4,128,1,128]{4,1,0,3,2:T(4,128)(2,1)}), bf16[2,4,128,1,128]{4,1,0,3,2:T(4,128)(2,1)S(1)}, u32[]{:S(2)}, u32[]{:S(2)}) async-start(bf16[2,4,128,1,128]{4,1,0,3,2:T(4,128)(2,1)} %copy.16), calls=%async_computation | async-start | bytes 524288 | tf_op jit(solution)/shard_map/all_to_all | solution.py:612
  9.9 3.2 %copy-start = (bf16[3,128,256]{2,1,0:T(8,128)(2,1)S(1)}, bf16[3,128,256]{2,1,0:T(8,128)(2,1)}, u32[]{:S(2)}) copy-start(bf16[3,128,256]{2,1,0:T(8,128)(2,1)} %constant.2.clone.matrices) | copy-start | bytes 589828
  9.9 3.2 %copy-start.1 = (f32[2,8,16,128]{3,2,1,0:T(8,128)S(1)}, f32[2,8,16,128]{3,2,1,0:T(8,128)}, u32[]{:S(2)}) copy-start(f32[2,8,16,128]{3,2,1,0:T(8,128)} %before.1) | copy-start | bytes 393220
  10.0 3.2 %copy-start.3 = (f32[8,16,128]{2,1,0:T(8,128)S(1)}, f32[8,16,128]{2,1,0:T(8,128)}, u32[]{:S(2)}) copy-start(f32[8,16,128]{2,1,0:T(8,128)} %speed.3) | copy-start | bytes 196612
  10.0 3.2 %copy-start.4 = (f32[8,16,128]{2,1,0:T(8,128)S(1)}, f32[8,16,128]{2,1,0:T(8,128)}, u32[]{:S(2)}) copy-start(f32[8,16,128]{2,1,0:T(8,128)} %epsilon.3) | copy-start | bytes 196612
  10.0 3.2 %copy-start.5 = (f32[8,16,128]{2,1,0:T(8,128)S(1)}, f32[8,16,128]{2,1,0:T(8,128)}, u32[]{:S(2)}) copy-start(f32[8,16,128]{2,1,0:T(8,128)} %delta.3) | copy-start | bytes 196612
  11.3 1.9 %copy-start.7 = (f32[4,128]{1,0:T(4,128)S(1)}, f32[4,128]{1,0:T(4,128)}, u32[]{:S(2)}) copy-start(f32[4,128]{1,0:T(4,128)} %traces.1) | copy-start | bytes 6148
  11.3 1.9 %copy-start.8 = (s32[128]{0:T(128)S(1)}, s32[128]{0:T(128)}, u32[]{:S(2)}) copy-start(s32[128]{0:T(128)} %receiver_row.1) | copy-start | bytes 1540
  11.3 1.9 %copy-start.9 = (s32[128]{0:T(128)S(1)}, s32[128]{0:T(128)}, u32[]{:S(2)}) copy-start(s32[128]{0:T(128)} %receiver_column.1) | copy-start | bytes 1540
  11.3 1.9 %copy-start.10 = (s32[32]{0:T(128)S(1)}, s32[32]{0:T(128)}, u32[]{:S(2)}) copy-start(s32[32]{0:T(128)} %table.1) | copy-start | bytes 388
  11.3 2.9 %collective-permute-start = (f32[40,16,128]{2,1,0:T(8,128)S(1)}, f32[40,16,128]{2,1,0:T(8,128)S(1)}, u32[]{:S(2)}, u32[]{:S(2)}) collective-permute-start(f32[40,16,128]{2,1,0:T(8,128)S(1)} %get-tuple-element.16), channel_id=1, source_target_pairs={{0,1},{1,0},{2,3},{3,2},{4,5},{5,4},{6,7},{7,6},{8,9},{9,8},{10,11... | collective-permute-start | bytes 983048 | tf_op jit(solution)/shard_map/ppermute | solution.py:611
  11.5 10.5 %copy-start.2 = (f32[2,8,16,128]{3,2,1,0:T(8,128)S(1)}, f32[2,8,16,128]{3,2,1,0:T(8,128)}, u32[]{:S(2)}) copy-start(f32[2,8,16,128]{3,2,1,0:T(8,128)} %prev.3) | copy-start | bytes 393220
  11.5 10.5 %collective-permute-start.1 = (f32[40,16,128]{2,1,0:T(8,128)S(1)}, f32[40,16,128]{2,1,0:T(8,128)S(1)}, u32[]{:S(2)}, u32[]{:S(2)}) collective-permute-start(f32[40,16,128]{2,1,0:T(8,128)S(1)} %get-tuple-element.17), channel_id=1, source_target_pairs={{1,2},{2,1},{3,4},{4,3},{5,6},{6,5},{7,8},{8,7},{9,10},{10,9},{11,... | collective-permute-start | bytes 983048 | tf_op jit(solution)/shard_map/ppermute | solution.py:610
  23.1 5.2 %collective-permute-start.3 = (f32[2,8,16,128]{3,2,1,0:T(8,128)S(1)}, f32[2,8,16,128]{3,2,1,0:T(8,128)S(1)}, u32[]{:S(2)}, u32[]{:S(2)}) collective-permute-start(f32[2,8,16,128]{3,2,1,0:T(8,128)S(1)} %get-tuple-element.22.now), channel_id=1, source_target_pairs={{1,2},{2,1},{3,4},{4,3},{5,6},{6,5},{7,8},{8,7},{9,10},{10,9},{11,... | collective-permute-start | bytes 393224 | tf_op jit(solution)/shard_map/ppermute | solution.py:643
  25.7 2.7 %collective-permute-start.2 = (f32[2,8,16,128]{3,2,1,0:T(8,128)S(1)}, f32[2,8,16,128]{3,2,1,0:T(8,128)S(1)}, u32[]{:S(2)}, u32[]{:S(2)}) collective-permute-start(f32[2,8,16,128]{3,2,1,0:T(8,128)S(1)} %get-tuple-element.22.now), channel_id=1, source_target_pairs={{0,1},{1,0},{2,3},{3,2},{4,5},{5,4},{6,7},{7,6},{8,9},{9,8},{10,11... | collective-permute-start | bytes 393224 | tf_op jit(solution)/shard_map/ppermute | solution.py:644

commit v5 on v4

--- a/solution.py
+++ b/solution.py
@@ -275,7 +275,7 @@
     )
 
 
-def pack_kernel(now, prev, speed, epsilon, delta, tilt, far, near, sems):
+def pack_kernel(now, prev, speed, epsilon, delta, tilt, source, far, near, sorted_source, sems):
     rows = now.shape[1]
     odd = lax.rem(lax.axis_index("gx"), 2)
     copies = []
@@ -299,6 +299,9 @@
                 field.at[pl.ds(edge_at, REACH)],
                 out.at[pl.ds(2 * HALO + (2 + m) * REACH, REACH)],
             )
+    for n in range(source.shape[0]):
+        for c in range(source.shape[1]):
+            copy(source.at[n, c], sorted_source.at[:, n, c])
     for one in copies:
         one.wait()
 
@@ -446,20 +449,6 @@
         )
 
 
-def first_image_kernel(source, mid, flux, offsets, images):
-    rows, width = flux.shape[1], flux.shape[2]
-
-    def image_row(row):
-        def emit(b, term):
-            images[b, row] = term
-
-        image_terms(
-            source, 0, row, mid[0, row + REACH], [flux[a, row] for a in range(3)], offsets, emit
-        )
-
-    each_row(rows, width, image_row)
-
-
 def late_kernel(
     now,
     mid,
@@ -470,11 +459,8 @@
     slopes,
     curves,
     matrices,
-    source,
-    offsets,
-    partial_images,
-    images,
     out,
+    imaged,
     p,
     q,
     *scratch,
@@ -515,13 +501,30 @@
     )
     slope_z, p1 = scratch[0], scratch[4]
 
+    def fluxes(row):
+        field, parts = flux_row(row, width, p1, slope_z[row + REACH], now[0, row])
+        for a, value in enumerate((field, *parts)):
+            imaged[a, row] = value
+
+    each_row(rows, width, fluxes)
+
+
+def image_kernel(source, mid, flux, imaged, offsets, images):
+    rows, width = flux.shape[1], flux.shape[2]
+
     def image_row(row):
-        field, flux = flux_row(row, width, p1, slope_z[row + REACH], now[0, row])
+        totals = [None] * NBIN
+
+        def keep(b, term):
+            totals[b] = term
 
         def finish(b, term):
-            images[b, row] = (partial_images[b, row] + term).astype(images.dtype)
-
-        image_terms(source, 1, row, field, flux, offsets, finish)
+            images[b, row] = (totals[b] + term).astype(images.dtype)
+
+        early = [flux[a, row] for a in range(3)]
+        image_terms(source, 0, row, mid[0, row + REACH], early, offsets, keep)
+        late = [imaged[a, row] for a in range(1, 4)]
+        image_terms(source, 1, row, imaged[0, row], late, offsets, finish)
 
     each_row(rows, width, image_row)
 
@@ -595,21 +598,27 @@
     matrices = jnp.asarray(depth_matrices(depth))
 
     packed = planes(2 * HALO + 6 * REACH)
-    far_pack, near_pack = call(
+    snaps, parts = source_store.shape[:2]
+    by_owner = source_store.reshape(snaps, parts, count, rows, depth)
+    far_pack, near_pack, sorted_source = call(
         pack_kernel,
-        (packed, packed),
+        (
+            packed,
+            packed,
+            jax.ShapeDtypeStruct((count, snaps, parts, rows, depth), source_store.dtype),
+        ),
         [
             pltpu.with_memory_space_constraint(x, pltpu.HBM)
-            for x in (wave_now, wave_prev, *medium)
+            for x in (wave_now, wave_prev, *medium, by_owner)
         ],
-        [in_hbm] * 6,
-        [pltpu.SemaphoreType.DMA((16,))],
-        80,
+        [in_hbm] * 7,
+        [pltpu.SemaphoreType.DMA((16 + snaps * parts,))],
+        120,
         200,
     )
     off_chip = lax.ppermute(far_pack, both_axes, off_chip_pairs)
     on_chip = lax.ppermute(near_pack, "gx", on_chip_pairs)
-    arrived = lax.all_to_all(source_store, "gx", split_axis=2, concat_axis=3, tiled=True)
+    arrived = lax.all_to_all(sorted_source, "gx", split_axis=0, concat_axis=0, tiled=True)
     own_coeffs, inject, slopes, curves, offsets = call(
         prep_kernel,
         (
@@ -651,36 +660,23 @@
         12 * wide,
         60 * rows,
     )
-    partial_images = call(
-        first_image_kernel,
-        planes(NBIN, rows),
-        (arrived, mid, flux, offsets),
-        [vmem] * 4,
+    final, imaged = call(
+        late_kernel,
+        (planes(2, rows), planes(4, rows)),
+        (now, mid, coeffs, on_chip, off_chip, inject, slopes, curves, matrices),
+        [vmem] * 9,
+        wave_scratch + step_scratch,
+        30 * wide,
+        400 * rows,
+    )
+    images = call(
+        image_kernel,
+        jax.ShapeDtypeStruct((NBIN, rows) + plane, jnp.bfloat16),
+        (jnp.transpose(arrived, (1, 2, 3, 0, 4)), mid, flux, imaged, offsets),
+        [vmem] * 5,
         [],
         16 * wide,
         60 * rows,
-    )
-    images, final = call(
-        late_kernel,
-        (jax.ShapeDtypeStruct((NBIN, rows) + plane, jnp.bfloat16), planes(2, rows)),
-        (
-            now,
-            mid,
-            coeffs,
-            on_chip,
-            off_chip,
-            inject,
-            slopes,
-            curves,
-            matrices,
-            arrived,
-            offsets,
-            partial_images,
-        ),
-        [vmem] * 12,
-        wave_scratch + step_scratch,
-        34 * wide,
-        500 * rows,
     )
     return images, final
 

time: 30.8 us -> 31.9 us (1.036)
  the two profiles are of different devices: /device:TPU:1 before, /device:TPU:21 now
where the time goes in v5:
time: 31.9 us; the launch traced here: 31.6 us
  waiting for transfers between devices  14 us (44%)
  starting transfers between devices  9.27 us (29%)
  Pallas kernels  7.34 us (23%)
  between operations  0.81 us (3%)
    ppermute x1, waiting for transfers between devices, local(): off_chip = lax.ppermute(far_pack, both_axes, off_chip_pairs)  9.5 us
    pallas_call x6, Pallas kernels, call(): pl.pallas_call(kernel, out_shape=outs, in_specs=in_specs, out_specs=jax.t...  7.34 us
    all_to_all x1, starting transfers between devices, local(): lax.all_to_all(sorted_source, 'gx', split_axis=0, concat_axis=0, tiled=True)  6.58 us
    ppermute x1, waiting for transfers between devices, local(): off_chip = lax.ppermute(side(odd == 1), both_axes, off_chip_pairs)  4.49 us
    ppermute x1, starting transfers between devices, local(): off_chip = lax.ppermute(far_pack, both_axes, off_chip_pairs)  1.18 us
    ppermute x1, starting transfers between devices, local(): off_chip = lax.ppermute(side(odd == 1), both_axes, off_chip_pairs)  1.04 us
  transfers between devices with their start and end apart: 5, of which 2 were waited for; matrix products, arithmetic and copies ran while one was open for 0% of the time, Pallas kernels for 13%

profile of v5, /device:TPU:21, one launch (start us, length us, event | category | flops | bytes accessed | tf_op | source)
XLA Modules:
  0.0 31.6 jit_solution(15666510502003124175)
XLA Ops:
  0.6 0.0 copy-start.6
  0.6 2.1 %shard_map.131 = (f32[40,16,128]{2,1,0:T(8,128)S(1)}, f32[40,16,128]{2,1,0:T(8,128)S(1)}, bf16[16,2,4,8,128]{4,3,2,1,0:T(8,128)(2,1)}) custom-call(f32[2,8,16,128]{3,2,1,0:T(8,128)} %before.1, f32[2,8,16,128]{3,2,1,0:T(8,128)} %prev.3, f32[8,16,128]{2,1,0:T(8,128)} %speed.3, f32[8,16,128]{2,1,0:T(8,128)} %epsilon.3, f32[8,16,128]{2,1,0:T(8,128)} %delta.3, ...), custom_call_target="tpu_custom_call" | custom-call | flops 409600 | bytes 102400 | tf_op jit(solution)/shard_map/pallas_call | solution.py:574
  2.7 0.0 copy-start
  2.7 0.0 copy-start.1
  2.7 0.0 copy-start.3
  2.7 0.0 copy-start.4
  2.8 0.0 copy-start.5
  2.8 6.6 %all-to-all-start = ((bf16[16,2,4,8,128]{4,3,2,1,0:T(8,128)(2,1)}), bf16[16,2,4,8,128]{4,3,2,1,0:T(8,128)(2,1)S(1)}, u32[]{:S(2)}, u32[]{:S(2)}) async-start(bf16[16,2,4,8,128]{4,3,2,1,0:T(8,128)(2,1)} %get-tuple-element.19), calls=%async_computation | async-start | bytes 524288 | tf_op jit(solution)/shard_map/all_to_all | solution.py:621
  9.4 0.0 copy-start.7
  9.4 0.0 copy-start.8
  9.4 0.0 copy-start.9
  9.4 0.0 copy-start.10
  9.4 0.5 %collective-permute-start = (f32[40,16,128]{2,1,0:T(8,128)S(1)}, f32[40,16,128]{2,1,0:T(8,128)S(1)}, u32[]{:S(2)}, u32[]{:S(2)}) collective-permute-start(f32[40,16,128]{2,1,0:T(8,128)S(1)} %get-tuple-element.20), channel_id=1, source_target_pairs={{0,1},{1,0},{2,3},{3,2},{4,5},{5,4},{6,7},{7,6},{8,9},{9,8},{10,11... | collective-permute-start | bytes 983048 | tf_op jit(solution)/shard_map/ppermute | solution.py:620
  9.9 0.0 copy-start.2
  9.9 1.2 %collective-permute-start.1 = (f32[40,16,128]{2,1,0:T(8,128)S(1)}, f32[40,16,128]{2,1,0:T(8,128)S(1)}, u32[]{:S(2)}, u32[]{:S(2)}) collective-permute-start(f32[40,16,128]{2,1,0:T(8,128)S(1)} %get-tuple-element.21), channel_id=1, source_target_pairs={{1,2},{2,1},{3,4},{4,3},{5,6},{6,5},{7,8},{8,7},{9,10},{10,9},{11,... | collective-permute-start | bytes 983048 | tf_op jit(solution)/shard_map/ppermute | solution.py:619
  11.0 0.0 copy-done.6
  11.0 0.0 copy-done
  11.0 0.0 copy-done.1
  11.1 0.0 copy-done.3
  11.1 0.0 copy-done.4
  11.1 0.0 copy-done.5
  11.1 0.0 copy-done.7
  11.1 0.0 copy-done.8
  11.1 0.0 copy-done.9
  11.1 0.0 copy-done.10
  11.1 1.0 %shard_map.132 = (f32[5,8,16,128]{3,2,1,0:T(8,128)S(1)}, f32[4,16,16,128]{3,2,1,0:T(8,128)S(1)}, f32[2,8,16,128]{3,2,1,0:T(8,128)S(1)}, f32[2,8,16,128]{3,2,1,0:T(8,128)S(1)}, f32[16,128]{1,0:T(8,128)S(1)}) custom-call(f32[2,8,16,128]{3,2,1,0:T(8,128)S(1)} %copy-done.1, f32[8,16,128]{2,1,0:T(8,128)S(1)} %copy-done.3, f32[8,16,128]{2,1,0:T(8,128)S(1)} %copy-done.4, ...), custom_call_target="tpu_custom_call" | custom-call | flops 983040 | bytes 245760 | tf_op jit(solution)/shard_map/pallas_call | solution.py:574
  12.2 0.0 collective-permute-done.on_chip
  12.2 9.5 %collective-permute-done.1.off_chip = f32[40,16,128]{2,1,0:T(8,128)S(1)} collective-permute-done((f32[40,16,128]{2,1,0:T(8,128)S(1)}, f32[40,16,128]{2,1,0:T(8,128)S(1)}, u32[]{:S(2)}, u32[]{:S(2)}) %collective-permute-start.1) | collective-permute-done | bytes 327712 | tf_op jit(solution)/shard_map/ppermute | solution.py:619
  21.7 0.0 copy-done.2
  21.7 1.1 %shard_map.133 = (f32[2,8,16,128]{3,2,1,0:T(8,128)S(1)}, f32[2,16,16,128]{3,2,1,0:T(8,128)S(1)}, f32[5,16,16,128]{3,2,1,0:T(8,128)S(1)}, f32[8,16,128]{2,1,0:T(8,128)S(1)}) custom-call(f32[2,8,16,128]{3,2,1,0:T(8,128)S(1)} %copy-done.1, f32[2,8,16,128]{3,2,1,0:T(8,128)S(1)} %copy-done.2, f32[40,16,128]{2,1,0:T(8,128)S(1)} %collective-permute-done.on_chip, ...), custom_call_target="tpu_custom_call" | custom-call | flops 6553600 | bytes 1638400 | tf_op jit(solution)/shard_map/pallas_call | solution.py:574
  22.8 1.0 %collective-permute-start.3 = (f32[2,8,16,128]{3,2,1,0:T(8,128)S(1)}, f32[2,8,16,128]{3,2,1,0:T(8,128)S(1)}, u32[]{:S(2)}, u32[]{:S(2)}) collective-permute-start(f32[2,8,16,128]{3,2,1,0:T(8,128)S(1)} %get-tuple-element.28.now), channel_id=1, source_target_pairs={{1,2},{2,1},{3,4},{4,3},{5,6},{6,5},{7,8},{8,7},{9,10},{10,9},{11,... | collective-permute-start | bytes 393224 | tf_op jit(solution)/shard_map/ppermute | solution.py:652
  23.9 0.0 collective-permute-start.2
  23.9 0.3 %shard_map.134 = (f32[3,8,16,128]{3,2,1,0:T(8,128)S(1)}, f32[2,8,16,128]{3,2,1,0:T(8,128)S(1)}, f32[2,8,16,128]{3,2,1,0:T(8,128)S(1)}) custom-call(f32[2,8,16,128]{3,2,1,0:T(8,128)S(1)} %copy-done.1, f32[2,16,16,128]{3,2,1,0:T(8,128)S(1)} %get-tuple-element.26.mid, f32[8,16,128]{2,1,0:T(8,128)S(1)} %get-tuple-element.27.slope_z, ...), custom_call_target="tpu_custom_call" | custom-call | flops 983040 | bytes 245760 | tf_op jit(solution)/shard_map/pallas_call | solution.py:574
  24.2 4.5 %collective-permute-done.3.off_chip = f32[2,8,16,128]{3,2,1,0:T(8,128)S(1)} collective-permute-done((f32[2,8,16,128]{3,2,1,0:T(8,128)S(1)}, f32[2,8,16,128]{3,2,1,0:T(8,128)S(1)}, u32[]{:S(2)}, u32[]{:S(2)}) %collective-permute-start.3) | collective-permute-done | bytes 131104 | tf_op jit(solution)/shard_map/ppermute | solution.py:652
  28.7 0.0 collective-permute-done.2.on_chip
  28.7 1.7 %shard_map.135 = (f32[2,8,16,128]{3,2,1,0:T(8,128)}, f32[4,8,16,128]{3,2,1,0:T(8,128)S(1)}) custom-call(f32[2,8,16,128]{3,2,1,0:T(8,128)S(1)} %get-tuple-element.28.now, f32[2,16,16,128]{3,2,1,0:T(8,128)S(1)} %get-tuple-element.26.mid, f32[5,16,16,128]{3,2,1,0:T(8,128)S(1)} %get-tuple-element.30.coeffs, ...), custom_call_target="tpu_custom_call" | custom-call | flops 6553600 | bytes 1638400 | tf_op jit(solution)/shard_map/pallas_call | solution.py:574
  30.4 0.0 all-to-all-done
  30.4 0.2 copy.17
  30.6 1.1 %shard_map.136 = bf16[8,8,16,128]{3,2,1,0:T(8,128)(2,1)} custom-call(bf16[2,4,8,16,128]{4,3,2,1,0:T(8,128)(2,1)S(1)} %bitcast.4, f32[2,16,16,128]{3,2,1,0:T(8,128)S(1)} %get-tuple-element.26.mid, f32[3,8,16,128]{3,2,1,0:T(8,128)S(1)} %get-tuple-element.29.flux, f32[4,8,16,128]{3,2,1,0:T(8,128)S(1)} %get-tuple-element.33.imaged, ...), custom_call_target="tpu_custom_call" | custom-call | flops 983040 | bytes 245760 | tf_op jit(solution)/shard_map/pallas_call | solution.py:574
Async XLA Ops:
  0.6 10.4 %copy-start.6 = (f32[8,16,128]{2,1,0:T(8,128)S(1)}, f32[8,16,128]{2,1,0:T(8,128)}, u32[]{:S(2)}) copy-start(f32[8,16,128]{2,1,0:T(8,128)} %tilt.3) | copy-start | bytes 196612
  2.7 8.3 %copy-start = (bf16[3,128,256]{2,1,0:T(8,128)(2,1)S(1)}, bf16[3,128,256]{2,1,0:T(8,128)(2,1)}, u32[]{:S(2)}) copy-start(bf16[3,128,256]{2,1,0:T(8,128)(2,1)} %constant.2.clone.matrices) | copy-start | bytes 589828
  2.7 8.3 %copy-start.1 = (f32[2,8,16,128]{3,2,1,0:T(8,128)S(1)}, f32[2,8,16,128]{3,2,1,0:T(8,128)}, u32[]{:S(2)}) copy-start(f32[2,8,16,128]{3,2,1,0:T(8,128)} %before.1) | copy-start | bytes 393220
  2.7 8.3 %copy-start.3 = (f32[8,16,128]{2,1,0:T(8,128)S(1)}, f32[8,16,128]{2,1,0:T(8,128)}, u32[]{:S(2)}) copy-start(f32[8,16,128]{2,1,0:T(8,128)} %speed.3) | copy-start | bytes 196612
  2.7 8.3 %copy-start.4 = (f32[8,16,128]{2,1,0:T(8,128)S(1)}, f32[8,16,128]{2,1,0:T(8,128)}, u32[]{:S(2)}) copy-start(f32[8,16,128]{2,1,0:T(8,128)} %epsilon.3) | copy-start | bytes 196612
  2.8 8.3 %copy-start.5 = (f32[8,16,128]{2,1,0:T(8,128)S(1)}, f32[8,16,128]{2,1,0:T(8,128)}, u32[]{:S(2)}) copy-start(f32[8,16,128]{2,1,0:T(8,128)} %delta.3) | copy-start | bytes 196612
  2.8 27.6 %all-to-all-start = ((bf16[16,2,4,8,128]{4,3,2,1,0:T(8,128)(2,1)}), bf16[16,2,4,8,128]{4,3,2,1,0:T(8,128)(2,1)S(1)}, u32[]{:S(2)}, u32[]{:S(2)}) async-start(bf16[16,2,4,8,128]{4,3,2,1,0:T(8,128)(2,1)} %get-tuple-element.19), calls=%async_computation | async-start | bytes 524288 | tf_op jit(solution)/shard_map/all_to_all | solution.py:621
  9.4 1.7 %copy-start.7 = (f32[4,128]{1,0:T(4,128)S(1)}, f32[4,128]{1,0:T(4,128)}, u32[]{:S(2)}) copy-start(f32[4,128]{1,0:T(4,128)} %traces.1) | copy-start | bytes 6148
  9.4 1.7 %copy-start.8 = (s32[128]{0:T(128)S(1)}, s32[128]{0:T(128)}, u32[]{:S(2)}) copy-start(s32[128]{0:T(128)} %receiver_row.1) | copy-start | bytes 1540
  9.4 1.7 %copy-start.9 = (s32[128]{0:T(128)S(1)}, s32[128]{0:T(128)}, u32[]{:S(2)}) copy-start(s32[128]{0:T(128)} %receiver_column.1) | copy-start | bytes 1540
  9.4 1.7 %copy-start.10 = (s32[32]{0:T(128)S(1)}, s32[32]{0:T(128)}, u32[]{:S(2)}) copy-start(s32[32]{0:T(128)} %table.1) | copy-start | bytes 388
  9.4 2.8 %collective-permute-start = (f32[40,16,128]{2,1,0:T(8,128)S(1)}, f32[40,16,128]{2,1,0:T(8,128)S(1)}, u32[]{:S(2)}, u32[]{:S(2)}) collective-permute-start(f32[40,16,128]{2,1,0:T(8,128)S(1)} %get-tuple-element.20), channel_id=1, source_target_pairs={{0,1},{1,0},{2,3},{3,2},{4,5},{5,4},{6,7},{7,6},{8,9},{9,8},{10,11... | collective-permute-start | bytes 983048 | tf_op jit(solution)/shard_map/ppermute | solution.py:620
  9.9 11.8 %copy-start.2 = (f32[2,8,16,128]{3,2,1,0:T(8,128)S(1)}, f32[2,8,16,128]{3,2,1,0:T(8,128)}, u32[]{:S(2)}) copy-start(f32[2,8,16,128]{3,2,1,0:T(8,128)} %prev.3) | copy-start | bytes 393220
  9.9 11.8 %collective-permute-start.1 = (f32[40,16,128]{2,1,0:T(8,128)S(1)}, f32[40,16,128]{2,1,0:T(8,128)S(1)}, u32[]{:S(2)}, u32[]{:S(2)}) collective-permute-start(f32[40,16,128]{2,1,0:T(8,128)S(1)} %get-tuple-element.21), channel_id=1, source_target_pairs={{1,2},{2,1},{3,4},{4,3},{5,6},{6,5},{7,8},{8,7},{9,10},{10,9},{11,... | collective-permute-start | bytes 983048 | tf_op jit(solution)/shard_map/ppermute | solution.py:619
  22.8 5.9 %collective-permute-start.3 = (f32[2,8,16,128]{3,2,1,0:T(8,128)S(1)}, f32[2,8,16,128]{3,2,1,0:T(8,128)S(1)}, u32[]{:S(2)}, u32[]{:S(2)}) collective-permute-start(f32[2,8,16,128]{3,2,1,0:T(8,128)S(1)} %get-tuple-element.28.now), channel_id=1, source_target_pairs={{1,2},{2,1},{3,4},{4,3},{5,6},{6,5},{7,8},{8,7},{9,10},{10,9},{11,... | collective-permute-start | bytes 393224 | tf_op jit(solution)/shard_map/ppermute | solution.py:652
  23.9 4.8 %collective-permute-start.2 = (f32[2,8,16,128]{3,2,1,0:T(8,128)S(1)}, f32[2,8,16,128]{3,2,1,0:T(8,128)S(1)}, u32[]{:S(2)}, u32[]{:S(2)}) collective-permute-start(f32[2,8,16,128]{3,2,1,0:T(8,128)S(1)} %get-tuple-element.28.now), channel_id=1, source_target_pairs={{0,1},{1,0},{2,3},{3,2},{4,5},{5,4},{6,7},{7,6},{8,9},{9,8},{10,11... | collective-permute-start | bytes 393224 | tf_op jit(solution)/shard_map/ppermute | solution.py:653

commit v6 on v5

--- a/solution.py
+++ b/solution.py
@@ -13,6 +13,7 @@
 REACH = 4
 HALO = 2 * REACH
 YPAD = 8
+OUT_PIECES = 4
 
 SECOND = (-205.0 / 72.0, 8.0 / 5.0, -1.0 / 5.0, 8.0 / 315.0, -1.0 / 560.0)
 FIRST = (4.0 / 5.0, -1.0 / 5.0, 4.0 / 105.0, -1.0 / 280.0)
@@ -179,9 +180,9 @@
     return now, (back * slope_x, back * slope_y, back * slope_z)
 
 
-def image_terms(source, n, row, field, flux, offsets, emit):
+def image_terms(source, field, flux, offsets, emit):
     fx, fy, fz = flux
-    s0, s1, s2, s3 = [source[n, c, row].astype(jnp.float32) for c in range(4)]
+    s0, s1, s2, s3 = source
     dot = s1 * fx + s2 * fy + s3 * fz
     lengths = jnp.sqrt(s1 * s1 + s2 * s2 + s3 * s3) * jnp.sqrt(fx * fx + fy * fy + fz * fz)
     cosine = dot / jnp.maximum(lengths, 1.0)
@@ -275,7 +276,9 @@
     )
 
 
-def pack_kernel(now, prev, speed, epsilon, delta, tilt, source, far, near, sorted_source, sems):
+def pack_kernel(
+    now, prev, speed, epsilon, delta, tilt, source, far, near, sorted_source, staged, sems
+):
     rows = now.shape[1]
     odd = lax.rem(lax.axis_index("gx"), 2)
     copies = []
@@ -284,6 +287,10 @@
         copies.append(pltpu.make_async_copy(src, dst, sems.at[len(copies)]))
         copies[-1].start()
 
+    for n in range(source.shape[0]):
+        for c in range(source.shape[1]):
+            copy(source.at[n, c], staged.at[:, n, c])
+    sources = len(copies)
     for out, tail in ((far, odd), (near, 1 - odd)):
         wave_at = tail * (rows - HALO)
         edge_at = tail * (rows - REACH)
@@ -299,10 +306,10 @@
                 field.at[pl.ds(edge_at, REACH)],
                 out.at[pl.ds(2 * HALO + (2 + m) * REACH, REACH)],
             )
-    for n in range(source.shape[0]):
-        for c in range(source.shape[1]):
-            copy(source.at[n, c], sorted_source.at[:, n, c])
-    for one in copies:
+    for one in copies[:sources]:
+        one.wait()
+    copy(staged, sorted_source)
+    for one in copies[sources:]:
         one.wait()
 
 
@@ -509,8 +516,19 @@
     each_row(rows, width, fluxes)
 
 
-def image_kernel(source, mid, flux, imaged, offsets, images):
-    rows, width = flux.shape[1], flux.shape[2]
+def image_kernel(
+    arrived, mid, flux, imaged, offsets, wave, images, wave_out, block, lines, sems
+):
+    rows, width, _ = flux.shape[1:]
+    whole = pltpu.make_async_copy(wave, wave_out, sems.at[0])
+    whole.start()
+    lines[...] = arrived[...].astype(jnp.float32).reshape(lines.shape)
+    parts = arrived.shape[2]
+    stride = lines.shape[0] // width
+
+    def source(n, row):
+        begin = n * parts * rows + row
+        return [lines[pl.ds(begin + c * rows, width, stride=stride), :] for c in range(parts)]
 
     def image_row(row):
         totals = [None] * NBIN
@@ -519,14 +537,25 @@
             totals[b] = term
 
         def finish(b, term):
-            images[b, row] = (totals[b] + term).astype(images.dtype)
+            block[b, row] = (totals[b] + term).astype(block.dtype)
 
         early = [flux[a, row] for a in range(3)]
-        image_terms(source, 0, row, mid[0, row + REACH], early, offsets, keep)
+        image_terms(source(0, row), mid[0, row + REACH], early, offsets, keep)
         late = [imaged[a, row] for a in range(1, 4)]
-        image_terms(source, 1, row, imaged[0, row], late, offsets, finish)
-
-    each_row(rows, width, image_row)
+        image_terms(source(1, row), imaged[0, row], late, offsets, finish)
+
+    pieces = []
+    size = rows // OUT_PIECES
+    for piece in range(OUT_PIECES):
+        each_row(size, width, lambda row: image_row(row + piece * size))
+        part = pl.ds(piece * size, size)
+        pieces.append(
+            pltpu.make_async_copy(block.at[:, part], images.at[:, part], sems.at[1 + piece])
+        )
+        pieces[-1].start()
+    for piece in pieces:
+        piece.wait()
+    whole.wait()
 
 
 def local(
@@ -570,12 +599,12 @@
     def planes(*lead):
         return jax.ShapeDtypeStruct(lead + plane, f32)
 
-    def call(kernel, outs, ins, in_specs, scratch, grant, cost):
+    def call(kernel, outs, ins, in_specs, scratch, grant, cost, out_specs=None):
         return pl.pallas_call(
             kernel,
             out_shape=outs,
             in_specs=in_specs,
-            out_specs=jax.tree.map(lambda _: vmem, outs),
+            out_specs=out_specs or jax.tree.map(lambda _: vmem, outs),
             scratch_shapes=scratch,
             compiler_params=pltpu.CompilerParams(
                 vmem_limit_bytes=4 * 1024 * 1024 + grant * plane_bytes
@@ -612,9 +641,13 @@
             for x in (wave_now, wave_prev, *medium, by_owner)
         ],
         [in_hbm] * 7,
-        [pltpu.SemaphoreType.DMA((16 + snaps * parts,))],
+        [
+            pltpu.VMEM((count, snaps, parts, rows, depth), source_store.dtype),
+            pltpu.SemaphoreType.DMA((17 + snaps * parts,)),
+        ],
         120,
         200,
+        (vmem, vmem, in_hbm),
     )
     off_chip = lax.ppermute(far_pack, both_axes, off_chip_pairs)
     on_chip = lax.ppermute(near_pack, "gx", on_chip_pairs)
@@ -669,16 +702,20 @@
         30 * wide,
         400 * rows,
     )
-    images = call(
+    return call(
         image_kernel,
-        jax.ShapeDtypeStruct((NBIN, rows) + plane, jnp.bfloat16),
-        (jnp.transpose(arrived, (1, 2, 3, 0, 4)), mid, flux, imaged, offsets),
-        [vmem] * 5,
-        [],
+        (jax.ShapeDtypeStruct((NBIN, rows) + plane, jnp.bfloat16), planes(2, rows)),
+        (arrived, mid, flux, imaged, offsets, final),
+        [vmem] * 6,
+        [
+            pltpu.VMEM((NBIN, rows) + plane, jnp.bfloat16),
+            pltpu.VMEM((sorted_source.size // depth, depth), f32),
+            pltpu.SemaphoreType.DMA((1 + OUT_PIECES,)),
+        ],
         16 * wide,
         60 * rows,
-    )
-    return images, final
+        (in_hbm, in_hbm),
+    )
 
 
 def solution(mesh):

time: 31.9 us -> 31 us (0.972)
  Pallas kernels: 7.34 us -> 6.59 us
    pallas_call x6, Pallas kernels: 7.34 us -> 6.59 us  [call(): pl.pallas_call(kernel, out_shape=outs, in_specs=in_specs, out_specs=out_s...]
  transfers between devices with their start and end apart: 5 -> 5, of which waited for: 2 -> 2; matrix products, arithmetic and copies ran while one was open for 0% -> 0% of each run, Pallas kernels for 13% -> 12%
where the time goes in v6:
time: 31 us; the launch traced here: 30.7 us
  waiting for transfers between devices  14 us (45%)
  starting transfers between devices  9.27 us (30%)
  Pallas kernels  6.59 us (21%)
  between operations  0.82 us (3%)
    ppermute x1, waiting for transfers between devices, local(): off_chip = lax.ppermute(far_pack, both_axes, off_chip_pairs)  9.5 us
    pallas_call x6, Pallas kernels, call(): pl.pallas_call(kernel, out_shape=outs, in_specs=in_specs, out_specs=out_s...  6.59 us
    all_to_all x1, starting transfers between devices, local(): lax.all_to_all(sorted_source, 'gx', split_axis=0, concat_axis=0, tiled=True)  6.58 us
    ppermute x1, waiting for transfers between devices, local(): off_chip = lax.ppermute(side(odd == 1), both_axes, off_chip_pairs)  4.49 us
    ppermute x1, starting transfers between devices, local(): off_chip = lax.ppermute(far_pack, both_axes, off_chip_pairs)  1.18 us
    ppermute x1, starting transfers between devices, local(): off_chip = lax.ppermute(side(odd == 1), both_axes, off_chip_pairs)  1.04 us
  transfers between devices with their start and end apart: 5, of which 2 were waited for; matrix products, arithmetic and copies ran while one was open for 0% of the time, Pallas kernels for 12%

profile of v6, /device:TPU:21, one launch (start us, length us, event | category | flops | bytes accessed | tf_op | source)
XLA Modules:
  0.0 30.7 jit_solution(1233651638122027762)
XLA Ops:
  0.6 0.0 copy-start.6
  0.6 1.8 %shard_map.131 = (f32[40,16,128]{2,1,0:T(8,128)S(1)}, f32[40,16,128]{2,1,0:T(8,128)S(1)}, bf16[16,2,4,8,128]{4,3,2,1,0:T(8,128)(2,1)}) custom-call(f32[2,8,16,128]{3,2,1,0:T(8,128)} %before.1, f32[2,8,16,128]{3,2,1,0:T(8,128)} %prev.3, f32[8,16,128]{2,1,0:T(8,128)} %speed.3, f32[8,16,128]{2,1,0:T(8,128)} %epsilon.3, f32[8,16,128]{2,1,0:T(8,128)} %delta.3, ...), custom_call_target="tpu_custom_call" | custom-call | flops 409600 | bytes 102400 | tf_op jit(solution)/shard_map/pallas_call | solution.py:603
  2.5 0.0 copy-start
  2.5 0.0 copy-start.1
  2.5 0.0 copy-start.3
  2.5 0.0 copy-start.4
  2.5 0.0 copy-start.5
  2.5 6.6 %all-to-all-start = ((bf16[16,2,4,8,128]{4,3,2,1,0:T(8,128)(2,1)}), bf16[16,2,4,8,128]{4,3,2,1,0:T(8,128)(2,1)S(1)}, u32[]{:S(2)}, u32[]{:S(2)}) async-start(bf16[16,2,4,8,128]{4,3,2,1,0:T(8,128)(2,1)} %get-tuple-element.19), calls=%async_computation | async-start | bytes 524288 | tf_op jit(solution)/shard_map/all_to_all | solution.py:654
  9.1 0.0 copy-start.7
  9.1 0.0 copy-start.8
  9.1 0.0 copy-start.9
  9.1 0.0 copy-start.10
  9.2 0.5 %collective-permute-start = (f32[40,16,128]{2,1,0:T(8,128)S(1)}, f32[40,16,128]{2,1,0:T(8,128)S(1)}, u32[]{:S(2)}, u32[]{:S(2)}) collective-permute-start(f32[40,16,128]{2,1,0:T(8,128)S(1)} %get-tuple-element.20), channel_id=1, source_target_pairs={{0,1},{1,0},{2,3},{3,2},{4,5},{5,4},{6,7},{7,6},{8,9},{9,8},{10,11... | collective-permute-start | bytes 983048 | tf_op jit(solution)/shard_map/ppermute | solution.py:653
  9.6 0.0 copy-start.2
  9.6 1.2 %collective-permute-start.1 = (f32[40,16,128]{2,1,0:T(8,128)S(1)}, f32[40,16,128]{2,1,0:T(8,128)S(1)}, u32[]{:S(2)}, u32[]{:S(2)}) collective-permute-start(f32[40,16,128]{2,1,0:T(8,128)S(1)} %get-tuple-element.21), channel_id=1, source_target_pairs={{1,2},{2,1},{3,4},{4,3},{5,6},{6,5},{7,8},{8,7},{9,10},{10,9},{11,... | collective-permute-start | bytes 983048 | tf_op jit(solution)/shard_map/ppermute | solution.py:652
  10.8 0.0 copy-done.6
  10.8 0.0 copy-done
  10.8 0.0 copy-done.1
  10.8 0.0 copy-done.3
  10.8 0.0 copy-done.4
  10.8 0.0 copy-done.5
  10.8 0.0 copy-done.7
  10.9 0.0 copy-done.8
  10.9 0.0 copy-done.9
  10.9 0.0 copy-done.10
  10.9 1.0 %shard_map.132 = (f32[5,8,16,128]{3,2,1,0:T(8,128)S(1)}, f32[4,16,16,128]{3,2,1,0:T(8,128)S(1)}, f32[2,8,16,128]{3,2,1,0:T(8,128)S(1)}, f32[2,8,16,128]{3,2,1,0:T(8,128)S(1)}, f32[16,128]{1,0:T(8,128)S(1)}) custom-call(f32[2,8,16,128]{3,2,1,0:T(8,128)S(1)} %copy-done.1, f32[8,16,128]{2,1,0:T(8,128)S(1)} %copy-done.3, f32[8,16,128]{2,1,0:T(8,128)S(1)} %copy-done.4, ...), custom_call_target="tpu_custom_call" | custom-call | flops 983040 | bytes 245760 | tf_op jit(solution)/shard_map/pallas_call | solution.py:603
  11.9 0.0 collective-permute-done.on_chip
  11.9 9.5 %collective-permute-done.1.off_chip = f32[40,16,128]{2,1,0:T(8,128)S(1)} collective-permute-done((f32[40,16,128]{2,1,0:T(8,128)S(1)}, f32[40,16,128]{2,1,0:T(8,128)S(1)}, u32[]{:S(2)}, u32[]{:S(2)}) %collective-permute-start.1) | collective-permute-done | bytes 327712 | tf_op jit(solution)/shard_map/ppermute | solution.py:652
  21.4 0.0 copy-done.2
  21.4 1.1 %shard_map.133 = (f32[2,8,16,128]{3,2,1,0:T(8,128)S(1)}, f32[2,16,16,128]{3,2,1,0:T(8,128)S(1)}, f32[5,16,16,128]{3,2,1,0:T(8,128)S(1)}, f32[8,16,128]{2,1,0:T(8,128)S(1)}) custom-call(f32[2,8,16,128]{3,2,1,0:T(8,128)S(1)} %copy-done.1, f32[2,8,16,128]{3,2,1,0:T(8,128)S(1)} %copy-done.2, f32[40,16,128]{2,1,0:T(8,128)S(1)} %collective-permute-done.on_chip, ...), custom_call_target="tpu_custom_call" | custom-call | flops 6553600 | bytes 1638400 | tf_op jit(solution)/shard_map/pallas_call | solution.py:603
  22.6 1.0 %collective-permute-start.3 = (f32[2,8,16,128]{3,2,1,0:T(8,128)S(1)}, f32[2,8,16,128]{3,2,1,0:T(8,128)S(1)}, u32[]{:S(2)}, u32[]{:S(2)}) collective-permute-start(f32[2,8,16,128]{3,2,1,0:T(8,128)S(1)} %get-tuple-element.28.now), channel_id=1, source_target_pairs={{1,2},{2,1},{3,4},{4,3},{5,6},{6,5},{7,8},{8,7},{9,10},{10,9},{11,... | collective-permute-start | bytes 393224 | tf_op jit(solution)/shard_map/ppermute | solution.py:685
  23.6 0.0 collective-permute-start.2
  23.6 0.3 %shard_map.134 = (f32[3,8,16,128]{3,2,1,0:T(8,128)S(1)}, f32[2,8,16,128]{3,2,1,0:T(8,128)S(1)}, f32[2,8,16,128]{3,2,1,0:T(8,128)S(1)}) custom-call(f32[2,8,16,128]{3,2,1,0:T(8,128)S(1)} %copy-done.1, f32[2,16,16,128]{3,2,1,0:T(8,128)S(1)} %get-tuple-element.26.mid, f32[8,16,128]{2,1,0:T(8,128)S(1)} %get-tuple-element.27.slope_z, ...), custom_call_target="tpu_custom_call" | custom-call | flops 983040 | bytes 245760 | tf_op jit(solution)/shard_map/pallas_call | solution.py:603
  24.0 4.5 %collective-permute-done.3.off_chip = f32[2,8,16,128]{3,2,1,0:T(8,128)S(1)} collective-permute-done((f32[2,8,16,128]{3,2,1,0:T(8,128)S(1)}, f32[2,8,16,128]{3,2,1,0:T(8,128)S(1)}, u32[]{:S(2)}, u32[]{:S(2)}) %collective-permute-start.3) | collective-permute-done | bytes 131104 | tf_op jit(solution)/shard_map/ppermute | solution.py:685
  28.5 0.0 collective-permute-done.2.on_chip
  28.5 1.0 %shard_map.135 = (f32[2,8,16,128]{3,2,1,0:T(8,128)S(1)}, f32[4,8,16,128]{3,2,1,0:T(8,128)S(1)}) custom-call(f32[2,8,16,128]{3,2,1,0:T(8,128)S(1)} %get-tuple-element.28.now, f32[2,16,16,128]{3,2,1,0:T(8,128)S(1)} %get-tuple-element.26.mid, f32[5,16,16,128]{3,2,1,0:T(8,128)S(1)} %get-tuple-element.30.coeffs, ...), custom_call_target="tpu_custom_call" | custom-call | flops 6553600 | bytes 1638400 | tf_op jit(solution)/shard_map/pallas_call | solution.py:603
  29.5 0.0 all-to-all-done.arrived
  29.5 1.2 %shard_map.136 = (bf16[8,8,16,128]{3,2,1,0:T(8,128)(2,1)}, f32[2,8,16,128]{3,2,1,0:T(8,128)}) custom-call(bf16[16,2,4,8,128]{4,3,2,1,0:T(8,128)(2,1)S(1)} %all-to-all-done.arrived, f32[2,16,16,128]{3,2,1,0:T(8,128)S(1)} %get-tuple-element.26.mid, f32[3,8,16,128]{3,2,1,0:T(8,128)S(1)} %get-tuple-element.29.flux, ...), custom_call_target="tpu_custom_call" | custom-call | flops 983040 | bytes 245760 | tf_op jit(solution)/shard_map/pallas_call | solution.py:603
Async XLA Ops:
  0.6 10.2 %copy-start.6 = (f32[8,16,128]{2,1,0:T(8,128)S(1)}, f32[8,16,128]{2,1,0:T(8,128)}, u32[]{:S(2)}) copy-start(f32[8,16,128]{2,1,0:T(8,128)} %tilt.3) | copy-start | bytes 196612
  2.5 8.3 %copy-start = (bf16[3,128,256]{2,1,0:T(8,128)(2,1)S(1)}, bf16[3,128,256]{2,1,0:T(8,128)(2,1)}, u32[]{:S(2)}) copy-start(bf16[3,128,256]{2,1,0:T(8,128)(2,1)} %constant.2.clone.matrices) | copy-start | bytes 589828
  2.5 8.3 %copy-start.1 = (f32[2,8,16,128]{3,2,1,0:T(8,128)S(1)}, f32[2,8,16,128]{3,2,1,0:T(8,128)}, u32[]{:S(2)}) copy-start(f32[2,8,16,128]{3,2,1,0:T(8,128)} %before.1) | copy-start | bytes 393220
  2.5 8.3 %copy-start.3 = (f32[8,16,128]{2,1,0:T(8,128)S(1)}, f32[8,16,128]{2,1,0:T(8,128)}, u32[]{:S(2)}) copy-start(f32[8,16,128]{2,1,0:T(8,128)} %speed.3) | copy-start | bytes 196612
  2.5 8.3 %copy-start.4 = (f32[8,16,128]{2,1,0:T(8,128)S(1)}, f32[8,16,128]{2,1,0:T(8,128)}, u32[]{:S(2)}) copy-start(f32[8,16,128]{2,1,0:T(8,128)} %epsilon.3) | copy-start | bytes 196612
  2.5 8.3 %copy-start.5 = (f32[8,16,128]{2,1,0:T(8,128)S(1)}, f32[8,16,128]{2,1,0:T(8,128)}, u32[]{:S(2)}) copy-start(f32[8,16,128]{2,1,0:T(8,128)} %delta.3) | copy-start | bytes 196612
  2.5 27.0 %all-to-all-start = ((bf16[16,2,4,8,128]{4,3,2,1,0:T(8,128)(2,1)}), bf16[16,2,4,8,128]{4,3,2,1,0:T(8,128)(2,1)S(1)}, u32[]{:S(2)}, u32[]{:S(2)}) async-start(bf16[16,2,4,8,128]{4,3,2,1,0:T(8,128)(2,1)} %get-tuple-element.19), calls=%async_computation | async-start | bytes 524288 | tf_op jit(solution)/shard_map/all_to_all | solution.py:654
  9.1 1.7 %copy-start.7 = (f32[4,128]{1,0:T(4,128)S(1)}, f32[4,128]{1,0:T(4,128)}, u32[]{:S(2)}) copy-start(f32[4,128]{1,0:T(4,128)} %traces.1) | copy-start | bytes 6148
  9.1 1.7 %copy-start.8 = (s32[128]{0:T(128)S(1)}, s32[128]{0:T(128)}, u32[]{:S(2)}) copy-start(s32[128]{0:T(128)} %receiver_row.1) | copy-start | bytes 1540
  9.1 1.7 %copy-start.9 = (s32[128]{0:T(128)S(1)}, s32[128]{0:T(128)}, u32[]{:S(2)}) copy-start(s32[128]{0:T(128)} %receiver_column.1) | copy-start | bytes 1540
  9.1 1.7 %copy-start.10 = (s32[32]{0:T(128)S(1)}, s32[32]{0:T(128)}, u32[]{:S(2)}) copy-start(s32[32]{0:T(128)} %table.1) | copy-start | bytes 388
  9.2 2.8 %collective-permute-start = (f32[40,16,128]{2,1,0:T(8,128)S(1)}, f32[40,16,128]{2,1,0:T(8,128)S(1)}, u32[]{:S(2)}, u32[]{:S(2)}) collective-permute-start(f32[40,16,128]{2,1,0:T(8,128)S(1)} %get-tuple-element.20), channel_id=1, source_target_pairs={{0,1},{1,0},{2,3},{3,2},{4,5},{5,4},{6,7},{7,6},{8,9},{9,8},{10,11... | collective-permute-start | bytes 983048 | tf_op jit(solution)/shard_map/ppermute | solution.py:653
  9.6 11.8 %copy-start.2 = (f32[2,8,16,128]{3,2,1,0:T(8,128)S(1)}, f32[2,8,16,128]{3,2,1,0:T(8,128)}, u32[]{:S(2)}) copy-start(f32[2,8,16,128]{3,2,1,0:T(8,128)} %prev.3) | copy-start | bytes 393220
  9.6 11.8 %collective-permute-start.1 = (f32[40,16,128]{2,1,0:T(8,128)S(1)}, f32[40,16,128]{2,1,0:T(8,128)S(1)}, u32[]{:S(2)}, u32[]{:S(2)}) collective-permute-start(f32[40,16,128]{2,1,0:T(8,128)S(1)} %get-tuple-element.21), channel_id=1, source_target_pairs={{1,2},{2,1},{3,4},{4,3},{5,6},{6,5},{7,8},{8,7},{9,10},{10,9},{11,... | collective-permute-start | bytes 983048 | tf_op jit(solution)/shard_map/ppermute | solution.py:652
  22.6 5.9 %collective-permute-start.3 = (f32[2,8,16,128]{3,2,1,0:T(8,128)S(1)}, f32[2,8,16,128]{3,2,1,0:T(8,128)S(1)}, u32[]{:S(2)}, u32[]{:S(2)}) collective-permute-start(f32[2,8,16,128]{3,2,1,0:T(8,128)S(1)} %get-tuple-element.28.now), channel_id=1, source_target_pairs={{1,2},{2,1},{3,4},{4,3},{5,6},{6,5},{7,8},{8,7},{9,10},{10,9},{11,... | collective-permute-start | bytes 393224 | tf_op jit(solution)/shard_map/ppermute | solution.py:685
  23.6 4.8 %collective-permute-start.2 = (f32[2,8,16,128]{3,2,1,0:T(8,128)S(1)}, f32[2,8,16,128]{3,2,1,0:T(8,128)S(1)}, u32[]{:S(2)}, u32[]{:S(2)}) collective-permute-start(f32[2,8,16,128]{3,2,1,0:T(8,128)S(1)} %get-tuple-element.28.now), channel_id=1, source_target_pairs={{0,1},{1,0},{2,3},{3,2},{4,5},{5,4},{6,7},{7,6},{8,9},{9,8},{10,11... | collective-permute-start | bytes 393224 | tf_op jit(solution)/shard_map/ppermute | solution.py:686

commit v7 on v6

--- a/solution.py
+++ b/solution.py
@@ -133,7 +133,7 @@
     return jnp.where(inside, local_row * width + column_ref[...].reshape(1, count), -1)
 
 
-def time_step(rows, width, fields, earlier, coeffs, slopes, curves, inject, emit):
+def time_step(begin, rows, width, fields, earlier, coeffs, slopes, curves, emit):
     p, q = fields
     slope_p, slope_q = slopes
     curve_p, curve_q = curves
@@ -162,9 +162,56 @@
         prev_p, prev_q = earlier(row)
         next_p = 2.0 * now_p - prev_p + (gain * across + mixed * rotated)
         next_q = 2.0 * now_q - prev_q + (mixed * across + speed * rotated)
-        emit(row, next_p + inject(row), next_q)
-
-    each_row(rows, width, update)
+        emit(row, next_p, next_q)
+
+    each_row(rows, width, lambda row: update(begin + row))
+
+
+def border_terms(row, rows, read, slope):
+    curve, mixed = None, None
+    for border in (REACH, rows + REACH):
+        for k in range(1, 5):
+            for other, sign in ((row + k, 1.0), (row - k, -1.0)):
+                low, high = min(row, other), max(row, other)
+                if low < border <= high:
+                    c = SECOND[k] * read(other)
+                    m = (sign * FIRST[k - 1]) * slope(other)
+                    curve = c if curve is None else curve + c
+                    mixed = m if mixed is None else mixed + m
+    return curve, mixed
+
+
+def add_border(row, rows, reads, slopes, coeffs, base):
+    next_p, next_q = base
+    xx_p, xz_p = border_terms(row, rows, reads[0], slopes[0])
+    if xx_p is None:
+        return next_p, next_q
+    xx_q, xz_q = border_terms(row, rows, reads[1], slopes[1])
+    speed, gain, mixed, sine_sq, sine_double = coeffs
+    across = xx_p - (sine_sq * xx_p + sine_double * xz_p)
+    rotated = sine_sq * xx_q + sine_double * xz_q
+    return (
+        next_p + (gain * across + mixed * rotated),
+        next_q + (mixed * across + speed * rotated),
+    )
+
+
+def block_step(rows, width, fields, slopes, curves, matrices, earlier, coeffs, emit):
+    p, q = fields
+    inner = slice(YPAD, YPAD + width)
+    for field, slope, curve in (
+        (lambda b, n: p[pl.ds(b, n), inner, :], slopes[0], curves[0]),
+        (lambda b, n: q[pl.ds(b, n)], slopes[1], curves[1]),
+    ):
+        depth_rows(field, slope, curve, REACH, rows, width, matrices)
+    time_step(0, rows, width, fields, earlier, coeffs, slopes, curves, emit)
+
+
+def clear_sides(rows, *refs):
+    for ref in refs:
+        zeros = jnp.zeros((REACH,) + ref.shape[1:], jnp.float32)
+        ref[pl.ds(0, REACH)] = zeros
+        ref[pl.ds(rows + REACH, REACH)] = zeros
 
 
 def flux_row(row, width, p, slope_z, before):
@@ -184,15 +231,16 @@
     fx, fy, fz = flux
     s0, s1, s2, s3 = source
     dot = s1 * fx + s2 * fy + s3 * fz
-    lengths = jnp.sqrt(s1 * s1 + s2 * s2 + s3 * s3) * jnp.sqrt(fx * fx + fy * fy + fz * fz)
-    cosine = dot / jnp.maximum(lengths, 1.0)
-    scaled = (cosine + 1.0) * offsets[NBIN + 1 : NBIN + 2, :]
+    squares = (s1 * s1 + s2 * s2 + s3 * s3) * (fx * fx + fy * fy + fz * fz)
+    cosine = dot * jnp.minimum(lax.rsqrt(squares), 1.0)
+    scaled = (cosine + 1.0) * offsets[NBIN : NBIN + 1, :]
     strength = s0 * field
-    ramps = [
-        jnp.clip(scaled - offsets[b : b + 1, :], 0.0, 1.0) * strength for b in range(NBIN + 1)
-    ]
-    for b in range(NBIN):
-        emit(b, ramps[b] - ramps[b + 1])
+    above = strength
+    for b in range(NBIN - 1):
+        beyond = jnp.clip(scaled - offsets[b + 1 : b + 2, :], 0.0, 1.0) * strength
+        emit(b, above - beyond)
+        above = beyond
+    emit(NBIN - 1, above)
 
 
 def clear_pads(ref, width):
@@ -224,123 +272,121 @@
     return (at > 0) & (at < lax.axis_size("gx") - 1)
 
 
-def two_steps(
-    t, rows, width, waves, own, first_prev, coeffs, inject, matrices, scratch, mid_emit, emit, second_prev
-):
-    p, q = waves
-    slope_p, slope_q, curve_p, curve_q, p1, q1 = scratch
+def second_step(rows, width, p1, q1, slopes, curves, earlier, coeffs, inject, matrices, emit):
     inner = slice(YPAD, YPAD + width)
-    clear_pads(p1, width)
-    for dst, src in zip((slope_p, slope_q, curve_p, curve_q), own):
-        dst[pl.ds(HALO, rows)] = src
-
-    def read_p(start, size):
-        return p[pl.ds(start, size), inner, :]
-
-    def read_q(start, size):
-        return q[pl.ds(start, size)]
-
-    for begin in (0, rows + HALO):
-        depth_rows(read_p, slope_p, curve_p, begin, HALO, width, matrices)
-        depth_rows(read_q, slope_q, curve_q, begin, HALO, width, matrices)
-
-    def keep(row, next_p, next_q):
-        p1[row, inner, :] = next_p
-        q1[row] = next_q
-        mid_emit(row, next_p, next_q)
-
     ext = rows + 2 * REACH
+    depth_rows(
+        lambda b, n: p1[pl.ds(b, n), inner, :], slopes[0], curves[0], 0, ext, width, matrices
+    )
+    depth_rows(lambda b, n: q1[pl.ds(b, n)], slopes[1], curves[1], 0, ext, width, matrices)
+
+    def finish(row, next_p, next_q):
+        emit(row, next_p + inject[row + REACH], next_q)
+
     time_step(
-        ext,
-        width,
-        waves,
-        first_prev,
-        lambda row: [coeffs[c, row] for c in range(5)],
-        (slope_p, slope_q),
-        (curve_p, curve_q),
-        lambda row: inject[t, row],
-        keep,
-    )
-    depth_rows(lambda b, n: p1[pl.ds(b, n), inner, :], slope_p, curve_p, 0, ext, width, matrices)
-    depth_rows(lambda b, n: q1[pl.ds(b, n)], slope_q, curve_q, 0, ext, width, matrices)
-    time_step(
+        0,
         rows,
         width,
         (p1, q1),
-        second_prev,
+        earlier,
         lambda row: [coeffs[c, row + REACH] for c in range(5)],
-        (slope_p, slope_q),
-        (curve_p, curve_q),
-        lambda row: inject[t + 1, row + REACH],
-        emit,
+        slopes,
+        curves,
+        finish,
     )
 
 
 def pack_kernel(
-    now, prev, speed, epsilon, delta, tilt, source, far, near, sorted_source, staged, sems
-):
-    rows = now.shape[1]
-    odd = lax.rem(lax.axis_index("gx"), 2)
-    copies = []
-
-    def copy(src, dst):
-        copies.append(pltpu.make_async_copy(src, dst, sems.at[len(copies)]))
-        copies[-1].start()
-
-    for n in range(source.shape[0]):
-        for c in range(source.shape[1]):
-            copy(source.at[n, c], staged.at[:, n, c])
-    sources = len(copies)
-    for out, tail in ((far, odd), (near, 1 - odd)):
-        wave_at = tail * (rows - HALO)
-        edge_at = tail * (rows - REACH)
-        for f in range(2):
-            copy(now.at[f, pl.ds(wave_at, HALO)], out.at[pl.ds(f * HALO, HALO)])
-        for f in range(2):
-            copy(
-                prev.at[f, pl.ds(edge_at, REACH)],
-                out.at[pl.ds(2 * HALO + f * REACH, REACH)],
-            )
-        for m, field in enumerate((speed, epsilon, delta, tilt)):
-            copy(
-                field.at[pl.ds(edge_at, REACH)],
-                out.at[pl.ds(2 * HALO + (2 + m) * REACH, REACH)],
-            )
-    for one in copies[:sources]:
-        one.wait()
-    copy(staged, sorted_source)
-    for one in copies[sources:]:
-        one.wait()
-
-
-def prep_kernel(
     now,
+    prev,
     speed,
     epsilon,
     delta,
     tilt,
-    receiver_row,
-    receiver_column,
-    traces,
-    table,
+    source,
     matrices,
+    far,
+    near,
+    sorted_source,
     coeffs,
-    inject,
+    base,
     slopes,
-    curves,
-    offsets,
+    staged,
+    p,
+    q,
+    before,
+    medium,
+    slope_p,
+    slope_q,
+    curve_p,
+    curve_q,
+    weights,
+    sems,
 ):
-    rows, width, depth = speed.shape
-    each_row(
+    rows, width = now.shape[1], now.shape[2]
+    odd = lax.rem(lax.axis_index("gx"), 2)
+    ends = ((far, odd), (near, 1 - odd))
+    copies = []
+    clear_pads(p, width)
+    clear_sides(rows, p, q, slope_p, slope_q)
+
+    def copy(src, dst):
+        copies.append(pltpu.make_async_copy(src, dst, sems.at[len(copies)]))
+        copies[-1].start()
+        return copies[-1]
+
+    own = pl.ds(REACH, rows)
+    local = [copy(matrices, weights)]
+    local.append(copy(now.at[0], p.at[own, pl.ds(YPAD, width)]))
+    local.append(copy(now.at[1], q.at[own]))
+    fields = (speed, epsilon, delta, tilt)
+    for m, field in enumerate(fields):
+        local.append(copy(field, medium.at[m]))
+    local.append(copy(prev, before))
+    arriving = []
+    for n in range(source.shape[0]):
+        for c in range(source.shape[1]):
+            arriving.append(copy(source.at[n, c], staged.at[:, n, c]))
+    edges = []
+    for out, tail in ends:
+        edge = pl.ds(tail * (rows - REACH), REACH)
+        for f in range(2):
+            edges.append(copy(now.at[f, edge], out.at[pl.ds(f * REACH, REACH)]))
+        for m, field in enumerate(fields):
+            edges.append(copy(field.at[edge], out.at[pl.ds((4 + m) * REACH, REACH)]))
+    for one in local + arriving:
+        one.wait()
+    leaving = copy(staged, sorted_source)
+    each_row(rows, width, lambda r: derive(coeffs, r, *[medium[m, r] for m in range(4)]))
+
+    def emit(row, next_p, next_q):
+        base[0, row] = next_p
+        base[1, row] = next_q
+
+    block_step(
         rows,
         width,
-        lambda r: derive(coeffs, r, speed[r], epsilon[r], delta[r], tilt[r]),
-    )
-    for f in range(2):
-        depth_rows(
-            lambda b, n: now[f, pl.ds(b, n)], slopes.at[f], curves.at[f], 0, rows, width, matrices
-        )
-    flat = receivers(receiver_row, receiver_column, rows, width)
+        (p, q),
+        (slope_p, slope_q),
+        (curve_p, curve_q),
+        weights,
+        lambda row: (before[0, row], before[1, row]),
+        lambda row: [coeffs[c, row] for c in range(5)],
+        emit,
+    )
+    slopes[0] = slope_p[own]
+    slopes[1] = slope_q[own]
+    for out, tail in ends:
+        for f in range(2):
+            out[pl.ds((2 + f) * REACH, REACH)] = base[f, pl.ds(tail * (rows - REACH), REACH)]
+    for one in edges:
+        one.wait()
+    leaving.wait()
+
+
+def prep_kernel(receiver_row, receiver_column, traces, table, inject, offsets):
+    _, ext, width, depth = inject.shape
+    flat = receivers(receiver_row, receiver_column, ext - 2 * REACH, width)
 
     def samples(row):
         cell = lax.broadcasted_iota(jnp.int32, (width, flat.shape[1]), 0) + row * width
@@ -350,7 +396,7 @@
             column = jnp.sum(jnp.where(hit, traces[t : t + 1, :], 0.0), axis=1, keepdims=True)
             inject[t, row] = jnp.where(lane == REC_DEPTH, column, 0.0)
 
-    each_row(rows + 2 * REACH, width, samples)
+    each_row(ext, width, samples)
     fine = table.shape[0]
     starts = [jnp.int32(0)] * NBIN
     for f in range(fine):
@@ -358,20 +404,19 @@
         for b in range(1, NBIN):
             starts[b] = starts[b] + (named < b).astype(jnp.int32)
     values = [s.astype(jnp.float32) - 1.0 for s in starts]
-    values = values + [jnp.float32(fine - 1), jnp.float32(0.5 * (fine - 1))]
+    values.append(jnp.float32(0.5 * (fine - 1)))
     for b, value in enumerate(values):
         offsets[b : b + 1, :] = jnp.full((1, depth), value, jnp.float32)
 
 
 def early_kernel(
     now,
-    prev,
     on_chip,
     off_chip,
     own_coeffs,
+    base,
+    own_slopes,
     inject,
-    slopes,
-    curves,
     matrices,
     out,
     mid,
@@ -379,41 +424,52 @@
     slope_out,
     p,
     q,
-    prev_ext,
-    *scratch,
+    ext_base,
+    slope_p,
+    slope_q,
+    curve_p,
+    curve_q,
+    p1,
 ):
     rows, width = now.shape[1], now.shape[2]
-    near, far = side_starts(rows, HALO)
+    inner = slice(YPAD, YPAD + width)
+    near, far = side_starts(rows, REACH)
     inside = has_far_side()
-    clear_pads(p, width)
-    place(
-        p,
-        q,
-        now,
-        (
-            (near, lambda a, n: on_chip[pl.ds(a, n)]),
-            (far, lambda a, n: jnp.where(inside, off_chip[pl.ds(a, n)], 0.0)),
-        ),
-        width,
-    )
-    near, far = side_starts(rows, REACH)
-    base = 2 * HALO
+    clear_pads(p1, width)
+    own = pl.ds(REACH, rows)
+    p[own], q[own] = now[0], now[1]
+    slope_p[own], slope_q[own] = own_slopes[0], own_slopes[1]
+    for f in range(2):
+        ext_base[f, own] = base[f]
     for c in range(5):
-        coeffs[c, pl.ds(REACH, rows)] = own_coeffs[c]
-    for f in range(2):
-        prev_ext[f, pl.ds(REACH, rows)] = prev[f]
-    for at, part, real in ((near, on_chip, True), (far, off_chip, inside)):
-
-        def only_real(value, real=real):
-            return value if real is True else jnp.where(real, value, 0.0)
-
-        for f in range(2):
-            prev_ext[f, pl.ds(at, REACH)] = only_real(part[pl.ds(base + f * REACH, REACH)])
+        coeffs[c, own] = own_coeffs[c]
+    for at, part, real in ((near, on_chip, None), (far, off_chip, inside)):
+
+        def take(index, real=real, part=part):
+            value = part[pl.ds(index * REACH, REACH)]
+            return value if real is None else jnp.where(real, value, 0.0)
+
+        side = pl.ds(at, REACH)
+        p[side], q[side] = take(0), take(1)
+        ext_base[0, side], ext_base[1, side] = take(2), take(3)
+        medium = [take(4)] + [part[pl.ds((5 + m) * REACH, REACH)] for m in range(3)]
         for r in range(REACH):
-            fields = [part[base + (2 + m) * REACH + r] for m in range(4)]
-            derive(coeffs, at + r, only_real(fields[0]), *fields[1:])
-
-    def mid_emit(row, next_p, next_q):
+            derive(coeffs, at + r, *[m[r] for m in medium])
+    for begin in (0, rows + REACH):
+        depth_rows(lambda b, n: p[pl.ds(b, n)], slope_p, curve_p, begin, REACH, width, matrices)
+        depth_rows(lambda b, n: q[pl.ds(b, n)], slope_q, curve_q, begin, REACH, width, matrices)
+    q1 = mid.at[1]
+    for row in range(rows + 2 * REACH):
+        next_p, next_q = add_border(
+            row,
+            rows,
+            (lambda i: p[i], lambda i: q[i]),
+            (lambda i: slope_p[i], lambda i: slope_q[i]),
+            [coeffs[c, row] for c in range(5)],
+            (ext_base[0, row], ext_base[1, row]),
+        )
+        next_p = next_p + inject[0, row]
+        p1[row, inner, :] = next_p
         mid[0, row] = next_p
         mid[1, row] = next_q
 
@@ -421,26 +477,42 @@
         out[0, row] = next_p
         out[1, row] = next_q
 
-    two_steps(
-        0,
+    second_step(
         rows,
         width,
-        (p, q),
-        (slopes[0], slopes[1], curves[0], curves[1]),
-        lambda row: (prev_ext[0, row], prev_ext[1, row]),
+        p1,
+        q1,
+        (slope_p, slope_q),
+        (curve_p, curve_q),
+        lambda row: (now[0, row], now[1, row]),
         coeffs,
-        inject,
+        inject.at[1],
         matrices,
-        scratch,
-        mid_emit,
         emit,
-        lambda row: (now[0, row], now[1, row]),
-    )
-    slope_out[...] = scratch[0][pl.ds(REACH, rows)]
-
-
-def side_kernel(before, mid, slope_z, now, matrices, flux, slopes, curves, p1):
+    )
+    slope_out[...] = slope_p[own]
+
+
+def side_kernel(
+    before,
+    mid,
+    slope_z,
+    now,
+    coeffs,
+    matrices,
+    flux,
+    base,
+    slopes,
+    p1,
+    p,
+    q,
+    slope_p,
+    slope_q,
+    curve_p,
+    curve_q,
+):
     rows, width = before.shape[1], before.shape[2]
+    own = pl.ds(REACH, rows)
     clear_pads(p1, width)
     p1[:, YPAD : YPAD + width, :] = mid[0]
 
@@ -450,10 +522,28 @@
             flux[a, row] = parts[a]
 
     each_row(rows, width, fluxes)
-    for f in range(2):
-        depth_rows(
-            lambda b, n: now[f, pl.ds(b, n)], slopes.at[f], curves.at[f], 0, rows, width, matrices
-        )
+    clear_pads(p, width)
+    clear_sides(rows, p, q, slope_p, slope_q)
+    p[own, YPAD : YPAD + width, :] = now[0]
+    q[own] = now[1]
+
+    def emit(row, next_p, next_q):
+        base[0, row] = next_p
+        base[1, row] = next_q
+
+    block_step(
+        rows,
+        width,
+        (p, q),
+        (slope_p, slope_q),
+        (curve_p, curve_q),
+        matrices,
+        lambda row: (mid[0, row + REACH], mid[1, row + REACH]),
+        lambda row: [coeffs[c, row + REACH] for c in range(5)],
+        emit,
+    )
+    slopes[0] = slope_p[own]
+    slopes[1] = slope_q[own]
 
 
 def late_kernel(
@@ -462,20 +552,27 @@
     coeffs,
     on_chip,
     off_chip,
+    base,
+    own_slopes,
     inject,
-    slopes,
-    curves,
     matrices,
     out,
     imaged,
     p,
     q,
-    *scratch,
+    slope_p,
+    slope_q,
+    curve_p,
+    curve_q,
+    p1,
+    q1,
 ):
     rows, width = now.shape[1], now.shape[2]
+    inner = slice(YPAD, YPAD + width)
     near, far = side_starts(rows, HALO)
     inside = has_far_side()
     clear_pads(p, width)
+    clear_pads(p1, width)
     place(
         p,
         q,
@@ -486,30 +583,61 @@
         ),
         width,
     )
+    own = pl.ds(HALO, rows)
+    slope_p[own], slope_q[own] = own_slopes[0], own_slopes[1]
+    for begin in (0, rows + HALO):
+        depth_rows(
+            lambda b, n: p[pl.ds(b, n), inner, :], slope_p, curve_p, begin, HALO, width, matrices
+        )
+        depth_rows(lambda b, n: q[pl.ds(b, n)], slope_q, curve_q, begin, HALO, width, matrices)
+
+    def keep(row, next_p, next_q):
+        p1[row, inner, :] = next_p + inject[2, row]
+        q1[row] = next_q
+
+    for begin in (0, rows + REACH):
+        time_step(
+            begin,
+            REACH,
+            width,
+            (p, q),
+            lambda row: (mid[0, row], mid[1, row]),
+            lambda row: [coeffs[c, row] for c in range(5)],
+            (slope_p, slope_q),
+            (curve_p, curve_q),
+            keep,
+        )
+    for row in range(REACH, rows + REACH):
+        result = add_border(
+            row,
+            rows,
+            (lambda i: p[i + REACH, inner, :], lambda i: q[i + REACH]),
+            (lambda i: slope_p[i + REACH], lambda i: slope_q[i + REACH]),
+            [coeffs[c, row] for c in range(5)],
+            (base[0, row - REACH], base[1, row - REACH]),
+        )
+        keep(row, *result)
 
     def emit(row, next_p, next_q):
         out[0, row] = next_p
         out[1, row] = next_q
 
-    two_steps(
-        2,
+    second_step(
         rows,
         width,
-        (p, q),
-        (slopes[0], slopes[1], curves[0], curves[1]),
-        lambda row: (mid[0, row], mid[1, row]),
+        p1,
+        q1,
+        (slope_p, slope_q),
+        (curve_p, curve_q),
+        lambda row: (now[0, row], now[1, row]),
         coeffs,
-        inject,
+        inject.at[3],
         matrices,
-        scratch,
-        lambda row, next_p, next_q: None,
         emit,
-        lambda row: (now[0, row], now[1, row]),
-    )
-    slope_z, p1 = scratch[0], scratch[4]
+    )
 
     def fluxes(row):
-        field, parts = flux_row(row, width, p1, slope_z[row + REACH], now[0, row])
+        field, parts = flux_row(row, width, p1, slope_p[row + REACH], now[0, row])
         for a, value in enumerate((field, *parts)):
             imaged[a, row] = value
 
@@ -614,66 +742,69 @@
             ),
         )(*ins)
 
-    step_scratch = [
-        pltpu.VMEM((wide,) + plane, f32),
-        pltpu.VMEM((wide,) + plane, f32),
-        pltpu.VMEM((wide,) + plane, f32),
-        pltpu.VMEM((wide,) + plane, f32),
-        pltpu.VMEM((ext,) + padded, f32),
-        pltpu.VMEM((ext,) + plane, f32),
-    ]
-    wave_scratch = [pltpu.VMEM((wide,) + padded, f32), pltpu.VMEM((wide,) + plane, f32)]
+    def room(count, lines=plane):
+        return pltpu.VMEM((count,) + lines, f32)
+
     medium = (speed_term, thomsen_epsilon, thomsen_delta, tilt_angle)
     matrices = jnp.asarray(depth_matrices(depth))
-
-    packed = planes(2 * HALO + 6 * REACH)
     snaps, parts = source_store.shape[:2]
     by_owner = source_store.reshape(snaps, parts, count, rows, depth)
-    far_pack, near_pack, sorted_source = call(
+    sorted_shape = (count, snaps, parts, rows, depth)
+    packed = planes(8 * REACH)
+    far_pack, near_pack, sorted_source, own_coeffs, base, slopes = call(
         pack_kernel,
         (
             packed,
             packed,
-            jax.ShapeDtypeStruct((count, snaps, parts, rows, depth), source_store.dtype),
+            jax.ShapeDtypeStruct(sorted_shape, source_store.dtype),
+            planes(5, rows),
+            planes(2, rows),
+            planes(2, rows),
         ),
         [
             pltpu.with_memory_space_constraint(x, pltpu.HBM)
-            for x in (wave_now, wave_prev, *medium, by_owner)
+            for x in (wave_now, wave_prev, *medium, by_owner, matrices)
         ],
-        [in_hbm] * 7,
+        [in_hbm] * 8,
         [
-            pltpu.VMEM((count, snaps, parts, rows, depth), source_store.dtype),
-            pltpu.SemaphoreType.DMA((17 + snaps * parts,)),
+            pltpu.VMEM(sorted_shape, source_store.dtype),
+            room(ext, padded),
+            room(ext),
+            pltpu.VMEM((2, rows) + plane, f32),
+            pltpu.VMEM((4, rows) + plane, f32),
+            *[room(ext)] * 4,
+            pltpu.VMEM(matrices.shape, matrices.dtype),
+            pltpu.SemaphoreType.DMA((21 + snaps * parts,)),
         ],
-        120,
+        16 * wide,
         200,
-        (vmem, vmem, in_hbm),
+        (vmem, vmem, in_hbm, vmem, vmem, vmem),
     )
     off_chip = lax.ppermute(far_pack, both_axes, off_chip_pairs)
     on_chip = lax.ppermute(near_pack, "gx", on_chip_pairs)
     arrived = lax.all_to_all(sorted_source, "gx", split_axis=0, concat_axis=0, tiled=True)
-    own_coeffs, inject, slopes, curves, offsets = call(
+    inject, offsets = call(
         prep_kernel,
-        (
-            planes(5, rows),
-            planes(STEPS, ext),
-            planes(2, rows),
-            planes(2, rows),
-            jax.ShapeDtypeStruct((16, depth), f32),
-        ),
-        (wave_now, *medium, receiver_row, receiver_column, receiver_traces, angle_table, matrices),
-        [vmem] * 8 + [smem, vmem],
+        (planes(STEPS, ext), jax.ShapeDtypeStruct((16, depth), f32)),
+        (receiver_row, receiver_column, receiver_traces, angle_table),
+        [vmem] * 3 + [smem],
         [],
-        20 * wide,
+        8 * wide,
         60 * rows,
     )
     now, mid, coeffs, slope_z = call(
         early_kernel,
         (planes(2, rows), planes(2, ext), planes(5, ext), planes(rows)),
-        (wave_now, wave_prev, on_chip, off_chip, own_coeffs, inject, slopes, curves, matrices),
-        [vmem] * 9,
-        wave_scratch + [pltpu.VMEM((2, ext) + plane, f32)] + step_scratch,
-        30 * wide,
+        (wave_now, on_chip, off_chip, own_coeffs, base, slopes, inject, matrices),
+        [vmem] * 8,
+        [
+            room(ext),
+            room(ext),
+            pltpu.VMEM((2, ext) + plane, f32),
+            *[room(ext)] * 4,
+            room(ext, padded),
+        ],
+        26 * wide,
         400 * rows,
     )
 
@@ -684,22 +815,22 @@
 
     off_chip = lax.ppermute(side(odd == 1), both_axes, off_chip_pairs)
     on_chip = lax.ppermute(side(odd == 0), "gx", on_chip_pairs)
-    flux, slopes, curves = call(
+    flux, base, slopes = call(
         side_kernel,
         (planes(3, rows), planes(2, rows), planes(2, rows)),
-        (wave_now, mid, slope_z, now, matrices),
-        [vmem] * 5,
-        [pltpu.VMEM((ext,) + padded, f32)],
-        12 * wide,
+        (wave_now, mid, slope_z, now, coeffs, matrices),
+        [vmem] * 6,
+        [room(ext, padded), room(ext, padded), *[room(ext)] * 5],
+        18 * wide,
         60 * rows,
     )
     final, imaged = call(
         late_kernel,
         (planes(2, rows), planes(4, rows)),
-        (now, mid, coeffs, on_chip, off_chip, inject, slopes, curves, matrices),
+        (now, mid, coeffs, on_chip, off_chip, base, slopes, inject, matrices),
         [vmem] * 9,
-        wave_scratch + step_scratch,
-        30 * wide,
+        [room(wide, padded), *[room(wide)] * 5, room(ext, padded), room(ext)],
+        28 * wide,
         400 * rows,
     )
     return call(

time: 31 us -> 29.5 us (0.952)
  the two profiles are of different devices: /device:TPU:21 before, /device:TPU:17 now
where the time goes in v7:
time: 29.5 us; the launch traced here: 29.3 us
  waiting for transfers between devices  12.6 us (43%)
  starting transfers between devices  9.57 us (32%)
  Pallas kernels  6.35 us (22%)
  between operations  0.74 us (3%)
    ppermute x1, waiting for transfers between devices, local(): off_chip = lax.ppermute(far_pack, both_axes, off_chip_pairs)  8.44 us
    all_to_all x1, starting transfers between devices, local(): lax.all_to_all(sorted_source, 'gx', split_axis=0, concat_axis=0, tiled=True)  6.58 us
    pallas_call x6, Pallas kernels, call(): pl.pallas_call(kernel, out_shape=outs, in_specs=in_specs, out_specs=out_s...  6.35 us
    ppermute x1, waiting for transfers between devices, local(): off_chip = lax.ppermute(side(odd == 1), both_axes, off_chip_pairs)  4.1 us
    ppermute x1, starting transfers between devices, local(): off_chip = lax.ppermute(far_pack, both_axes, off_chip_pairs)  1.18 us
    ppermute x1, starting transfers between devices, local(): off_chip = lax.ppermute(side(odd == 1), both_axes, off_chip_pairs)  0.91 us
  transfers between devices with their start and end apart: 5, of which 2 were waited for; matrix products, arithmetic and copies ran while one was open for 0% of the time, Pallas kernels for 10%

profile of v7, /device:TPU:17, one launch (start us, length us, event | category | flops | bytes accessed | tf_op | source)
XLA Modules:
  0.0 29.3 jit_solution(12707888151372248268)
XLA Ops:
  0.6 2.2 %shard_map.131 = (f32[32,16,128]{2,1,0:T(8,128)S(1)}, f32[32,16,128]{2,1,0:T(8,128)S(1)}, bf16[16,2,4,8,128]{4,3,2,1,0:T(8,128)(2,1)}, f32[5,8,16,128]{3,2,1,0:T...) custom-call(f32[2,8,16,128]{3,2,1,0:T(8,128)} %before.1, f32[2,8,16,128]{3,2,1,0:T(8,128)} %prev.1, ...), custom_call_target="tpu_custom_call" | custom-call | flops 409600 | bytes 102400 | tf_op jit(solution)/shard_map/pallas_call | solution.py:731
  2.8 0.0 copy-start
  2.8 0.0 copy-start.1
  2.8 6.6 %all-to-all-start = ((bf16[16,2,4,8,128]{4,3,2,1,0:T(8,128)(2,1)}), bf16[16,2,4,8,128]{4,3,2,1,0:T(8,128)(2,1)S(1)}, u32[]{:S(2)}, u32[]{:S(2)}) async-start(bf16[16,2,4,8,128]{4,3,2,1,0:T(8,128)(2,1)} %get-tuple-element.19), calls=%async_computation | async-start | bytes 524288 | tf_op jit(solution)/shard_map/all_to_all | solution.py:785
  9.4 0.0 copy-start.2
  9.4 0.0 copy-start.3
  9.4 0.0 copy-start.4
  9.4 0.0 copy-start.5
  9.5 0.5 %collective-permute-start = (f32[32,16,128]{2,1,0:T(8,128)S(1)}, f32[32,16,128]{2,1,0:T(8,128)S(1)}, u32[]{:S(2)}, u32[]{:S(2)}) collective-permute-start(f32[32,16,128]{2,1,0:T(8,128)S(1)} %get-tuple-element.20), channel_id=1, source_target_pairs={{0,1},{1,0},{2,3},{3,2},{4,5},{5,4},{6,7},{7,6},{8,9},{9,8},{10,11... | collective-permute-start | bytes 786440 | tf_op jit(solution)/shard_map/ppermute | solution.py:784
  9.9 1.2 %collective-permute-start.1 = (f32[32,16,128]{2,1,0:T(8,128)S(1)}, f32[32,16,128]{2,1,0:T(8,128)S(1)}, u32[]{:S(2)}, u32[]{:S(2)}) collective-permute-start(f32[32,16,128]{2,1,0:T(8,128)S(1)} %get-tuple-element.21), channel_id=1, source_target_pairs={{1,2},{2,1},{3,4},{4,3},{5,6},{6,5},{7,8},{8,7},{9,10},{10,9},{11,... | collective-permute-start | bytes 786440 | tf_op jit(solution)/shard_map/ppermute | solution.py:783
  11.1 0.0 copy-done.2
  11.1 0.0 copy-done.3
  11.1 0.0 copy-done.4
  11.1 0.0 copy-done.5
  11.1 0.9 %shard_map.132 = (f32[4,16,16,128]{3,2,1,0:T(8,128)S(1)}, f32[16,128]{1,0:T(8,128)S(1)}) custom-call(s32[128]{0:T(128)S(1)} %copy-done.3, s32[128]{0:T(128)S(1)} %copy-done.4, f32[4,128]{1,0:T(4,128)S(1)} %copy-done.2, s32[32]{0:T(128)S(1)} %copy-done.5), custom_call_target="tpu_custom_call" | custom-call | flops 983040 | bytes 245760 | tf_op jit(solution)/shard_map/pallas_call | solution.py:731
  12.0 0.0 collective-permute-done.on_chip
  12.0 8.4 %collective-permute-done.1.off_chip = f32[32,16,128]{2,1,0:T(8,128)S(1)} collective-permute-done((f32[32,16,128]{2,1,0:T(8,128)S(1)}, f32[32,16,128]{2,1,0:T(8,128)S(1)}, u32[]{:S(2)}, u32[]{:S(2)}) %collective-permute-start.1) | collective-permute-done | bytes 262176 | tf_op jit(solution)/shard_map/ppermute | solution.py:783
  20.5 0.0 copy-done
  20.5 0.0 copy-done.1
  20.5 0.9 %shard_map.133 = (f32[2,8,16,128]{3,2,1,0:T(8,128)S(1)}, f32[2,16,16,128]{3,2,1,0:T(8,128)S(1)}, f32[5,16,16,128]{3,2,1,0:T(8,128)S(1)}, f32[8,16,128]{2,1,0:T(8,128)S(1)}) custom-call(f32[2,8,16,128]{3,2,1,0:T(8,128)S(1)} %copy-done.1, f32[32,16,128]{2,1,0:T(8,128)S(1)} %collective-permute-done.on_chip, f32[32,16,128]{2,1,0:T(8,128)S(1)} %collective-permute-done.1.off_chip, ...), custom_call_target="tpu_custom_call" | custom-call | flops 6553600 | bytes 1638400 | tf_op jit(solution)/shard_map/pallas_call | solution.py:731
  21.4 0.9 %collective-permute-start.3 = (f32[2,8,16,128]{3,2,1,0:T(8,128)S(1)}, f32[2,8,16,128]{3,2,1,0:T(8,128)S(1)}, u32[]{:S(2)}, u32[]{:S(2)}) collective-permute-start(f32[2,8,16,128]{3,2,1,0:T(8,128)S(1)} %get-tuple-element.28.now), channel_id=1, source_target_pairs={{1,2},{2,1},{3,4},{4,3},{5,6},{6,5},{7,8},{8,7},{9,10},{10,9},{11,... | collective-permute-start | bytes 393224 | tf_op jit(solution)/shard_map/ppermute | solution.py:816
  22.3 0.4 %collective-permute-start.2 = (f32[2,8,16,128]{3,2,1,0:T(8,128)S(1)}, f32[2,8,16,128]{3,2,1,0:T(8,128)S(1)}, u32[]{:S(2)}, u32[]{:S(2)}) collective-permute-start(f32[2,8,16,128]{3,2,1,0:T(8,128)S(1)} %get-tuple-element.28.now), channel_id=1, source_target_pairs={{0,1},{1,0},{2,3},{3,2},{4,5},{5,4},{6,7},{7,6},{8,9},{9,8},{10,11... | collective-permute-start | bytes 393224 | tf_op jit(solution)/shard_map/ppermute | solution.py:817
  22.7 0.4 %shard_map.134 = (f32[3,8,16,128]{3,2,1,0:T(8,128)S(1)}, f32[2,8,16,128]{3,2,1,0:T(8,128)S(1)}, f32[2,8,16,128]{3,2,1,0:T(8,128)S(1)}) custom-call(f32[2,8,16,128]{3,2,1,0:T(8,128)S(1)} %copy-done.1, f32[2,16,16,128]{3,2,1,0:T(8,128)S(1)} %get-tuple-element.26.mid, f32[8,16,128]{2,1,0:T(8,128)S(1)} %get-tuple-element.27.slope_z, ...), custom_call_target="tpu_custom_call" | custom-call | flops 983040 | bytes 245760 | tf_op jit(solution)/shard_map/pallas_call | solution.py:731
  23.1 4.1 %collective-permute-done.3.off_chip = f32[2,8,16,128]{3,2,1,0:T(8,128)S(1)} collective-permute-done((f32[2,8,16,128]{3,2,1,0:T(8,128)S(1)}, f32[2,8,16,128]{3,2,1,0:T(8,128)S(1)}, u32[]{:S(2)}, u32[]{:S(2)}) %collective-permute-start.3) | collective-permute-done | bytes 131104 | tf_op jit(solution)/shard_map/ppermute | solution.py:816
  27.2 0.0 collective-permute-done.2.on_chip
  27.2 0.9 %shard_map.135 = (f32[2,8,16,128]{3,2,1,0:T(8,128)S(1)}, f32[4,8,16,128]{3,2,1,0:T(8,128)S(1)}) custom-call(f32[2,8,16,128]{3,2,1,0:T(8,128)S(1)} %get-tuple-element.28.now, f32[2,16,16,128]{3,2,1,0:T(8,128)S(1)} %get-tuple-element.26.mid, f32[5,16,16,128]{3,2,1,0:T(8,128)S(1)} %get-tuple-element.29.coeffs, ...), custom_call_target="tpu_custom_call" | custom-call | flops 6553600 | bytes 1638400 | tf_op jit(solution)/shard_map/pallas_call | solution.py:731
  28.1 0.0 all-to-all-done.arrived
  28.1 1.1 %shard_map.136 = (bf16[8,8,16,128]{3,2,1,0:T(8,128)(2,1)}, f32[2,8,16,128]{3,2,1,0:T(8,128)}) custom-call(bf16[16,2,4,8,128]{4,3,2,1,0:T(8,128)(2,1)S(1)} %all-to-all-done.arrived, f32[2,16,16,128]{3,2,1,0:T(8,128)S(1)} %get-tuple-element.26.mid, f32[3,8,16,128]{3,2,1,0:T(8,128)S(1)} %get-tuple-element.30.flux, ...), custom_call_target="tpu_custom_call" | custom-call | flops 983040 | bytes 245760 | tf_op jit(solution)/shard_map/pallas_call | solution.py:731
Async XLA Ops:
  2.8 17.7 %copy-start = (bf16[3,128,256]{2,1,0:T(8,128)(2,1)S(1)}, bf16[3,128,256]{2,1,0:T(8,128)(2,1)}, u32[]{:S(2)}) copy-start(bf16[3,128,256]{2,1,0:T(8,128)(2,1)} %constant.2.clone.matrices) | copy-start | bytes 589828
  2.8 17.7 %copy-start.1 = (f32[2,8,16,128]{3,2,1,0:T(8,128)S(1)}, f32[2,8,16,128]{3,2,1,0:T(8,128)}, u32[]{:S(2)}) copy-start(f32[2,8,16,128]{3,2,1,0:T(8,128)} %before.1) | copy-start | bytes 393220
  2.8 25.3 %all-to-all-start = ((bf16[16,2,4,8,128]{4,3,2,1,0:T(8,128)(2,1)}), bf16[16,2,4,8,128]{4,3,2,1,0:T(8,128)(2,1)S(1)}, u32[]{:S(2)}, u32[]{:S(2)}) async-start(bf16[16,2,4,8,128]{4,3,2,1,0:T(8,128)(2,1)} %get-tuple-element.19), calls=%async_computation | async-start | bytes 524288 | tf_op jit(solution)/shard_map/all_to_all | solution.py:785
  9.4 1.7 %copy-start.2 = (f32[4,128]{1,0:T(4,128)S(1)}, f32[4,128]{1,0:T(4,128)}, u32[]{:S(2)}) copy-start(f32[4,128]{1,0:T(4,128)} %traces.1) | copy-start | bytes 6148
  9.4 1.7 %copy-start.3 = (s32[128]{0:T(128)S(1)}, s32[128]{0:T(128)}, u32[]{:S(2)}) copy-start(s32[128]{0:T(128)} %receiver_row.1) | copy-start | bytes 1540
  9.4 1.7 %copy-start.4 = (s32[128]{0:T(128)S(1)}, s32[128]{0:T(128)}, u32[]{:S(2)}) copy-start(s32[128]{0:T(128)} %receiver_column.1) | copy-start | bytes 1540
  9.4 1.7 %copy-start.5 = (s32[32]{0:T(128)S(1)}, s32[32]{0:T(128)}, u32[]{:S(2)}) copy-start(s32[32]{0:T(128)} %table.1) | copy-start | bytes 388
  9.5 2.6 %collective-permute-start = (f32[32,16,128]{2,1,0:T(8,128)S(1)}, f32[32,16,128]{2,1,0:T(8,128)S(1)}, u32[]{:S(2)}, u32[]{:S(2)}) collective-permute-start(f32[32,16,128]{2,1,0:T(8,128)S(1)} %get-tuple-element.20), channel_id=1, source_target_pairs={{0,1},{1,0},{2,3},{3,2},{4,5},{5,4},{6,7},{7,6},{8,9},{9,8},{10,11... | collective-permute-start | bytes 786440 | tf_op jit(solution)/shard_map/ppermute | solution.py:784
  9.9 10.6 %collective-permute-start.1 = (f32[32,16,128]{2,1,0:T(8,128)S(1)}, f32[32,16,128]{2,1,0:T(8,128)S(1)}, u32[]{:S(2)}, u32[]{:S(2)}) collective-permute-start(f32[32,16,128]{2,1,0:T(8,128)S(1)} %get-tuple-element.21), channel_id=1, source_target_pairs={{1,2},{2,1},{3,4},{4,3},{5,6},{6,5},{7,8},{8,7},{9,10},{10,9},{11,... | collective-permute-start | bytes 786440 | tf_op jit(solution)/shard_map/ppermute | solution.py:783
  21.4 5.9 %collective-permute-start.3 = (f32[2,8,16,128]{3,2,1,0:T(8,128)S(1)}, f32[2,8,16,128]{3,2,1,0:T(8,128)S(1)}, u32[]{:S(2)}, u32[]{:S(2)}) collective-permute-start(f32[2,8,16,128]{3,2,1,0:T(8,128)S(1)} %get-tuple-element.28.now), channel_id=1, source_target_pairs={{1,2},{2,1},{3,4},{4,3},{5,6},{6,5},{7,8},{8,7},{9,10},{10,9},{11,... | collective-permute-start | bytes 393224 | tf_op jit(solution)/shard_map/ppermute | solution.py:816
  22.3 5.0 %collective-permute-start.2 = (f32[2,8,16,128]{3,2,1,0:T(8,128)S(1)}, f32[2,8,16,128]{3,2,1,0:T(8,128)S(1)}, u32[]{:S(2)}, u32[]{:S(2)}) collective-permute-start(f32[2,8,16,128]{3,2,1,0:T(8,128)S(1)} %get-tuple-element.28.now), channel_id=1, source_target_pairs={{0,1},{1,0},{2,3},{3,2},{4,5},{5,4},{6,7},{7,6},{8,9},{9,8},{10,11... | collective-permute-start | bytes 393224 | tf_op jit(solution)/shard_map/ppermute | solution.py:817

commit v8 on v7

--- a/solution.py
+++ b/solution.py
@@ -1,3 +1,5 @@
+import math
+
 import jax
 import jax.numpy as jnp
 import numpy as np
@@ -17,6 +19,11 @@
 
 SECOND = (-205.0 / 72.0, 8.0 / 5.0, -1.0 / 5.0, 8.0 / 315.0, -1.0 / 560.0)
 FIRST = (4.0 / 5.0, -1.0 / 5.0, 4.0 / 105.0, -1.0 / 280.0)
+
+
+def exchange_order(count):
+    step = next(n for n in (5, 7, 3, 1) if math.gcd(n, count) == 1)
+    return [(count // 2 - 1 + step * j) % count for j in range(count)]
 
 
 def each_row(count, width, body):
@@ -55,18 +62,23 @@
     return total
 
 
-def depth_matrices(depth):
-    eye = [np.eye(depth, k=k, dtype=np.float64) for k in range(-4, 5)]
-    slope = sum(np.float32(FIRST[k - 1]) * (eye[4 - k] - eye[4 + k]) for k in range(1, 5))
-    curve = np.float32(SECOND[0]) * eye[4] + sum(
-        np.float32(SECOND[k]) * (eye[4 - k] + eye[4 + k]) for k in range(1, 5)
-    )
-    rest = np.concatenate([slope, curve], axis=1).astype(np.float32)
-    parts = []
-    for _ in range(3):
-        parts.append(rest.astype(jnp.bfloat16))
-        rest = rest - parts[-1].astype(np.float32)
-    return np.stack(parts)
+def build_matrices(out):
+    depth = out.shape[1]
+    slope = {k: -FIRST[k - 1] for k in range(1, 5)}
+    slope = {d: c for k, v in slope.items() for d, c in ((-k, v), (k, -v))}
+    curve = {d: SECOND[abs(d)] for d in range(-4, 5)}
+    line = lax.broadcasted_iota(jnp.int32, (depth, depth), 0)
+    apart = line - lax.broadcasted_iota(jnp.int32, (depth, depth), 1)
+    hits = {d: apart == d for d in range(-4, 5)}
+    for side, coefficients in enumerate((slope, curve)):
+        rest = {d: np.float32(c) for d, c in coefficients.items()}
+        for part in range(3):
+            rounded = {d: c.astype(jnp.bfloat16).astype(np.float32) for d, c in rest.items()}
+            rest = {d: c - rounded[d] for d, c in rest.items()}
+            values = jnp.zeros((depth, depth), jnp.float32)
+            for d, c in rounded.items():
+                values = jnp.where(hits[d], float(c), values)
+            out[part, :, side * depth : (side + 1) * depth] = values.astype(jnp.bfloat16)
 
 
 def depth_diffs(field, matrices):
@@ -251,13 +263,10 @@
 
 
 def place(dst_p, dst_q, centre, sides, width):
-    rows = centre.shape[1]
     inner = pl.ds(YPAD, width)
-    dst_p[pl.ds(HALO, rows), inner, :] = centre[0]
-    dst_q[pl.ds(HALO, rows)] = centre[1]
-    for at, read in sides:
-        dst_p[pl.ds(at, HALO), inner, :] = read(0, HALO)
-        dst_q[pl.ds(at, HALO)] = read(HALO, HALO)
+    for at, count, read in ((HALO, centre.shape[1], lambda f: centre[f]), *sides):
+        dst_p[pl.ds(at, count), inner, :] = read(0)
+        dst_q[pl.ds(at, count)] = read(1)
 
 
 def side_starts(rows, reach):
@@ -304,13 +313,21 @@
     delta,
     tilt,
     source,
-    matrices,
+    receiver_row,
+    receiver_column,
+    traces,
+    table,
     far,
     near,
     sorted_source,
     coeffs,
     base,
     slopes,
+    weights,
+    row_out,
+    column_out,
+    traces_out,
+    table_out,
     staged,
     p,
     q,
@@ -320,43 +337,38 @@
     slope_q,
     curve_p,
     curve_q,
-    weights,
     sems,
 ):
     rows, width = now.shape[1], now.shape[2]
     odd = lax.rem(lax.axis_index("gx"), 2)
-    ends = ((far, odd), (near, 1 - odd))
-    copies = []
+    started = []
+
+    def copy(src, dst):
+        started.append(pltpu.make_async_copy(src, dst, sems.at[len(started)]))
+        started[-1].start()
+        return started[-1]
+
+    arriving = []
+    for place, owner in enumerate(exchange_order(source.shape[2])):
+        arriving.append(copy(source.at[:, :, owner], staged.at[place]))
     clear_pads(p, width)
     clear_sides(rows, p, q, slope_p, slope_q)
-
-    def copy(src, dst):
-        copies.append(pltpu.make_async_copy(src, dst, sems.at[len(copies)]))
-        copies[-1].start()
-        return copies[-1]
-
     own = pl.ds(REACH, rows)
-    local = [copy(matrices, weights)]
+    inner = slice(YPAD, YPAD + width)
+    local = [copy(field, medium.at[m]) for m, field in enumerate((speed, epsilon, delta, tilt))]
     local.append(copy(now.at[0], p.at[own, pl.ds(YPAD, width)]))
     local.append(copy(now.at[1], q.at[own]))
-    fields = (speed, epsilon, delta, tilt)
-    for m, field in enumerate(fields):
-        local.append(copy(field, medium.at[m]))
     local.append(copy(prev, before))
-    arriving = []
-    for n in range(source.shape[0]):
-        for c in range(source.shape[1]):
-            arriving.append(copy(source.at[n, c], staged.at[:, n, c]))
-    edges = []
-    for out, tail in ends:
-        edge = pl.ds(tail * (rows - REACH), REACH)
-        for f in range(2):
-            edges.append(copy(now.at[f, edge], out.at[pl.ds(f * REACH, REACH)]))
-        for m, field in enumerate(fields):
-            edges.append(copy(field.at[edge], out.at[pl.ds((4 + m) * REACH, REACH)]))
-    for one in local + arriving:
+    local.append(copy(receiver_row, row_out))
+    local.append(copy(receiver_column, column_out))
+    local.append(copy(traces, traces_out))
+    local.append(copy(table, table_out))
+    build_matrices(weights)
+    for one in arriving:
         one.wait()
     leaving = copy(staged, sorted_source)
+    for one in local:
+        one.wait()
     each_row(rows, width, lambda r: derive(coeffs, r, *[medium[m, r] for m in range(4)]))
 
     def emit(row, next_p, next_q):
@@ -376,37 +388,59 @@
     )
     slopes[0] = slope_p[own]
     slopes[1] = slope_q[own]
-    for out, tail in ends:
-        for f in range(2):
-            out[pl.ds((2 + f) * REACH, REACH)] = base[f, pl.ds(tail * (rows - REACH), REACH)]
-    for one in edges:
-        one.wait()
+    for out, tail in ((far, odd), (near, 1 - odd)):
+        first_row = tail * (rows - REACH)
+        edge = pl.ds(first_row, REACH)
+        edge_fields = [
+            p[pl.ds(REACH + first_row, REACH), inner, :],
+            q[pl.ds(REACH + first_row, REACH)],
+            base[0, edge],
+            base[1, edge],
+            *[medium[m, edge] for m in range(4)],
+        ]
+        for index, value in enumerate(edge_fields):
+            out[pl.ds(index * REACH, REACH)] = value
     leaving.wait()
 
 
 def prep_kernel(receiver_row, receiver_column, traces, table, inject, offsets):
     _, ext, width, depth = inject.shape
     flat = receivers(receiver_row, receiver_column, ext - 2 * REACH, width)
-
-    def samples(row):
-        cell = lax.broadcasted_iota(jnp.int32, (width, flat.shape[1]), 0) + row * width
-        lane = lax.broadcasted_iota(jnp.int32, (width, depth), 1)
-        hit = cell == flat
+    count = flat.shape[1]
+    at_depth = lax.broadcasted_iota(jnp.int32, (depth, count), 0) == REC_DEPTH
+    parts = []
+    rest = traces[...]
+    for _ in range(3):
+        parts.append(rest.astype(jnp.bfloat16).astype(jnp.float32))
+        rest = rest - parts[-1]
+    samples = [
+        jnp.concatenate(
+            [jnp.where(at_depth, part[t : t + 1, :], 0.0) for t in range(STEPS)], axis=0
+        ).astype(jnp.bfloat16)
+        for part in reversed(parts)
+    ]
+
+    def chunk(start, size):
+        lines = size * width
+        cell = lax.broadcasted_iota(jnp.int32, (lines, count), 0) + start * width
+        hit = jnp.where(cell == flat, 1.0, 0.0).astype(jnp.bfloat16)
+        total = None
+        for sample in samples:
+            term = lax.dot_general(
+                hit, sample, (((1,), (1,)), ((), ())), preferred_element_type=jnp.float32
+            )
+            total = term if total is None else total + term
         for t in range(STEPS):
-            column = jnp.sum(jnp.where(hit, traces[t : t + 1, :], 0.0), axis=1, keepdims=True)
-            inject[t, row] = jnp.where(lane == REC_DEPTH, column, 0.0)
-
-    each_row(ext, width, samples)
+            part = total[:, t * depth : (t + 1) * depth]
+            inject[t, pl.ds(start, size)] = part.reshape(size, width, depth)
+
+    each_chunk(ext, width, chunk)
     fine = table.shape[0]
-    starts = [jnp.int32(0)] * NBIN
-    for f in range(fine):
-        named = table[f]
-        for b in range(1, NBIN):
-            starts[b] = starts[b] + (named < b).astype(jnp.int32)
-    values = [s.astype(jnp.float32) - 1.0 for s in starts]
-    values.append(jnp.float32(0.5 * (fine - 1)))
-    for b, value in enumerate(values):
-        offsets[b : b + 1, :] = jnp.full((1, depth), value, jnp.float32)
+    names = table[...].reshape(1, fine)
+    for b in range(NBIN):
+        begin = jnp.sum((names < b).astype(jnp.float32), axis=1, keepdims=True) - 1.0
+        offsets[b : b + 1, :] = jnp.broadcast_to(begin, (1, depth))
+    offsets[NBIN : NBIN + 1, :] = jnp.full((1, depth), 0.5 * (fine - 1), jnp.float32)
 
 
 def early_kernel(
@@ -419,6 +453,8 @@
     inject,
     matrices,
     out,
+    far_near,
+    far_outer,
     mid,
     coeffs,
     slope_out,
@@ -491,6 +527,11 @@
         emit,
     )
     slope_out[...] = slope_p[own]
+    tail = lax.rem(lax.axis_index("gx"), 2)
+    for f in range(2):
+        far_near[f] = out[f, pl.ds(tail * (rows - REACH), REACH)]
+        outer = out[f, pl.ds(REACH + tail * (rows - HALO - REACH), REACH)]
+        far_outer[f] = outer.astype(far_outer.dtype)
 
 
 def side_kernel(
@@ -551,7 +592,8 @@
     mid,
     coeffs,
     on_chip,
-    off_chip,
+    off_near,
+    off_outer,
     base,
     own_slopes,
     inject,
@@ -571,15 +613,21 @@
     inner = slice(YPAD, YPAD + width)
     near, far = side_starts(rows, HALO)
     inside = has_far_side()
+    odd = lax.rem(lax.axis_index("gx"), 2)
     clear_pads(p, width)
     clear_pads(p1, width)
+
+    def far_rows(part, f):
+        return jnp.where(inside, part[f].astype(jnp.float32), 0.0)
+
     place(
         p,
         q,
         now,
         (
-            (near, lambda a, n: on_chip[a // HALO]),
-            (far, lambda a, n: jnp.where(inside, off_chip[a // HALO], 0.0)),
+            (near, HALO, lambda f: on_chip[f]),
+            (far + (1 - odd) * REACH, REACH, lambda f: far_rows(off_near, f)),
+            (far + odd * REACH, REACH, lambda f: far_rows(off_outer, f)),
         ),
         width,
     )
@@ -647,12 +695,14 @@
 def image_kernel(
     arrived, mid, flux, imaged, offsets, wave, images, wave_out, block, lines, sems
 ):
-    rows, width, _ = flux.shape[1:]
+    rows, width, depth = flux.shape[1:]
     whole = pltpu.make_async_copy(wave, wave_out, sems.at[0])
     whole.start()
-    lines[...] = arrived[...].astype(jnp.float32).reshape(lines.shape)
     parts = arrived.shape[2]
     stride = lines.shape[0] // width
+    for place, column in enumerate(exchange_order(width)):
+        block_lines = arrived[place].astype(jnp.float32).reshape(stride, depth)
+        lines[column * stride : (column + 1) * stride, :] = block_lines
 
     def source(n, row):
         begin = n * parts * rows + row
@@ -717,7 +767,6 @@
     f32 = jnp.float32
     ext, wide = rows + 2 * REACH, rows + 2 * HALO
     vmem = pl.BlockSpec(memory_space=pltpu.VMEM)
-    smem = pl.BlockSpec(memory_space=pltpu.SMEM)
     in_hbm = pl.BlockSpec(memory_space=pltpu.HBM)
     plane = (width, depth)
     padded = (width + 2 * YPAD, depth)
@@ -746,12 +795,13 @@
         return pltpu.VMEM((count,) + lines, f32)
 
     medium = (speed_term, thomsen_epsilon, thomsen_delta, tilt_angle)
-    matrices = jnp.asarray(depth_matrices(depth))
+    matrices = jax.ShapeDtypeStruct((3, depth, 2 * depth), jnp.bfloat16)
     snaps, parts = source_store.shape[:2]
     by_owner = source_store.reshape(snaps, parts, count, rows, depth)
     sorted_shape = (count, snaps, parts, rows, depth)
     packed = planes(8 * REACH)
-    far_pack, near_pack, sorted_source, own_coeffs, base, slopes = call(
+    tables = (receiver_row, receiver_column, receiver_traces, angle_table)
+    far_pack, near_pack, sorted_source, own_coeffs, base, slopes, matrices, *small = call(
         pack_kernel,
         (
             packed,
@@ -760,12 +810,14 @@
             planes(5, rows),
             planes(2, rows),
             planes(2, rows),
+            matrices,
+            *[jax.ShapeDtypeStruct(x.shape, x.dtype) for x in tables],
         ),
         [
             pltpu.with_memory_space_constraint(x, pltpu.HBM)
-            for x in (wave_now, wave_prev, *medium, by_owner, matrices)
+            for x in (wave_now, wave_prev, *medium, by_owner, *tables)
         ],
-        [in_hbm] * 8,
+        [in_hbm] * 11,
         [
             pltpu.VMEM(sorted_shape, source_store.dtype),
             room(ext, padded),
@@ -773,28 +825,41 @@
             pltpu.VMEM((2, rows) + plane, f32),
             pltpu.VMEM((4, rows) + plane, f32),
             *[room(ext)] * 4,
-            pltpu.VMEM(matrices.shape, matrices.dtype),
-            pltpu.SemaphoreType.DMA((21 + snaps * parts,)),
+            pltpu.SemaphoreType.DMA((12 + count,)),
         ],
         16 * wide,
         200,
-        (vmem, vmem, in_hbm, vmem, vmem, vmem),
+        (vmem, vmem, in_hbm, *[vmem] * 8),
     )
     off_chip = lax.ppermute(far_pack, both_axes, off_chip_pairs)
     on_chip = lax.ppermute(near_pack, "gx", on_chip_pairs)
-    arrived = lax.all_to_all(sorted_source, "gx", split_axis=0, concat_axis=0, tiled=True)
+    arrived = lax.all_to_all(
+        sorted_source,
+        "gx",
+        split_axis=0,
+        concat_axis=0,
+        tiled=True,
+        axis_index_groups=[exchange_order(count)],
+    )
     inject, offsets = call(
         prep_kernel,
         (planes(STEPS, ext), jax.ShapeDtypeStruct((16, depth), f32)),
-        (receiver_row, receiver_column, receiver_traces, angle_table),
-        [vmem] * 3 + [smem],
+        small,
+        [vmem] * 4,
         [],
         8 * wide,
         60 * rows,
     )
-    now, mid, coeffs, slope_z = call(
+    now, far_near, far_outer, mid, coeffs, slope_z = call(
         early_kernel,
-        (planes(2, rows), planes(2, ext), planes(5, ext), planes(rows)),
+        (
+            planes(2, rows),
+            planes(2, REACH),
+            jax.ShapeDtypeStruct((2, REACH) + plane, jnp.bfloat16),
+            planes(2, ext),
+            planes(5, ext),
+            planes(rows),
+        ),
         (wave_now, on_chip, off_chip, own_coeffs, base, slopes, inject, matrices),
         [vmem] * 8,
         [
@@ -813,7 +878,8 @@
             return now
         return lax.dynamic_slice_in_dim(now, jnp.where(tail, rows - HALO, 0), HALO, axis=1)
 
-    off_chip = lax.ppermute(side(odd == 1), both_axes, off_chip_pairs)
+    off_near = lax.ppermute(far_near, both_axes, off_chip_pairs)
+    off_outer = lax.ppermute(far_outer, both_axes, off_chip_pairs)
     on_chip = lax.ppermute(side(odd == 0), "gx", on_chip_pairs)
     flux, base, slopes = call(
         side_kernel,
@@ -827,8 +893,8 @@
     final, imaged = call(
         late_kernel,
         (planes(2, rows), planes(4, rows)),
-        (now, mid, coeffs, on_chip, off_chip, base, slopes, inject, matrices),
-        [vmem] * 9,
+        (now, mid, coeffs, on_chip, off_near, off_outer, base, slopes, inject, matrices),
+        [vmem] * 10,
         [room(wide, padded), *[room(wide)] * 5, room(ext, padded), room(ext)],
         28 * wide,
         400 * rows,

time: 29.5 us -> 28.4 us (0.963)
  the two profiles are of different devices: /device:TPU:17 before, /device:TPU:1 now
where the time goes in v8:
time: 28.4 us; the launch traced here: 28.1 us
  waiting for transfers between devices  10.9 us (38%)
  starting transfers between devices  10.7 us (38%)
  Pallas kernels  5.72 us (20%)
  between operations  0.7 us (2%)
    ppermute x1, waiting for transfers between devices, local(): off_chip = lax.ppermute(far_pack, both_axes, off_chip_pairs)  7.48 us
    all_to_all x1, starting transfers between devices, local(): lax.all_to_all(sorted_source, 'gx', split_axis=0, concat_axis=0, tiled=Tr...  7.34 us
    pallas_call x6, Pallas kernels, call(): pl.pallas_call(kernel, out_shape=outs, in_specs=in_specs, out_specs=out_s...  5.72 us
    ppermute x1, waiting for transfers between devices, local(): off_outer = lax.ppermute(far_outer, both_axes, off_chip_pairs)  2.85 us
    ppermute x1, starting transfers between devices, local(): off_near = lax.ppermute(far_near, both_axes, off_chip_pairs)  2.55 us
    ppermute x1, waiting for transfers between devices, local(): on_chip = lax.ppermute(near_pack, 'gx', on_chip_pairs)  0.59 us
  transfers between devices with their start and end apart: 6, of which 3 were waited for; matrix products, arithmetic and copies ran while one was open for 0% of the time, Pallas kernels for 9%

profile of v8, /device:TPU:1, one launch (start us, length us, event | category | flops | bytes accessed | tf_op | source)
XLA Modules:
  0.0 28.1 jit_solution(14196114827291535869)
XLA Ops:
  0.6 2.0 %shard_map.122 = (f32[32,16,128]{2,1,0:T(8,128)S(1)}, f32[32,16,128]{2,1,0:T(8,128)S(1)}, bf16[16,2,4,8,128]{4,3,2,1,0:T(8,128)(2,1)}, f32[5,8,16,128]{3,2,1,0:T...) custom-call(f32[2,8,16,128]{3,2,1,0:T(8,128)} %before.1, ...), custom_call_target="tpu_custom_call" | custom-call | flops 409600 | bytes 102400 | tf_op jit(solution)/shard_map/pallas_call | solution.py:780
  2.7 0.0 copy-start
  2.7 7.3 %all-to-all-start = ((bf16[16,2,4,8,128]{4,3,2,1,0:T(8,128)(2,1)}), bf16[16,2,4,8,128]{4,3,2,1,0:T(8,128)(2,1)S(1)}, u32[]{:S(2)}, u32[]{:S(2)}) async-start(bf16[16,2,4,8,128]{4,3,2,1,0:T(8,128)(2,1)} %get-tuple-element.26), calls=%async_computation | async-start | bytes 524288 | tf_op jit(solution)/shard_map/all_to_all | solution.py:836
  10.0 0.4 %collective-permute-start = (f32[32,16,128]{2,1,0:T(8,128)S(1)}, f32[32,16,128]{2,1,0:T(8,128)S(1)}, u32[]{:S(2)}, u32[]{:S(2)}) collective-permute-start(f32[32,16,128]{2,1,0:T(8,128)S(1)} %get-tuple-element.27), channel_id=1, source_target_pairs={{0,1},{1,0},{2,3},{3,2},{4,5},{5,4},{6,7},{7,6},{8,9},{9,8},{10,11... | collective-permute-start | bytes 786440 | tf_op jit(solution)/shard_map/ppermute | solution.py:835
  10.4 0.3 %collective-permute-start.1 = (f32[32,16,128]{2,1,0:T(8,128)S(1)}, f32[32,16,128]{2,1,0:T(8,128)S(1)}, u32[]{:S(2)}, u32[]{:S(2)}) collective-permute-start(f32[32,16,128]{2,1,0:T(8,128)S(1)} %get-tuple-element.28), channel_id=1, source_target_pairs={{1,2},{2,1},{3,4},{4,3},{5,6},{6,5},{7,8},{8,7},{9,10},{10,9},{11,... | collective-permute-start | bytes 786440 | tf_op jit(solution)/shard_map/ppermute | solution.py:834
  10.7 0.4 %shard_map.123 = (f32[4,16,16,128]{3,2,1,0:T(8,128)S(1)}, f32[16,128]{1,0:T(8,128)S(1)}) custom-call(s32[128]{0:T(128)S(1)} %get-tuple-element.32.receiver_row, s32[128]{0:T(128)S(1)} %get-tuple-element.33.receiver_column, f32[4,128]{1,0:T(4,128)S(1)} %get-tuple-element.34.traces, s32[32]{0:T(128)S(1)} %get-tuple-element.35.table), custom_call_target="tpu_custom_call" | custom-call | flops 983040 | bytes 245760 | tf_op jit(solution)/shard_map/pallas_call | solution.py:780
  11.1 0.6 %collective-permute-done.on_chip = f32[32,16,128]{2,1,0:T(8,128)S(1)} collective-permute-done((f32[32,16,128]{2,1,0:T(8,128)S(1)}, f32[32,16,128]{2,1,0:T(8,128)S(1)}, u32[]{:S(2)}, u32[]{:S(2)}) %collective-permute-start) | collective-permute-done | bytes 262176 | tf_op jit(solution)/shard_map/ppermute | solution.py:835
  11.7 7.5 %collective-permute-done.1.off_chip = f32[32,16,128]{2,1,0:T(8,128)S(1)} collective-permute-done((f32[32,16,128]{2,1,0:T(8,128)S(1)}, f32[32,16,128]{2,1,0:T(8,128)S(1)}, u32[]{:S(2)}, u32[]{:S(2)}) %collective-permute-start.1) | collective-permute-done | bytes 262176 | tf_op jit(solution)/shard_map/ppermute | solution.py:834
  19.2 0.0 copy-done
  19.2 0.9 %shard_map.124 = (f32[2,8,16,128]{3,2,1,0:T(8,128)S(1)}, f32[2,4,16,128]{3,2,1,0:T(8,128)S(1)}, bf16[2,4,16,128]{3,2,1,0:T(8,128)(2,1)S(1)}, f32[2,16,16,128]{3,...) custom-call(f32[2,8,16,128]{3,2,1,0:T(8,128)S(1)} %copy-done, ...), custom_call_target="tpu_custom_call" | custom-call | flops 6553600 | bytes 1638400 | tf_op jit(solution)/shard_map/pallas_call | solution.py:780
  20.1 0.1 collective-permute-start.2
  20.2 2.5 %collective-permute-start.3 = (f32[2,4,16,128]{3,2,1,0:T(8,128)S(1)}, f32[2,4,16,128]{3,2,1,0:T(8,128)S(1)}, u32[]{:S(2)}, u32[]{:S(2)}) collective-permute-start(f32[2,4,16,128]{3,2,1,0:T(8,128)S(1)} %get-tuple-element.43), channel_id=1, source_target_pairs={{1,2},{2,1},{3,4},{4,3},{5,6},{6,5},{7,8},{8,7},{9,10},{10,9},{11,... | collective-permute-start | bytes 196616 | tf_op jit(solution)/shard_map/ppermute | solution.py:881
  22.7 0.1 collective-permute-start.4
  22.8 0.4 %shard_map.125 = (f32[3,8,16,128]{3,2,1,0:T(8,128)S(1)}, f32[2,8,16,128]{3,2,1,0:T(8,128)S(1)}, f32[2,8,16,128]{3,2,1,0:T(8,128)S(1)}) custom-call(f32[2,8,16,128]{3,2,1,0:T(8,128)S(1)} %copy-done, f32[2,16,16,128]{3,2,1,0:T(8,128)S(1)} %get-tuple-element.38.mid, f32[8,16,128]{2,1,0:T(8,128)S(1)} %get-tuple-element.39.slope_z, ...), custom_call_target="tpu_custom_call" | custom-call | flops 983040 | bytes 245760 | tf_op jit(solution)/shard_map/pallas_call | solution.py:780
  23.2 2.8 %collective-permute-done.4.off_outer = bf16[2,4,16,128]{3,2,1,0:T(8,128)(2,1)S(1)} collective-permute-done((bf16[2,4,16,128]{3,2,1,0:T(8,128)(2,1)S(1)}, bf16[2,4,16,128]{3,2,1,0:T(8,128)(2,1)S(1)}, u32[]{:S(2)}, u32[]{:S(2)}) %collective-permute-start.4) | collective-permute-done | bytes 32800 | tf_op jit(solution)/shard_map/ppermute | solution.py:882
  26.0 0.0 collective-permute-done.3.off_near
  26.1 0.0 collective-permute-done.2.on_chip
  26.1 0.9 %shard_map.126 = (f32[2,8,16,128]{3,2,1,0:T(8,128)S(1)}, f32[4,8,16,128]{3,2,1,0:T(8,128)S(1)}) custom-call(f32[2,8,16,128]{3,2,1,0:T(8,128)S(1)} %get-tuple-element.40.now, f32[2,16,16,128]{3,2,1,0:T(8,128)S(1)} %get-tuple-element.38.mid, f32[5,16,16,128]{3,2,1,0:T(8,128)S(1)} %get-tuple-element.41.coeffs, ...), custom_call_target="tpu_custom_call" | custom-call | flops 6553600 | bytes 1638400 | tf_op jit(solution)/shard_map/pallas_call | solution.py:780
  26.9 0.0 all-to-all-done.arrived
  26.9 1.1 %shard_map.127 = (bf16[8,8,16,128]{3,2,1,0:T(8,128)(2,1)}, f32[2,8,16,128]{3,2,1,0:T(8,128)}) custom-call(bf16[16,2,4,8,128]{4,3,2,1,0:T(8,128)(2,1)S(1)} %all-to-all-done.arrived, f32[2,16,16,128]{3,2,1,0:T(8,128)S(1)} %get-tuple-element.38.mid, f32[3,8,16,128]{3,2,1,0:T(8,128)S(1)} %get-tuple-element.42.flux, ...), custom_call_target="tpu_custom_call" | custom-call | flops 983040 | bytes 245760 | tf_op jit(solution)/shard_map/pallas_call | solution.py:780
Async XLA Ops:
  2.7 16.5 %copy-start = (f32[2,8,16,128]{3,2,1,0:T(8,128)S(1)}, f32[2,8,16,128]{3,2,1,0:T(8,128)}, u32[]{:S(2)}) copy-start(f32[2,8,16,128]{3,2,1,0:T(8,128)} %before.1) | copy-start | bytes 393220
  2.7 24.3 %all-to-all-start = ((bf16[16,2,4,8,128]{4,3,2,1,0:T(8,128)(2,1)}), bf16[16,2,4,8,128]{4,3,2,1,0:T(8,128)(2,1)S(1)}, u32[]{:S(2)}, u32[]{:S(2)}) async-start(bf16[16,2,4,8,128]{4,3,2,1,0:T(8,128)(2,1)} %get-tuple-element.26), calls=%async_computation | async-start | bytes 524288 | tf_op jit(solution)/shard_map/all_to_all | solution.py:836
  10.0 1.7 %collective-permute-start = (f32[32,16,128]{2,1,0:T(8,128)S(1)}, f32[32,16,128]{2,1,0:T(8,128)S(1)}, u32[]{:S(2)}, u32[]{:S(2)}) collective-permute-start(f32[32,16,128]{2,1,0:T(8,128)S(1)} %get-tuple-element.27), channel_id=1, source_target_pairs={{0,1},{1,0},{2,3},{3,2},{4,5},{5,4},{6,7},{7,6},{8,9},{9,8},{10,11... | collective-permute-start | bytes 786440 | tf_op jit(solution)/shard_map/ppermute | solution.py:835
  10.4 8.7 %collective-permute-start.1 = (f32[32,16,128]{2,1,0:T(8,128)S(1)}, f32[32,16,128]{2,1,0:T(8,128)S(1)}, u32[]{:S(2)}, u32[]{:S(2)}) collective-permute-start(f32[32,16,128]{2,1,0:T(8,128)S(1)} %get-tuple-element.28), channel_id=1, source_target_pairs={{1,2},{2,1},{3,4},{4,3},{5,6},{6,5},{7,8},{8,7},{9,10},{10,9},{11,... | collective-permute-start | bytes 786440 | tf_op jit(solution)/shard_map/ppermute | solution.py:834
  20.1 6.0 %collective-permute-start.2 = (f32[2,8,16,128]{3,2,1,0:T(8,128)S(1)}, f32[2,8,16,128]{3,2,1,0:T(8,128)S(1)}, u32[]{:S(2)}, u32[]{:S(2)}) collective-permute-start(f32[2,8,16,128]{3,2,1,0:T(8,128)S(1)} %get-tuple-element.40.now), channel_id=1, source_target_pairs={{0,1},{1,0},{2,3},{3,2},{4,5},{5,4},{6,7},{7,6},{8,9},{9,8},{10,11... | collective-permute-start | bytes 393224 | tf_op jit(solution)/shard_map/ppermute | solution.py:883
  20.2 5.9 %collective-permute-start.3 = (f32[2,4,16,128]{3,2,1,0:T(8,128)S(1)}, f32[2,4,16,128]{3,2,1,0:T(8,128)S(1)}, u32[]{:S(2)}, u32[]{:S(2)}) collective-permute-start(f32[2,4,16,128]{3,2,1,0:T(8,128)S(1)} %get-tuple-element.43), channel_id=1, source_target_pairs={{1,2},{2,1},{3,4},{4,3},{5,6},{6,5},{7,8},{8,7},{9,10},{10,9},{11,... | collective-permute-start | bytes 196616 | tf_op jit(solution)/shard_map/ppermute | solution.py:881
  22.7 3.3 %collective-permute-start.4 = (bf16[2,4,16,128]{3,2,1,0:T(8,128)(2,1)S(1)}, bf16[2,4,16,128]{3,2,1,0:T(8,128)(2,1)S(1)}, u32[]{:S(2)}, u32[]{:S(2)}) collective-permute-start(bf16[2,4,16,128]{3,2,1,0:T(8,128)(2,1)S(1)} %get-tuple-element.44), channel_id=1, source_target_pairs={{1,2},{2,1},{3,4},{4,3},{5,6},{6,5},{7,8},{8,7},{9,10},{10,9},{11,... | collective-permute-start | bytes 98312 | tf_op jit(solution)/shard_map/ppermute | solution.py:882

commit v9 on v8

--- a/solution.py
+++ b/solution.py
@@ -22,7 +22,7 @@
 
 
 def exchange_order(count):
-    step = next(n for n in (5, 7, 3, 1) if math.gcd(n, count) == 1)
+    step = next(n for n in (13, 5, 3, 1) if math.gcd(n, count) == 1)
     return [(count // 2 - 1 + step * j) % count for j in range(count)]
 
 
@@ -35,7 +35,7 @@
 
 
 def each_chunk(count, width, body):
-    size = max(1, min(count, 512 // width))
+    size = max(1, min(count, 256 // width))
     while count % size:
         size -= 1
     if count // size <= 2:
@@ -104,15 +104,21 @@
     return both[:, :depth], both[:, depth:]
 
 
-def depth_rows(read, slope, curve, begin, count, width, matrices, shift=0):
+def depth_rows(items, count, width, matrices):
     def chunk(start, size):
-        field = read(begin + start, size)
-        depth = field.shape[-1]
-        s, c = depth_diffs(field.reshape(size * width, depth), matrices)
-        slope[pl.ds(begin + shift + start, size)] = s.reshape(size, width, depth)
-        curve[pl.ds(begin + shift + start, size)] = c.reshape(size, width, depth)
-
-    each_chunk(count, width, chunk)
+        lines = size * width
+        fields = [read(begin + start, size) for read, _, _, begin in items]
+        depth = fields[0].shape[-1]
+        joined = jnp.concatenate([f.reshape(lines, depth) for f in fields], axis=0)
+        slopes, curves = depth_diffs(joined, matrices)
+        for i, (_, slope, curve, begin) in enumerate(items):
+            part = slice(i * lines, (i + 1) * lines)
+            rows = pl.ds(begin + start, size)
+            slope[rows] = slopes[part].reshape(size, width, depth)
+            if curve is not None:
+                curve[rows] = curves[part].reshape(size, width, depth)
+
+    each_chunk(count, width * len(items), chunk)
 
 
 def sine_terms(angle):
@@ -211,11 +217,11 @@
 def block_step(rows, width, fields, slopes, curves, matrices, earlier, coeffs, emit):
     p, q = fields
     inner = slice(YPAD, YPAD + width)
-    for field, slope, curve in (
-        (lambda b, n: p[pl.ds(b, n), inner, :], slopes[0], curves[0]),
-        (lambda b, n: q[pl.ds(b, n)], slopes[1], curves[1]),
-    ):
-        depth_rows(field, slope, curve, REACH, rows, width, matrices)
+    items = (
+        (lambda b, n: p[pl.ds(b, n), inner, :], slopes[0], curves[0], REACH),
+        (lambda b, n: q[pl.ds(b, n)], slopes[1], curves[1], REACH),
+    )
+    depth_rows(items, rows, width, matrices)
     time_step(0, rows, width, fields, earlier, coeffs, slopes, curves, emit)
 
 
@@ -284,10 +290,11 @@
 def second_step(rows, width, p1, q1, slopes, curves, earlier, coeffs, inject, matrices, emit):
     inner = slice(YPAD, YPAD + width)
     ext = rows + 2 * REACH
-    depth_rows(
-        lambda b, n: p1[pl.ds(b, n), inner, :], slopes[0], curves[0], 0, ext, width, matrices
-    )
-    depth_rows(lambda b, n: q1[pl.ds(b, n)], slopes[1], curves[1], 0, ext, width, matrices)
+    items = (
+        (lambda b, n: p1[pl.ds(b, n), inner, :], slopes[0], curves[0], 0),
+        (lambda b, n: q1[pl.ds(b, n)], slopes[1], curves[1], 0),
+    )
+    depth_rows(items, ext, width, matrices)
 
     def finish(row, next_p, next_q):
         emit(row, next_p + inject[row + REACH], next_q)
@@ -491,9 +498,11 @@
         medium = [take(4)] + [part[pl.ds((5 + m) * REACH, REACH)] for m in range(3)]
         for r in range(REACH):
             derive(coeffs, at + r, *[m[r] for m in medium])
+    items = []
     for begin in (0, rows + REACH):
-        depth_rows(lambda b, n: p[pl.ds(b, n)], slope_p, curve_p, begin, REACH, width, matrices)
-        depth_rows(lambda b, n: q[pl.ds(b, n)], slope_q, curve_q, begin, REACH, width, matrices)
+        items.append((lambda b, n: p[pl.ds(b, n)], slope_p, None, begin))
+        items.append((lambda b, n: q[pl.ds(b, n)], slope_q, None, begin))
+    depth_rows(items, REACH, width, matrices)
     q1 = mid.at[1]
     for row in range(rows + 2 * REACH):
         next_p, next_q = add_border(
@@ -634,10 +643,10 @@
     own = pl.ds(HALO, rows)
     slope_p[own], slope_q[own] = own_slopes[0], own_slopes[1]
     for begin in (0, rows + HALO):
-        depth_rows(
-            lambda b, n: p[pl.ds(b, n), inner, :], slope_p, curve_p, begin, HALO, width, matrices
-        )
-        depth_rows(lambda b, n: q[pl.ds(b, n)], slope_q, curve_q, begin, HALO, width, matrices)
+        item = (lambda b, n: p[pl.ds(b, n), inner, :], slope_p, curve_p, begin)
+        depth_rows((item,), HALO, width, matrices)
+        item = (lambda b, n: q[pl.ds(b, n)], slope_q, curve_q, begin)
+        depth_rows((item,), HALO, width, matrices)
 
     def keep(row, next_p, next_q):
         p1[row, inner, :] = next_p + inject[2, row]

time: 28.4 us -> 28.3 us (level)
  no operation moved by 1% of the time
where the time goes in v9:
time: 28.3 us; the launch traced here: 28 us
  waiting for transfers between devices  10.9 us (39%)
  starting transfers between devices  10.7 us (38%)
  Pallas kernels  5.6 us (20%)
  between operations  0.69 us (2%)
    ppermute x1, waiting for transfers between devices, local(): off_chip = lax.ppermute(far_pack, both_axes, off_chip_pairs)  7.48 us
    all_to_all x1, starting transfers between devices, local(): lax.all_to_all(sorted_source, 'gx', split_axis=0, concat_axis=0, tiled=Tr...  7.35 us
    pallas_call x6, Pallas kernels, call(): pl.pallas_call(kernel, out_shape=outs, in_specs=in_specs, out_specs=out_s...  5.6 us
    ppermute x1, waiting for transfers between devices, local(): off_outer = lax.ppermute(far_outer, both_axes, off_chip_pairs)  2.84 us
    ppermute x1, starting transfers between devices, local(): off_near = lax.ppermute(far_near, both_axes, off_chip_pairs)  2.55 us
    ppermute x1, waiting for transfers between devices, local(): on_chip = lax.ppermute(near_pack, 'gx', on_chip_pairs)  0.59 us
  transfers between devices with their start and end apart: 6, of which 3 were waited for; matrix products, arithmetic and copies ran while one was open for 0% of the time, Pallas kernels for 9%

profile of v9, /device:TPU:1, one launch (start us, length us, event | category | flops | bytes accessed | tf_op | source)
XLA Modules:
  0.0 28.0 jit_solution(10853360811017642457)
XLA Ops:
  0.6 2.0 %shard_map.122 = (f32[32,16,128]{2,1,0:T(8,128)S(1)}, f32[32,16,128]{2,1,0:T(8,128)S(1)}, bf16[16,2,4,8,128]{4,3,2,1,0:T(8,128)(2,1)}, f32[5,8,16,128]{3,2,1,0:T...) custom-call(f32[2,8,16,128]{3,2,1,0:T(8,128)} %before.1, ...), custom_call_target="tpu_custom_call" | custom-call | flops 409600 | bytes 102400 | tf_op jit(solution)/shard_map/pallas_call | solution.py:789
  2.6 0.0 copy-start
  2.6 7.3 %all-to-all-start = ((bf16[16,2,4,8,128]{4,3,2,1,0:T(8,128)(2,1)}), bf16[16,2,4,8,128]{4,3,2,1,0:T(8,128)(2,1)S(1)}, u32[]{:S(2)}, u32[]{:S(2)}) async-start(bf16[16,2,4,8,128]{4,3,2,1,0:T(8,128)(2,1)} %get-tuple-element.26), calls=%async_computation | async-start | bytes 524288 | tf_op jit(solution)/shard_map/all_to_all | solution.py:845
  10.0 0.4 %collective-permute-start = (f32[32,16,128]{2,1,0:T(8,128)S(1)}, f32[32,16,128]{2,1,0:T(8,128)S(1)}, u32[]{:S(2)}, u32[]{:S(2)}) collective-permute-start(f32[32,16,128]{2,1,0:T(8,128)S(1)} %get-tuple-element.27), channel_id=1, source_target_pairs={{0,1},{1,0},{2,3},{3,2},{4,5},{5,4},{6,7},{7,6},{8,9},{9,8},{10,11... | collective-permute-start | bytes 786440 | tf_op jit(solution)/shard_map/ppermute | solution.py:844
  10.4 0.3 %collective-permute-start.1 = (f32[32,16,128]{2,1,0:T(8,128)S(1)}, f32[32,16,128]{2,1,0:T(8,128)S(1)}, u32[]{:S(2)}, u32[]{:S(2)}) collective-permute-start(f32[32,16,128]{2,1,0:T(8,128)S(1)} %get-tuple-element.28), channel_id=1, source_target_pairs={{1,2},{2,1},{3,4},{4,3},{5,6},{6,5},{7,8},{8,7},{9,10},{10,9},{11,... | collective-permute-start | bytes 786440 | tf_op jit(solution)/shard_map/ppermute | solution.py:843
  10.7 0.4 %shard_map.123 = (f32[4,16,16,128]{3,2,1,0:T(8,128)S(1)}, f32[16,128]{1,0:T(8,128)S(1)}) custom-call(s32[128]{0:T(128)S(1)} %get-tuple-element.32.receiver_row, s32[128]{0:T(128)S(1)} %get-tuple-element.33.receiver_column, f32[4,128]{1,0:T(4,128)S(1)} %get-tuple-element.34.traces, s32[32]{0:T(128)S(1)} %get-tuple-element.35.table), custom_call_target="tpu_custom_call" | custom-call | flops 983040 | bytes 245760 | tf_op jit(solution)/shard_map/pallas_call | solution.py:789
  11.1 0.6 %collective-permute-done.on_chip = f32[32,16,128]{2,1,0:T(8,128)S(1)} collective-permute-done((f32[32,16,128]{2,1,0:T(8,128)S(1)}, f32[32,16,128]{2,1,0:T(8,128)S(1)}, u32[]{:S(2)}, u32[]{:S(2)}) %collective-permute-start) | collective-permute-done | bytes 262176 | tf_op jit(solution)/shard_map/ppermute | solution.py:844
  11.7 7.5 %collective-permute-done.1.off_chip = f32[32,16,128]{2,1,0:T(8,128)S(1)} collective-permute-done((f32[32,16,128]{2,1,0:T(8,128)S(1)}, f32[32,16,128]{2,1,0:T(8,128)S(1)}, u32[]{:S(2)}, u32[]{:S(2)}) %collective-permute-start.1) | collective-permute-done | bytes 262176 | tf_op jit(solution)/shard_map/ppermute | solution.py:843
  19.1 0.0 copy-done
  19.1 0.8 %shard_map.124 = (f32[2,8,16,128]{3,2,1,0:T(8,128)S(1)}, f32[2,4,16,128]{3,2,1,0:T(8,128)S(1)}, bf16[2,4,16,128]{3,2,1,0:T(8,128)(2,1)S(1)}, f32[2,16,16,128]{3,...) custom-call(f32[2,8,16,128]{3,2,1,0:T(8,128)S(1)} %copy-done, ...), custom_call_target="tpu_custom_call" | custom-call | flops 6553600 | bytes 1638400 | tf_op jit(solution)/shard_map/pallas_call | solution.py:789
  20.0 0.1 collective-permute-start.2
  20.1 2.6 %collective-permute-start.3 = (f32[2,4,16,128]{3,2,1,0:T(8,128)S(1)}, f32[2,4,16,128]{3,2,1,0:T(8,128)S(1)}, u32[]{:S(2)}, u32[]{:S(2)}) collective-permute-start(f32[2,4,16,128]{3,2,1,0:T(8,128)S(1)} %get-tuple-element.43), channel_id=1, source_target_pairs={{1,2},{2,1},{3,4},{4,3},{5,6},{6,5},{7,8},{8,7},{9,10},{10,9},{11,... | collective-permute-start | bytes 196616 | tf_op jit(solution)/shard_map/ppermute | solution.py:890
  22.6 0.1 collective-permute-start.4
  22.7 0.4 %shard_map.125 = (f32[3,8,16,128]{3,2,1,0:T(8,128)S(1)}, f32[2,8,16,128]{3,2,1,0:T(8,128)S(1)}, f32[2,8,16,128]{3,2,1,0:T(8,128)S(1)}) custom-call(f32[2,8,16,128]{3,2,1,0:T(8,128)S(1)} %copy-done, f32[2,16,16,128]{3,2,1,0:T(8,128)S(1)} %get-tuple-element.38.mid, f32[8,16,128]{2,1,0:T(8,128)S(1)} %get-tuple-element.39.slope_z, ...), custom_call_target="tpu_custom_call" | custom-call | flops 983040 | bytes 245760 | tf_op jit(solution)/shard_map/pallas_call | solution.py:789
  23.1 2.8 %collective-permute-done.4.off_outer = bf16[2,4,16,128]{3,2,1,0:T(8,128)(2,1)S(1)} collective-permute-done((bf16[2,4,16,128]{3,2,1,0:T(8,128)(2,1)S(1)}, bf16[2,4,16,128]{3,2,1,0:T(8,128)(2,1)S(1)}, u32[]{:S(2)}, u32[]{:S(2)}) %collective-permute-start.4) | collective-permute-done | bytes 32800 | tf_op jit(solution)/shard_map/ppermute | solution.py:891
  25.9 0.0 collective-permute-done.3.off_near
  26.0 0.0 collective-permute-done.2.on_chip
  26.0 0.9 %shard_map.126 = (f32[2,8,16,128]{3,2,1,0:T(8,128)S(1)}, f32[4,8,16,128]{3,2,1,0:T(8,128)S(1)}) custom-call(f32[2,8,16,128]{3,2,1,0:T(8,128)S(1)} %get-tuple-element.40.now, f32[2,16,16,128]{3,2,1,0:T(8,128)S(1)} %get-tuple-element.38.mid, f32[5,16,16,128]{3,2,1,0:T(8,128)S(1)} %get-tuple-element.41.coeffs, ...), custom_call_target="tpu_custom_call" | custom-call | flops 6553600 | bytes 1638400 | tf_op jit(solution)/shard_map/pallas_call | solution.py:789
  26.8 0.0 all-to-all-done.arrived
  26.8 1.1 %shard_map.127 = (bf16[8,8,16,128]{3,2,1,0:T(8,128)(2,1)}, f32[2,8,16,128]{3,2,1,0:T(8,128)}) custom-call(bf16[16,2,4,8,128]{4,3,2,1,0:T(8,128)(2,1)S(1)} %all-to-all-done.arrived, f32[2,16,16,128]{3,2,1,0:T(8,128)S(1)} %get-tuple-element.38.mid, f32[3,8,16,128]{3,2,1,0:T(8,128)S(1)} %get-tuple-element.42.flux, ...), custom_call_target="tpu_custom_call" | custom-call | flops 983040 | bytes 245760 | tf_op jit(solution)/shard_map/pallas_call | solution.py:789
Async XLA Ops:
  2.6 16.5 %copy-start = (f32[2,8,16,128]{3,2,1,0:T(8,128)S(1)}, f32[2,8,16,128]{3,2,1,0:T(8,128)}, u32[]{:S(2)}) copy-start(f32[2,8,16,128]{3,2,1,0:T(8,128)} %before.1) | copy-start | bytes 393220
  2.6 24.2 %all-to-all-start = ((bf16[16,2,4,8,128]{4,3,2,1,0:T(8,128)(2,1)}), bf16[16,2,4,8,128]{4,3,2,1,0:T(8,128)(2,1)S(1)}, u32[]{:S(2)}, u32[]{:S(2)}) async-start(bf16[16,2,4,8,128]{4,3,2,1,0:T(8,128)(2,1)} %get-tuple-element.26), calls=%async_computation | async-start | bytes 524288 | tf_op jit(solution)/shard_map/all_to_all | solution.py:845
  10.0 1.7 %collective-permute-start = (f32[32,16,128]{2,1,0:T(8,128)S(1)}, f32[32,16,128]{2,1,0:T(8,128)S(1)}, u32[]{:S(2)}, u32[]{:S(2)}) collective-permute-start(f32[32,16,128]{2,1,0:T(8,128)S(1)} %get-tuple-element.27), channel_id=1, source_target_pairs={{0,1},{1,0},{2,3},{3,2},{4,5},{5,4},{6,7},{7,6},{8,9},{9,8},{10,11... | collective-permute-start | bytes 786440 | tf_op jit(solution)/shard_map/ppermute | solution.py:844
  10.4 8.7 %collective-permute-start.1 = (f32[32,16,128]{2,1,0:T(8,128)S(1)}, f32[32,16,128]{2,1,0:T(8,128)S(1)}, u32[]{:S(2)}, u32[]{:S(2)}) collective-permute-start(f32[32,16,128]{2,1,0:T(8,128)S(1)} %get-tuple-element.28), channel_id=1, source_target_pairs={{1,2},{2,1},{3,4},{4,3},{5,6},{6,5},{7,8},{8,7},{9,10},{10,9},{11,... | collective-permute-start | bytes 786440 | tf_op jit(solution)/shard_map/ppermute | solution.py:843
  20.0 6.0 %collective-permute-start.2 = (f32[2,8,16,128]{3,2,1,0:T(8,128)S(1)}, f32[2,8,16,128]{3,2,1,0:T(8,128)S(1)}, u32[]{:S(2)}, u32[]{:S(2)}) collective-permute-start(f32[2,8,16,128]{3,2,1,0:T(8,128)S(1)} %get-tuple-element.40.now), channel_id=1, source_target_pairs={{0,1},{1,0},{2,3},{3,2},{4,5},{5,4},{6,7},{7,6},{8,9},{9,8},{10,11... | collective-permute-start | bytes 393224 | tf_op jit(solution)/shard_map/ppermute | solution.py:892
  20.1 5.9 %collective-permute-start.3 = (f32[2,4,16,128]{3,2,1,0:T(8,128)S(1)}, f32[2,4,16,128]{3,2,1,0:T(8,128)S(1)}, u32[]{:S(2)}, u32[]{:S(2)}) collective-permute-start(f32[2,4,16,128]{3,2,1,0:T(8,128)S(1)} %get-tuple-element.43), channel_id=1, source_target_pairs={{1,2},{2,1},{3,4},{4,3},{5,6},{6,5},{7,8},{8,7},{9,10},{10,9},{11,... | collective-permute-start | bytes 196616 | tf_op jit(solution)/shard_map/ppermute | solution.py:890
  22.6 3.3 %collective-permute-start.4 = (bf16[2,4,16,128]{3,2,1,0:T(8,128)(2,1)S(1)}, bf16[2,4,16,128]{3,2,1,0:T(8,128)(2,1)S(1)}, u32[]{:S(2)}, u32[]{:S(2)}) collective-permute-start(bf16[2,4,16,128]{3,2,1,0:T(8,128)(2,1)S(1)} %get-tuple-element.44), channel_id=1, source_target_pairs={{1,2},{2,1},{3,4},{4,3},{5,6},{6,5},{7,8},{8,7},{9,10},{10,9},{11,... | collective-permute-start | bytes 98312 | tf_op jit(solution)/shard_map/ppermute | solution.py:891

commit v10 on v9

--- a/solution.py
+++ b/solution.py
@@ -261,11 +261,10 @@
     emit(NBIN - 1, above)
 
 
-def clear_pads(ref, width):
-    rows, _, depth = ref.shape
-    zeros = jnp.zeros((rows, YPAD, depth), jnp.float32)
-    ref[:, :YPAD, :] = zeros
-    ref[:, YPAD + width :, :] = zeros
+def clear_pads(ref, width, begin, rows):
+    zeros = jnp.zeros((rows, YPAD, ref.shape[2]), jnp.float32)
+    ref[pl.ds(begin, rows), :YPAD, :] = zeros
+    ref[pl.ds(begin, rows), YPAD + width :, :] = zeros
 
 
 def place(dst_p, dst_q, centre, sides, width):
@@ -358,7 +357,7 @@
     arriving = []
     for place, owner in enumerate(exchange_order(source.shape[2])):
         arriving.append(copy(source.at[:, :, owner], staged.at[place]))
-    clear_pads(p, width)
+    clear_pads(p, width, REACH, rows)
     clear_sides(rows, p, q, slope_p, slope_q)
     own = pl.ds(REACH, rows)
     inner = slice(YPAD, YPAD + width)
@@ -478,7 +477,7 @@
     inner = slice(YPAD, YPAD + width)
     near, far = side_starts(rows, REACH)
     inside = has_far_side()
-    clear_pads(p1, width)
+    clear_pads(p1, width, REACH, rows)
     own = pl.ds(REACH, rows)
     p[own], q[own] = now[0], now[1]
     slope_p[own], slope_q[own] = own_slopes[0], own_slopes[1]
@@ -563,7 +562,7 @@
 ):
     rows, width = before.shape[1], before.shape[2]
     own = pl.ds(REACH, rows)
-    clear_pads(p1, width)
+    clear_pads(p1, width, REACH, rows)
     p1[:, YPAD : YPAD + width, :] = mid[0]
 
     def fluxes(row):
@@ -572,7 +571,7 @@
             flux[a, row] = parts[a]
 
     each_row(rows, width, fluxes)
-    clear_pads(p, width)
+    clear_pads(p, width, REACH, rows)
     clear_sides(rows, p, q, slope_p, slope_q)
     p[own, YPAD : YPAD + width, :] = now[0]
     q[own] = now[1]
@@ -623,8 +622,9 @@
     near, far = side_starts(rows, HALO)
     inside = has_far_side()
     odd = lax.rem(lax.axis_index("gx"), 2)
-    clear_pads(p, width)
-    clear_pads(p1, width)
+    for begin in (REACH, rows + HALO):
+        clear_pads(p, width, begin, REACH)
+    clear_pads(p1, width, REACH, rows)
 
     def far_rows(part, f):
         return jnp.where(inside, part[f].astype(jnp.float32), 0.0)

time: 28.3 us -> 28.3 us (level)
  no operation moved by 1% of the time
where the time goes in v10:
time: 28.3 us; the launch traced here: 28 us
  waiting for transfers between devices  10.9 us (39%)
  starting transfers between devices  10.7 us (38%)
  Pallas kernels  5.61 us (20%)
  between operations  0.69 us (2%)
    ppermute x1, waiting for transfers between devices, local(): off_chip = lax.ppermute(far_pack, both_axes, off_chip_pairs)  7.48 us
    all_to_all x1, starting transfers between devices, local(): lax.all_to_all(sorted_source, 'gx', split_axis=0, concat_axis=0, tiled=Tr...  7.35 us
    pallas_call x6, Pallas kernels, call(): pl.pallas_call(kernel, out_shape=outs, in_specs=in_specs, out_specs=out_s...  5.61 us
    ppermute x1, waiting for transfers between devices, local(): off_outer = lax.ppermute(far_outer, both_axes, off_chip_pairs)  2.84 us
    ppermute x1, starting transfers between devices, local(): off_near = lax.ppermute(far_near, both_axes, off_chip_pairs)  2.55 us
    ppermute x1, waiting for transfers between devices, local(): on_chip = lax.ppermute(near_pack, 'gx', on_chip_pairs)  0.59 us
  transfers between devices with their start and end apart: 6, of which 3 were waited for; matrix products, arithmetic and copies ran while one was open for 0% of the time, Pallas kernels for 9%

profile of v10, /device:TPU:1, one launch (start us, length us, event | category | flops | bytes accessed | tf_op | source)
XLA Modules:
  0.0 28.0 jit_solution(2685456643824514755)
XLA Ops:
  0.6 2.0 %shard_map.122 = (f32[32,16,128]{2,1,0:T(8,128)S(1)}, f32[32,16,128]{2,1,0:T(8,128)S(1)}, bf16[16,2,4,8,128]{4,3,2,1,0:T(8,128)(2,1)}, f32[5,8,16,128]{3,2,1,0:T...) custom-call(f32[2,8,16,128]{3,2,1,0:T(8,128)} %before.1, ...), custom_call_target="tpu_custom_call" | custom-call | flops 409600 | bytes 102400 | tf_op jit(solution)/shard_map/pallas_call | solution.py:789
  2.6 0.0 copy-start
  2.6 7.3 %all-to-all-start = ((bf16[16,2,4,8,128]{4,3,2,1,0:T(8,128)(2,1)}), bf16[16,2,4,8,128]{4,3,2,1,0:T(8,128)(2,1)S(1)}, u32[]{:S(2)}, u32[]{:S(2)}) async-start(bf16[16,2,4,8,128]{4,3,2,1,0:T(8,128)(2,1)} %get-tuple-element.26), calls=%async_computation | async-start | bytes 524288 | tf_op jit(solution)/shard_map/all_to_all | solution.py:845
  10.0 0.4 %collective-permute-start = (f32[32,16,128]{2,1,0:T(8,128)S(1)}, f32[32,16,128]{2,1,0:T(8,128)S(1)}, u32[]{:S(2)}, u32[]{:S(2)}) collective-permute-start(f32[32,16,128]{2,1,0:T(8,128)S(1)} %get-tuple-element.27), channel_id=1, source_target_pairs={{0,1},{1,0},{2,3},{3,2},{4,5},{5,4},{6,7},{7,6},{8,9},{9,8},{10,11... | collective-permute-start | bytes 786440 | tf_op jit(solution)/shard_map/ppermute | solution.py:844
  10.4 0.3 %collective-permute-start.1 = (f32[32,16,128]{2,1,0:T(8,128)S(1)}, f32[32,16,128]{2,1,0:T(8,128)S(1)}, u32[]{:S(2)}, u32[]{:S(2)}) collective-permute-start(f32[32,16,128]{2,1,0:T(8,128)S(1)} %get-tuple-element.28), channel_id=1, source_target_pairs={{1,2},{2,1},{3,4},{4,3},{5,6},{6,5},{7,8},{8,7},{9,10},{10,9},{11,... | collective-permute-start | bytes 786440 | tf_op jit(solution)/shard_map/ppermute | solution.py:843
  10.7 0.4 %shard_map.123 = (f32[4,16,16,128]{3,2,1,0:T(8,128)S(1)}, f32[16,128]{1,0:T(8,128)S(1)}) custom-call(s32[128]{0:T(128)S(1)} %get-tuple-element.32.receiver_row, s32[128]{0:T(128)S(1)} %get-tuple-element.33.receiver_column, f32[4,128]{1,0:T(4,128)S(1)} %get-tuple-element.34.traces, s32[32]{0:T(128)S(1)} %get-tuple-element.35.table), custom_call_target="tpu_custom_call" | custom-call | flops 983040 | bytes 245760 | tf_op jit(solution)/shard_map/pallas_call | solution.py:789
  11.1 0.6 %collective-permute-done.on_chip = f32[32,16,128]{2,1,0:T(8,128)S(1)} collective-permute-done((f32[32,16,128]{2,1,0:T(8,128)S(1)}, f32[32,16,128]{2,1,0:T(8,128)S(1)}, u32[]{:S(2)}, u32[]{:S(2)}) %collective-permute-start) | collective-permute-done | bytes 262176 | tf_op jit(solution)/shard_map/ppermute | solution.py:844
  11.7 7.5 %collective-permute-done.1.off_chip = f32[32,16,128]{2,1,0:T(8,128)S(1)} collective-permute-done((f32[32,16,128]{2,1,0:T(8,128)S(1)}, f32[32,16,128]{2,1,0:T(8,128)S(1)}, u32[]{:S(2)}, u32[]{:S(2)}) %collective-permute-start.1) | collective-permute-done | bytes 262176 | tf_op jit(solution)/shard_map/ppermute | solution.py:843
  19.1 0.0 copy-done
  19.1 0.8 %shard_map.124 = (f32[2,8,16,128]{3,2,1,0:T(8,128)S(1)}, f32[2,4,16,128]{3,2,1,0:T(8,128)S(1)}, bf16[2,4,16,128]{3,2,1,0:T(8,128)(2,1)S(1)}, f32[2,16,16,128]{3,...) custom-call(f32[2,8,16,128]{3,2,1,0:T(8,128)S(1)} %copy-done, ...), custom_call_target="tpu_custom_call" | custom-call | flops 6553600 | bytes 1638400 | tf_op jit(solution)/shard_map/pallas_call | solution.py:789
  20.0 0.1 collective-permute-start.2
  20.1 2.6 %collective-permute-start.3 = (f32[2,4,16,128]{3,2,1,0:T(8,128)S(1)}, f32[2,4,16,128]{3,2,1,0:T(8,128)S(1)}, u32[]{:S(2)}, u32[]{:S(2)}) collective-permute-start(f32[2,4,16,128]{3,2,1,0:T(8,128)S(1)} %get-tuple-element.43), channel_id=1, source_target_pairs={{1,2},{2,1},{3,4},{4,3},{5,6},{6,5},{7,8},{8,7},{9,10},{10,9},{11,... | collective-permute-start | bytes 196616 | tf_op jit(solution)/shard_map/ppermute | solution.py:890
  22.6 0.1 collective-permute-start.4
  22.7 0.4 %shard_map.125 = (f32[3,8,16,128]{3,2,1,0:T(8,128)S(1)}, f32[2,8,16,128]{3,2,1,0:T(8,128)S(1)}, f32[2,8,16,128]{3,2,1,0:T(8,128)S(1)}) custom-call(f32[2,8,16,128]{3,2,1,0:T(8,128)S(1)} %copy-done, f32[2,16,16,128]{3,2,1,0:T(8,128)S(1)} %get-tuple-element.38.mid, f32[8,16,128]{2,1,0:T(8,128)S(1)} %get-tuple-element.39.slope_z, ...), custom_call_target="tpu_custom_call" | custom-call | flops 983040 | bytes 245760 | tf_op jit(solution)/shard_map/pallas_call | solution.py:789
  23.1 2.8 %collective-permute-done.4.off_outer = bf16[2,4,16,128]{3,2,1,0:T(8,128)(2,1)S(1)} collective-permute-done((bf16[2,4,16,128]{3,2,1,0:T(8,128)(2,1)S(1)}, bf16[2,4,16,128]{3,2,1,0:T(8,128)(2,1)S(1)}, u32[]{:S(2)}, u32[]{:S(2)}) %collective-permute-start.4) | collective-permute-done | bytes 32800 | tf_op jit(solution)/shard_map/ppermute | solution.py:891
  25.9 0.0 collective-permute-done.3.off_near
  26.0 0.0 collective-permute-done.2.on_chip
  26.0 0.9 %shard_map.126 = (f32[2,8,16,128]{3,2,1,0:T(8,128)S(1)}, f32[4,8,16,128]{3,2,1,0:T(8,128)S(1)}) custom-call(f32[2,8,16,128]{3,2,1,0:T(8,128)S(1)} %get-tuple-element.40.now, f32[2,16,16,128]{3,2,1,0:T(8,128)S(1)} %get-tuple-element.38.mid, f32[5,16,16,128]{3,2,1,0:T(8,128)S(1)} %get-tuple-element.41.coeffs, ...), custom_call_target="tpu_custom_call" | custom-call | flops 6553600 | bytes 1638400 | tf_op jit(solution)/shard_map/pallas_call | solution.py:789
  26.8 0.0 all-to-all-done.arrived
  26.8 1.1 %shard_map.127 = (bf16[8,8,16,128]{3,2,1,0:T(8,128)(2,1)}, f32[2,8,16,128]{3,2,1,0:T(8,128)}) custom-call(bf16[16,2,4,8,128]{4,3,2,1,0:T(8,128)(2,1)S(1)} %all-to-all-done.arrived, f32[2,16,16,128]{3,2,1,0:T(8,128)S(1)} %get-tuple-element.38.mid, f32[3,8,16,128]{3,2,1,0:T(8,128)S(1)} %get-tuple-element.42.flux, ...), custom_call_target="tpu_custom_call" | custom-call | flops 983040 | bytes 245760 | tf_op jit(solution)/shard_map/pallas_call | solution.py:789
Async XLA Ops:
  2.6 16.5 %copy-start = (f32[2,8,16,128]{3,2,1,0:T(8,128)S(1)}, f32[2,8,16,128]{3,2,1,0:T(8,128)}, u32[]{:S(2)}) copy-start(f32[2,8,16,128]{3,2,1,0:T(8,128)} %before.1) | copy-start | bytes 393220
  2.6 24.2 %all-to-all-start = ((bf16[16,2,4,8,128]{4,3,2,1,0:T(8,128)(2,1)}), bf16[16,2,4,8,128]{4,3,2,1,0:T(8,128)(2,1)S(1)}, u32[]{:S(2)}, u32[]{:S(2)}) async-start(bf16[16,2,4,8,128]{4,3,2,1,0:T(8,128)(2,1)} %get-tuple-element.26), calls=%async_computation | async-start | bytes 524288 | tf_op jit(solution)/shard_map/all_to_all | solution.py:845
  10.0 1.7 %collective-permute-start = (f32[32,16,128]{2,1,0:T(8,128)S(1)}, f32[32,16,128]{2,1,0:T(8,128)S(1)}, u32[]{:S(2)}, u32[]{:S(2)}) collective-permute-start(f32[32,16,128]{2,1,0:T(8,128)S(1)} %get-tuple-element.27), channel_id=1, source_target_pairs={{0,1},{1,0},{2,3},{3,2},{4,5},{5,4},{6,7},{7,6},{8,9},{9,8},{10,11... | collective-permute-start | bytes 786440 | tf_op jit(solution)/shard_map/ppermute | solution.py:844
  10.4 8.7 %collective-permute-start.1 = (f32[32,16,128]{2,1,0:T(8,128)S(1)}, f32[32,16,128]{2,1,0:T(8,128)S(1)}, u32[]{:S(2)}, u32[]{:S(2)}) collective-permute-start(f32[32,16,128]{2,1,0:T(8,128)S(1)} %get-tuple-element.28), channel_id=1, source_target_pairs={{1,2},{2,1},{3,4},{4,3},{5,6},{6,5},{7,8},{8,7},{9,10},{10,9},{11,... | collective-permute-start | bytes 786440 | tf_op jit(solution)/shard_map/ppermute | solution.py:843
  20.0 6.0 %collective-permute-start.2 = (f32[2,8,16,128]{3,2,1,0:T(8,128)S(1)}, f32[2,8,16,128]{3,2,1,0:T(8,128)S(1)}, u32[]{:S(2)}, u32[]{:S(2)}) collective-permute-start(f32[2,8,16,128]{3,2,1,0:T(8,128)S(1)} %get-tuple-element.40.now), channel_id=1, source_target_pairs={{0,1},{1,0},{2,3},{3,2},{4,5},{5,4},{6,7},{7,6},{8,9},{9,8},{10,11... | collective-permute-start | bytes 393224 | tf_op jit(solution)/shard_map/ppermute | solution.py:892
  20.1 5.9 %collective-permute-start.3 = (f32[2,4,16,128]{3,2,1,0:T(8,128)S(1)}, f32[2,4,16,128]{3,2,1,0:T(8,128)S(1)}, u32[]{:S(2)}, u32[]{:S(2)}) collective-permute-start(f32[2,4,16,128]{3,2,1,0:T(8,128)S(1)} %get-tuple-element.43), channel_id=1, source_target_pairs={{1,2},{2,1},{3,4},{4,3},{5,6},{6,5},{7,8},{8,7},{9,10},{10,9},{11,... | collective-permute-start | bytes 196616 | tf_op jit(solution)/shard_map/ppermute | solution.py:890
  22.6 3.3 %collective-permute-start.4 = (bf16[2,4,16,128]{3,2,1,0:T(8,128)(2,1)S(1)}, bf16[2,4,16,128]{3,2,1,0:T(8,128)(2,1)S(1)}, u32[]{:S(2)}, u32[]{:S(2)}) collective-permute-start(bf16[2,4,16,128]{3,2,1,0:T(8,128)(2,1)S(1)} %get-tuple-element.44), channel_id=1, source_target_pairs={{1,2},{2,1},{3,4},{4,3},{5,6},{6,5},{7,8},{8,7},{9,10},{10,9},{11,... | collective-permute-start | bytes 98312 | tf_op jit(solution)/shard_map/ppermute | solution.py:891
